TPU v7x, 32 devices: a whole 2x2x4 slice. The times are simulated.
32 devices in a mesh: group: 4 (over z), replica: 8 (over y, x, core).
Axes of the slice: x: 2, y: 2, z: 4, core: 2. Of those that a mesh axis runs over, the one named last changes fastest.
Arguments:
- inputs: bfloat16 [8, 512, 1024], P('replica', 'group'), may hold values from -6 to 6
- cotangent: bfloat16 [8, 512, 1024], P('replica', 'group'), may hold values from -6 to 6
- norm_gain: bfloat16 [2, 2, 1024], P(None, None, 'group'), may hold values from 0.5 to 1.5
- norm_bias: bfloat16 [2, 2, 1024], P(None, None, 'group'), may hold values from -4 to 4
- w_qkv: bfloat16 [2, 1024, 3072], P(None, 'group'), may hold values from -0.1875 to 0.1875
- bias_qv: bfloat16 [2, 2048], P(None, 'group'), may hold values from -6 to 6
- w_out: bfloat16 [2, 1024, 1024], P(None, 'group'), may hold values from -0.75 to 0.75
- bias_out: bfloat16 [2, 1024], P(None, 'group'), may hold values from -6 to 6
- w_up: bfloat16 [2, 1024, 4096], P(None, 'group'), may hold values from -0.1875 to 0.1875
- bias_up: bfloat16 [2, 4096], P(None, 'group'), may hold values from -6 to 6
- w_down: bfloat16 [2, 4096, 1024], P(None, 'group'), may hold values from -0.09375 to 0.09375
- bias_down: bfloat16 [2, 1024], P(None, 'group'), may hold values from -6 to 6
Outputs:
- outputs: bfloat16 [8, 512, 1024], P('replica', 'group')
- input_grad: float32 [8, 512, 1024], P('replica', 'group')
- grad_norm_gain: float32 [2, 2, 1024], P(None, None, 'group')
- grad_norm_bias: float32 [2, 2, 1024], P(None, None, 'group')
- grad_qkv: float32 [2, 1024, 3072], P(None, 'group')
- grad_qv_bias: float32 [2, 2048], P(None, 'group')
- grad_out: float32 [2, 1024, 1024], P(None, 'group')
- grad_out_bias: float32 [2, 1024], P(None, 'group')
- grad_up: float32 [2, 1024, 4096], P(None, 'group')
- grad_up_bias: float32 [2, 4096], P(None, 'group')
- grad_down: float32 [2, 4096, 1024], P(None, 'group')
- grad_down_bias: float32 [2, 1024], P(None, 'group')
All inputs are finite; a program needn't handle non-finite values.
Results may differ from a plain program's by a relative error of at most 0.024.
Values may be sent and summed in bfloat16 or wider, within the bound.
A program may use at most 256 MiB of HBM per device.

v0:
```python
import functools

import jax
import jax.numpy as jnp
from jax import lax
from jax.experimental import pallas as pl
from jax.experimental.pallas import tpu as pltpu
from jax.sharding import PartitionSpec as P

HEADS = 16
HEAD_DIM = 64

EPS = 1e-05
NEG = -1e30
GELU_C = 0.7978845608028654
GELU_A = 0.044715
F32 = jnp.float32
B16 = jnp.bfloat16
MESH = pl.DeviceIdType.MESH


def norm_apply(values_in, gain_row, bias_row):
    row_mean = jnp.mean(values_in, axis=-1, keepdims=True)
    centered = values_in - row_mean
    variance = jnp.mean(centered * centered, axis=-1, keepdims=True)
    inverse = lax.rsqrt(variance + EPS)
    normed = centered * inverse
    return (normed * gain_row + bias_row, normed, inverse)


def norm_back(grad_in, normed, inverse, gain_row):
    scaled = grad_in * gain_row
    return inverse * (
        scaled
        - jnp.mean(scaled, axis=-1, keepdims=True)
        - normed * jnp.mean(scaled * normed, axis=-1, keepdims=True)
    )


def gelu_parts(pre_act):
    tanh_val = jnp.tanh(GELU_C * (pre_act + GELU_A * pre_act * pre_act * pre_act))
    gelu_value = 0.5 * pre_act * (1.0 + tanh_val)
    gelu_slope = 0.5 * (1.0 + tanh_val) + 0.5 * pre_act * (1.0 - tanh_val * tanh_val) * GELU_C * (
        1.0 + 3.0 * GELU_A * pre_act * pre_act
    )
    return (gelu_value, gelu_slope)


def dot(a, b):
    return jnp.dot(a, b, preferred_element_type=F32)


def dot_nt(a, b):
    return lax.dot_general(a, b, (((1,), (1,)), ((), ())), preferred_element_type=F32)


def dot_tn(a, b):
    return lax.dot_general(a, b, (((0,), (0,)), ((), ())), preferred_element_type=F32)


def greet(peers):
    barrier = pltpu.get_barrier_semaphore()
    for peer in peers:
        pl.semaphore_signal(barrier, inc=1, device_id={"group": peer}, device_id_type=MESH)
    pl.semaphore_wait(barrier, len(peers))


def gather_kernel(groups, x_ref, *refs):
    o_ref, send_sems, recv_sems = refs[-3:]
    me = lax.axis_index("group")
    rows = x_ref.shape[0]
    peers = [lax.rem(me + step, groups) for step in range(1, groups)]
    greet(peers)
    here = pl.ds(pl.multiple_of(me * rows, rows), rows)
    copies = []
    for step, peer in enumerate(peers):
        copy = pltpu.make_async_remote_copy(
            src_ref=x_ref,
            dst_ref=o_ref.at[here],
            send_sem=send_sems.at[step],
            recv_sem=recv_sems.at[step],
            device_id={"group": peer},
            device_id_type=MESH,
        )
        copy.start()
        copies.append(copy)
    o_ref[here, :] = x_ref[...]
    for copy in copies:
        copy.wait()


def scatter_kernel(groups, x_ref, *refs):
    o_ref, landed, send_sems, recv_sems = refs[-4:]
    me = lax.axis_index("group")
    rows = o_ref.shape[0]
    peers = [lax.rem(me + step, groups) for step in range(1, groups)]
    greet(peers)
    copies = []
    for step, peer in enumerate(peers):
        copy = pltpu.make_async_remote_copy(
            src_ref=x_ref.at[pl.ds(pl.multiple_of(peer * rows, rows), rows)],
            dst_ref=landed.at[step],
            send_sem=send_sems.at[step],
            recv_sem=recv_sems.at[step],
            device_id={"group": peer},
            device_id_type=MESH,
        )
        copy.start()
        copies.append(copy)
    total = x_ref[pl.ds(pl.multiple_of(me * rows, rows), rows), :].astype(F32)
    for step, copy in enumerate(copies):
        copy.wait_recv()
        total = total + landed[step].astype(F32)
    o_ref[...] = total
    for copy in copies:
        copy.wait_send()


VMEM_SPEC = pl.BlockSpec(memory_space=pltpu.VMEM)


def gather_rows(block, collective_id=0, after=()):
    groups = lax.axis_size("group")
    rows, cols = block.shape
    return pl.pallas_call(
        functools.partial(gather_kernel, groups),
        out_shape=jax.ShapeDtypeStruct((groups * rows, cols), block.dtype),
        in_specs=[VMEM_SPEC] + [pl.BlockSpec(memory_space=pl.ANY)] * len(after),
        out_specs=VMEM_SPEC,
        scratch_shapes=[
            pltpu.SemaphoreType.DMA((groups - 1,)),
            pltpu.SemaphoreType.DMA((groups - 1,)),
        ],
        compiler_params=pltpu.CompilerParams(
            collective_id=collective_id, has_side_effects=True, vmem_limit_bytes=16 * 1024 * 1024
        ),
        cost_estimate=pl.CostEstimate(
            flops=0, bytes_accessed=640 * block.size, transcendentals=0
        ),
    )(block, *after)


def scatter_rows(block, collective_id=1, after=()):
    groups = lax.axis_size("group")
    rows, cols = block.shape[0] // groups, block.shape[1]
    return pl.pallas_call(
        functools.partial(scatter_kernel, groups),
        out_shape=jax.ShapeDtypeStruct((rows, cols), F32),
        in_specs=[VMEM_SPEC] + [pl.BlockSpec(memory_space=pl.ANY)] * len(after),
        out_specs=VMEM_SPEC,
        scratch_shapes=[
            pltpu.VMEM((groups - 1, rows, cols), block.dtype),
            pltpu.SemaphoreType.DMA((groups - 1,)),
            pltpu.SemaphoreType.DMA((groups - 1,)),
        ],
        compiler_params=pltpu.CompilerParams(
            collective_id=collective_id, has_side_effects=True, vmem_limit_bytes=16 * 1024 * 1024
        ),
        cost_estimate=pl.CostEstimate(
            flops=0, bytes_accessed=640 * block.size // groups, transcendentals=0
        ),
    )(block, *after)


def attention(q, k, v, first_head, heads_here):
    tokens = q.shape[0]
    split = lambda m: m.reshape(tokens, heads_here, HEAD_DIM).transpose(1, 0, 2)
    q, k, v = split(q), split(k), split(v)
    head_ids = (first_head + jnp.arange(heads_here, dtype=jnp.int32)).astype(F32)
    slopes = 2.0 ** (-8.0 * (head_ids + 1.0) / HEADS)
    pos = jnp.arange(tokens, dtype=jnp.int32)
    offset = (pos[:, None] - pos[None, :]).astype(F32)
    raw = jnp.einsum("hqd,hkd->hqk", q, k, preferred_element_type=F32)
    scores = raw * HEAD_DIM ** (-0.5) - slopes[:, None, None] * offset[None]
    scores = jnp.where((offset >= 0.0)[None], scores, NEG)
    row_top = jnp.max(scores, axis=-1, keepdims=True)
    exps_raw = jnp.exp(scores - row_top)
    row_total = jnp.sum(exps_raw, axis=-1, keepdims=True)
    probs = (exps_raw * (1.0 / row_total)).astype(B16)
    context = jnp.einsum("hqk,hkd->hqd", probs, v, preferred_element_type=F32).astype(B16)
    return context.transpose(1, 0, 2).reshape(tokens, -1), (q, k, v, probs, context)


def attention_back(d_context, saved):
    q, k, v, probs, context = saved
    heads_here, tokens, _ = q.shape
    dc = d_context.reshape(tokens, heads_here, HEAD_DIM).transpose(1, 0, 2)
    d_probs = jnp.einsum("hqd,hkd->hqk", dc, v, preferred_element_type=F32)
    delta = jnp.sum(dc.astype(F32) * context.astype(F32), axis=-1, keepdims=True)
    ds = (probs.astype(F32) * (d_probs - delta)).astype(B16)
    scale = HEAD_DIM ** (-0.5)
    dq = jnp.einsum("hqk,hkd->hqd", ds, k, preferred_element_type=F32) * scale
    dk = jnp.einsum("hqk,hqd->hkd", ds, q, preferred_element_type=F32) * scale
    dv = jnp.einsum("hqk,hqd->hkd", probs, dc, preferred_element_type=F32)
    sums = (jnp.sum(dq, axis=1).reshape(-1), jnp.sum(dv, axis=1).reshape(-1))
    join = lambda m: m.astype(B16).transpose(1, 0, 2).reshape(tokens, -1)
    return jnp.concatenate([join(dq), join(dk), join(dv)], axis=1), sums


def local(
    inputs,
    cotangent,
    norm_gain,
    norm_bias,
    w_qkv,
    bias_qv,
    w_out,
    bias_out,
    w_up,
    bias_up,
    w_down,
    bias_down,
):
    groups = lax.axis_size("group")
    replicas = lax.axis_size("replica")
    me = lax.axis_index("group")
    copy_idx = lax.axis_index("replica")
    layers, own, _ = w_qkv.shape
    width = own * groups
    ff_own = w_down.shape[1]
    heads_here = HEADS // groups
    piece = own // replicas

    qkv_piece = lax.dynamic_slice_in_dim(w_qkv, copy_idx * piece, piece, axis=1)
    qkv_piece = qkv_piece.reshape(layers, piece, 3, groups, own).transpose(0, 3, 1, 2, 4)
    qkv_piece = qkv_piece.reshape(layers, groups, piece, 3 * own)
    up_piece = lax.dynamic_slice_in_dim(w_up, copy_idx * piece, piece, axis=1)
    up_piece = up_piece.reshape(layers, piece, groups, ff_own).transpose(0, 2, 1, 3)

    def exchange(block):
        return lax.all_to_all(block, "group", split_axis=0, concat_axis=0, tiled=True)

    def share(block):
        full = lax.all_gather(block, "replica", axis=1, tiled=True)
        return full.reshape(width, -1)

    first = share(exchange(qkv_piece[0]))
    rest = exchange(
        jnp.concatenate([up_piece[l] for l in range(layers)] + [qkv_piece[l] for l in range(1, layers)], axis=2)
    )
    cuts = [ff_own * l for l in range(1, layers + 1)]
    cuts += [ff_own * layers + 3 * own * l for l in range(1, layers - 1)]
    parts = jnp.split(rest, cuts, axis=2)
    wu_cols = [None] * layers
    wq_cols = [first] + [None] * (layers - 1)
    for l in range(layers):
        if l:
            wq_cols[l] = share(parts[layers + l - 1])
        wu_cols[l] = share(parts[l])

    small = jnp.concatenate(
        [norm_gain, norm_bias, bias_qv.reshape(layers, 2, own), bias_out[:, None], bias_down[:, None]],
        axis=1,
    )
    small = lax.all_gather(small, "group", axis=0).astype(F32)
    rows_of = lambda i: small[:, :, i].transpose(1, 0, 2).reshape(layers, width)
    gains = [rows_of(0), rows_of(1)]
    shifts = [rows_of(2), rows_of(3)]
    qv_full = small[:, :, 4:6].transpose(1, 0, 2, 3).reshape(layers, 2 * width)
    q_bias = lax.dynamic_slice_in_dim(qv_full, me * own, own, axis=1)
    v_bias = lax.dynamic_slice_in_dim(qv_full, width + me * own, own, axis=1)
    out_bias, down_bias = rows_of(6), rows_of(7)
    up_bias = bias_up.astype(F32)

    cot_all = gather_rows(cotangent[0])
    x = inputs[0].astype(F32)
    kept = []
    for l in range(layers):
        a1, n0, i0 = norm_apply(x, gains[0][l], shifts[0][l])
        a1_all = gather_rows(a1.astype(B16))
        proj = dot(a1_all, wq_cols[l])
        q = (proj[:, :own] + q_bias[l]).astype(B16)
        k = proj[:, own : 2 * own].astype(B16)
        v = (proj[:, 2 * own :] + v_bias[l]).astype(B16)
        context, attn_saved = attention(q, k, v, me * heads_here, heads_here)
        h = x + scatter_rows(dot(context, w_out[l]).astype(B16)) + out_bias[l]
        a2, n1, i1 = norm_apply(h, gains[1][l], shifts[1][l])
        a2_all = gather_rows(a2.astype(B16))
        value, slope = gelu_parts(dot(a2_all, wu_cols[l]) + up_bias[l])
        hidden = value.astype(B16)
        x = h + scatter_rows(dot(hidden, w_down[l]).astype(B16)) + down_bias[l]
        kept.append((n0, i0, a1_all, attn_saved, context, n1, i1, a2_all, slope, hidden))
    outputs = x.astype(B16)[None]

    def reduce_pair(cols_grad, rows_grad):
        cols = cols_grad.shape[1]
        blocks = [cols_grad[i * own : (i + 1) * own] for i in range(groups)]
        folds = rows_grad.shape[0] // own
        blocks += [rows_grad[i * own : (i + 1) * own] for i in range(folds)]
        return lax.psum_scatter(
            jnp.concatenate(blocks, axis=1), "replica", scatter_dimension=0, tiled=True
        )

    def share_pair(mine, cols, minor):
        cut = groups * cols
        left = exchange(mine[:, :cut].reshape(piece, groups, cols).transpose(1, 0, 2))
        left = left.reshape(groups, piece, minor, cols // minor).transpose(1, 2, 0, 3)
        mine = jnp.concatenate([left.reshape(piece, cut), mine[:, cut:]], axis=1)
        return lax.all_gather(mine, "replica", axis=0, tiled=True)

    def unpack_pair(full, cols):
        cut = groups * cols
        folds = (full.shape[1] - cut) // width
        rows = [full[:, cut + i * width : cut + (i + 1) * width] for i in range(folds)]
        return full[:, :cut].astype(F32), jnp.concatenate(rows, axis=0).astype(F32)

    g = cotangent[0].astype(F32)
    grads = [None] * layers
    smalls = [None] * layers
    held = {}
    zeros_qv = jnp.zeros((2 * width,), F32)
    for l in reversed(range(layers)):
        n0, i0, a1_all, attn_saved, context, n1, i1, a2_all, slope, hidden = kept[l]
        prev = held.get(l + 1)
        if prev is None:
            g_all = cot_all
        else:
            g_all = gather_rows(g.astype(B16), 3, (prev["ffn_sum"],))
            prev["ffn"] = share_pair(prev["ffn_sum"], ff_own, 1)
        gr_down_bias = jnp.sum(g, axis=0)
        d_pre = dot_nt(g_all, w_down[l]) * slope
        gr_up_bias = jnp.sum(d_pre, axis=0)
        pre_b16 = d_pre.astype(B16)
        da2 = scatter_rows(dot_nt(pre_b16, wu_cols[l]).astype(B16))
        gr_down = dot_tn(hidden, g_all).astype(B16)
        gr_up = dot_tn(a2_all, pre_b16).astype(B16)
        held[l] = {"ffn_sum": reduce_pair(gr_up, gr_down)}
        gr_gain1, gr_bias1 = jnp.sum(da2 * n1, axis=0), jnp.sum(da2, axis=0)
        dh = g + norm_back(da2, n1, i1, gains[1][l])
        gr_out_bias = jnp.sum(dh, axis=0)
        if prev is None:
            dh_all = gather_rows(dh.astype(B16))
        else:
            dh_all = gather_rows(dh.astype(B16), 4, (prev["attn_sum"], prev["ffn"]))
            prev["attn"] = share_pair(prev["attn_sum"], 3 * own, 3)
        dc = dot_nt(dh_all, w_out[l]).astype(B16)
        d_proj, (dq_sum, dv_sum) = attention_back(dc, attn_saved)
        da1_part = dot_nt(d_proj, wq_cols[l]).astype(B16)
        da1 = scatter_rows(da1_part) if prev is None else scatter_rows(da1_part, 5, (held[l]["ffn_sum"],))
        gr_out = dot_tn(context, dh_all).astype(B16)
        gr_qkv = dot_tn(a1_all, d_proj).astype(B16)
        gr_gain0, gr_bias0 = jnp.sum(da1 * n0, axis=0), jnp.sum(da1, axis=0)
        g = dh + norm_back(da1, n0, i0, gains[0][l])
        qv = lax.dynamic_update_slice_in_dim(zeros_qv, dq_sum, me * own, axis=0)
        qv = lax.dynamic_update_slice_in_dim(qv, dv_sum, width + me * own, axis=0)
        smalls[l] = (
            jnp.concatenate([gr_gain0, gr_gain1, gr_bias0, gr_bias1, qv, gr_out_bias, gr_down_bias]),
            gr_up_bias,
        )
        held[l]["attn_sum"] = reduce_pair(gr_qkv, gr_out)

    for l in range(layers):
        ffn = held[l]["ffn"] if "ffn" in held[l] else share_pair(held[l]["ffn_sum"], ff_own, 1)
        attn = held[l]["attn"] if "attn" in held[l] else share_pair(held[l]["attn_sum"], 3 * own, 3)
        grads[l] = unpack_pair(attn, 3 * own) + unpack_pair(ffn, ff_own)

    wide = jnp.stack([s[0] for s in smalls])
    per_owner = lambda lo, n: wide[:, lo * width : (lo + n) * width].reshape(layers, n, groups, own)
    gain_bias = per_owner(0, 4).transpose(2, 0, 1, 3)
    qv = wide[:, 4 * width : 6 * width].reshape(layers, groups, 2, own).transpose(1, 0, 2, 3)
    dense = per_owner(6, 2).transpose(2, 0, 1, 3)
    wide = jnp.concatenate([gain_bias, qv, dense], axis=2)
    mine = scatter_rows(wide.reshape(groups * layers * 8, own), 2)
    ups = jnp.stack([s[1] for s in smalls])
    flat = jnp.concatenate([mine.reshape(-1), ups.reshape(-1)]).reshape(-1, 128)
    total = lax.psum(flat, "replica").reshape(-1)
    cut = layers * 8 * own
    own_cols = total[:cut].reshape(layers, 8, own)
    up_total = total[cut:].reshape(layers, ff_own)
    qv_total = own_cols[:, 4:6].reshape(layers, 2 * own)
    stack = lambda i: jnp.stack([grads[l][i] for l in range(layers)])
    return (
        outputs,
        g[None],
        own_cols[:, 0:2],
        own_cols[:, 2:4],
        stack(0),
        qv_total,
        stack(1),
        own_cols[:, 6],
        stack(2),
        up_total,
        stack(3),
        own_cols[:, 7],
    )


def solution(mesh):
    rows = P("replica", "group", None)
    vec = P(None, None, "group")
    mat = P(None, "group", None)
    bias = P(None, "group")
    params = (vec, vec, mat, bias, mat, bias, mat, bias, mat, bias)
    return jax.shard_map(
        local,
        mesh=mesh,
        in_specs=(rows, rows) + params,
        out_specs=(rows, rows) + params,
        check_vma=False,
    )
```

profile of v0, /device:TPU:0, one launch (start us, length us, event | category | flops | bytes accessed | tf_op | source)
XLA Modules:
  0.0 698.1 jit_solution(15019363482401744174)
XLA Ops:
  9.9 13.7 %all_to_all.30 = bf16[4,32,768]{2,1,0:T(8,128)(2,1)} all-to-all(bf16[4,32,768]{2,1,0:T(8,128)(2,1)S(1)} %squeeze.59), channel_id=1, replica_groups=mesh['group'=4,'replica'=8] {'group'}, dimensions={0} | all-to-all | bytes 393216 | tf_op jit(solution)/shard_map/all_to_all | solution.py:231
  25.8 21.0 %all_to_all.31 = bf16[4,32,2816]{2,1,0:T(8,128)(2,1)S(1)} all-to-all(bf16[4,32,2816]{2,1,0:T(8,128)(2,1)S(1)} %copy.186), channel_id=1, replica_groups=mesh['group'=4,'replica'=8] {'group'}, dimensions={0} | all-to-all | bytes 1441792 | tf_op jit(solution)/shard_map/all_to_all | solution.py:231
  47.8 13.1 %all-gather = bf16[8,8,256]{2,1,0:T(8,128)(2,1)S(1)} all-gather(bf16[2,8,256]{2,1,0:T(8,128)(2,1)S(1)} %concatenate.84), channel_id=2, replica_groups=mesh['group'=4,'replica'=8] {'group'}, dimensions={0}, use_global_device_ids=true | all-gather | bytes 40960 | tf_op jit(solution)/shard_map/all_gather | solution.py:255
  62.8 17.7 %shard_map.211 = bf16[512,1024]{1,0:T(8,128)(2,1)S(1)} custom-call(bf16[128,1024]{1,0:T(8,128)(2,1)S(1)} %fusion.69.x_ref), custom_call_target="tpu_custom_call" | custom-call | bytes 83886080 | tf_op jit(solution)/shard_map/pallas_call | solution.py:125
  81.4 24.3 %shard_map.219 = bf16[512,1024]{1,0:T(8,128)(2,1)S(1)} custom-call(bf16[128,1024]{1,0:T(8,128)(2,1)S(1)} %bitcast.348), custom_call_target="tpu_custom_call" | custom-call | bytes 83886080 | tf_op jit(solution)/shard_map/pallas_call | solution.py:125
  122.3 24.5 %shard_map.212 = f32[128,1024]{1,0:T(8,128)S(1)} custom-call(bf16[512,1024]{1,0:T(8,128)(2,1)S(1)} %convolution_convert_fusion.11.x_ref), custom_call_target="tpu_custom_call" | custom-call | bytes 83886080 | tf_op jit(solution)/shard_map/pallas_call | solution.py:146
  147.3 24.2 %shard_map.213 = bf16[512,1024]{1,0:T(8,128)(2,1)S(1)} custom-call(bf16[128,1024]{1,0:T(8,128)(2,1)S(1)} %add_convert_fusion.3.x_ref), custom_call_target="tpu_custom_call" | custom-call | bytes 83886080 | tf_op jit(solution)/shard_map/pallas_call | solution.py:125
  182.2 24.4 %shard_map.214 = f32[128,1024]{1,0:T(8,128)S(1)} custom-call(bf16[512,1024]{1,0:T(8,128)(2,1)S(1)} %fusion.42.x_ref), custom_call_target="tpu_custom_call" | custom-call | bytes 83886080 | tf_op jit(solution)/shard_map/pallas_call | solution.py:146
  207.1 24.2 %shard_map.215 = bf16[512,1024]{1,0:T(8,128)(2,1)S(1)} custom-call(bf16[128,1024]{1,0:T(8,128)(2,1)S(1)} %add_convert_fusion.2.x_ref), custom_call_target="tpu_custom_call" | custom-call | bytes 83886080 | tf_op jit(solution)/shard_map/pallas_call | solution.py:125
  245.5 24.4 %shard_map.216 = f32[128,1024]{1,0:T(8,128)S(1)} custom-call(bf16[512,1024]{1,0:T(8,128)(2,1)S(1)} %convolution_convert_fusion.10.x_ref), custom_call_target="tpu_custom_call" | custom-call | bytes 83886080 | tf_op jit(solution)/shard_map/pallas_call | solution.py:146
  270.5 24.2 %shard_map.217 = bf16[512,1024]{1,0:T(8,128)(2,1)S(1)} custom-call(bf16[128,1024]{1,0:T(8,128)(2,1)S(1)} %add_convert_fusion.1.x_ref), custom_call_target="tpu_custom_call" | custom-call | bytes 83886080 | tf_op jit(solution)/shard_map/pallas_call | solution.py:125
  317.4 24.4 %shard_map.218 = f32[128,1024]{1,0:T(8,128)S(1)} custom-call(bf16[512,1024]{1,0:T(8,128)(2,1)S(1)} %fusion.45.x_ref), custom_call_target="tpu_custom_call" | custom-call | bytes 83886080 | tf_op jit(solution)/shard_map/pallas_call | solution.py:146
  343.2 24.4 %shard_map.220 = f32[128,1024]{1,0:T(8,128)S(1)} custom-call(bf16[512,1024]{1,0:T(8,128)(2,1)S(1)} %convolution_convert_fusion.9.x_ref), custom_call_target="tpu_custom_call" | custom-call | bytes 83886080 | tf_op jit(solution)/shard_map/pallas_call | solution.py:146
  368.9 24.2 %shard_map.221 = bf16[512,1024]{1,0:T(8,128)(2,1)S(1)} custom-call(bf16[128,1024]{1,0:T(8,128)(2,1)S(1)} %convert_element_type.281.x_ref), custom_call_target="tpu_custom_call" | custom-call | bytes 83886080 | tf_op jit(solution)/shard_map/pallas_call | solution.py:125
  402.8 14.7 %all_to_all.32 = bf16[4,32,1024]{2,1,0:T(8,128)(2,1)S(1)} all-to-all(bf16[4,32,1024]{2,1,0:T(8,128)(2,1)S(1)} %bitcast.381), channel_id=1, replica_groups=mesh['group'=4,'replica'=8] {'group'}, dimensions={0} | all-to-all | bytes 524288 | tf_op jit(solution)/shard_map/all_to_all | solution.py:231
  421.4 18.3 %shard_map.222 = f32[128,1024]{1,0:T(8,128)S(1)} custom-call(bf16[512,1024]{1,0:T(8,128)(2,1)S(1)} %convolution_convert_fusion.7.x_ref), custom_call_target="tpu_custom_call" | custom-call | bytes 83886080 | tf_op jit(solution)/shard_map/pallas_call | solution.py:146
  440.8 26.1 %shard_map.223 = bf16[512,1024]{1,0:T(8,128)(2,1)S(1)} custom-call(bf16[128,1024]{1,0:T(8,128)(2,1)S(1)} %convert_element_type.293.x_ref, bf16[32,8192]{1,0:T(8,128)(2,1)S(1)} %copy-done.3), custom_call_target="tpu_custom_call" | custom-call | bytes 83886080 | tf_op jit(solution)/shard_map/pallas_call | solution.py:125
  499.0 18.4 %shard_map.224 = f32[128,1024]{1,0:T(8,128)S(1)} custom-call(bf16[512,1024]{1,0:T(8,128)(2,1)S(1)} %convolution_convert_fusion.8.x_ref), custom_call_target="tpu_custom_call" | custom-call | bytes 83886080 | tf_op jit(solution)/shard_map/pallas_call | solution.py:146
  520.9 24.4 %shard_map.225 = bf16[512,1024]{1,0:T(8,128)(2,1)S(1)} custom-call(bf16[128,1024]{1,0:T(8,128)(2,1)S(1)} %convert_element_type.299.x_ref, bf16[32,4096]{1,0:T(8,128)(2,1)S(1)} %copy-done.15, bf16[256,8192]{1,0:T(8,128)(2,1)S(1)} %copy-done.2), custom_call_target="tpu_custom_call" | custom-call | bytes 83886080 | tf_op jit(solution)/shard_map/pallas_call | solution.py:125
  563.2 14.3 %all_to_all.33 = bf16[4,32,1024]{2,1,0:T(8,128)(2,1)S(1)} all-to-all(bf16[4,32,1024]{2,1,0:T(8,128)(2,1)S(1)} %bitcast.384), channel_id=1, replica_groups=mesh['group'=4,'replica'=8] {'group'}, dimensions={0} | all-to-all | bytes 524288 | tf_op jit(solution)/shard_map/all_to_all | solution.py:231
  586.5 18.5 %shard_map.226 = f32[128,1024]{1,0:T(8,128)S(1)} custom-call(bf16[512,1024]{1,0:T(8,128)(2,1)S(1)} %convolution_convert_fusion.6.x_ref, bf16[32,8192]{1,0:T(8,128)(2,1)S(1)} %copy-done.4), custom_call_target="tpu_custom_call" | custom-call | bytes 83886080 | tf_op jit(solution)/shard_map/pallas_call | solution.py:146
  605.6 10.0 %shard_map.227 = f32[16,256]{1,0:T(8,128)S(1)} custom-call(f32[64,256]{1,0:T(8,128)S(1)} %bitcast.349), custom_call_target="tpu_custom_call" | custom-call | bytes 2621440 | tf_op jit(solution)/shard_map/pallas_call | solution.py:146
  615.6 22.8 %psum.7 = f32[48,128]{1,0:T(8,128)S(1)} all-reduce(f32[48,128]{1,0:T(8,128)S(1)} %maximum_bitcast_fusion), channel_id=1, replica_groups=mesh['group'=4,'replica'=8] {'replica'}, use_global_device_ids=true, to_apply=%region_43.44 | all-reduce | flops 6144 | bytes 49152 | tf_op jit(solution)/shard_map/psum | solution.py:366
  665.9 17.8 %all-gather.20.cloned.1.call-done = bf16[256,4096]{1,0:T(8,128)(2,1)} async-done(((bf16[32,4096]{1,0:T(8,128)(2,1)}), bf16[256,4096]{1,0:T(8,128)(2,1)}) %all-gather.20.cloned.1.call-update) | async-done | bytes 2097168 | tf_op jit(solution)/shard_map/all_gather | solution.py:299
  (467 shorter events, 187.5 us)
Async XLA Ops:
  7.2 102.0 %all-gather.10.cloned.1.call-start = ((), (), s32[]{:S(2)}) async-start(), calls=%async_computation.10 | async-start | bytes 1769472 | tf_op jit(solution)/shard_map/all_gather | solution.py:234
  23.6 147.9 %all-gather.14.cloned.1.call-start = ((), (), s32[]{:S(2)}) async-start(), calls=%async_computation.12 | async-start | bytes 1769472 | tf_op jit(solution)/shard_map/all_gather | solution.py:234
  25.7 35.3 %copy-start.26 = (bf16[1,128,1024]{2,1,0:T(8,128)(2,1)S(1)}, bf16[1,128,1024]{2,1,0:T(8,128)(2,1)}, u32[]{:S(2)}) copy-start(bf16[1,128,1024]{2,1,0:T(8,128)(2,1)} %param.12) | copy-start | bytes 786436
  47.7 127.0 %all-gather.12.cloned.1.call-start = ((), (), s32[]{:S(2)}) async-start(), calls=%async_computation.11 | async-start | bytes 2359296 | tf_op jit(solution)/shard_map/all_gather | solution.py:234
  62.2 232.6 %all-gather.16.cloned.1.call-start = ((), (), s32[]{:S(2)}) async-start(), calls=%async_computation.13 | async-start | bytes 2359296 | tf_op jit(solution)/shard_map/all_gather | solution.py:234
  62.8 45.1 %copy-start.79 = (bf16[2,1024]{1,0:T(2,128)(2,1)S(1)}, bf16[2,1024]{1,0:T(2,128)(2,1)}, u32[]{:S(2)}) copy-start(bf16[2,1024]{1,0:T(2,128)(2,1)} %param.21) | copy-start | bytes 12292
  81.4 27.7 %copy-start.7 = (bf16[512,1024]{1,0:T(8,128)(2,1)S(1)}, bf16[512,1024]{1,0:T(8,128)(2,1)}, u32[]{:S(2)}) copy-start(bf16[512,1024]{1,0:T(8,128)(2,1)} %copy-done.6) | copy-start | bytes 3145732
  108.9 292.8 %reduce-scatter.5.cloned.1.call-start = ((), (), s32[]{:S(2)}) async-start(), calls=%async_computation.14 | async-start | bytes 4718592 | tf_op jit(solution)/shard_map/reduce_scatter | solution.py:290
  146.9 59.7 %copy-start.20 = (f32[128,1024]{1,0:T(8,128)}, f32[128,1024]{1,0:T(8,128)S(1)}, u32[]{:S(2)}) copy-start(f32[128,1024]{1,0:T(8,128)S(1)} %get-tuple-element.51) | copy-start | bytes 1572868
  206.7 63.2 %copy-start.22 = (f32[128,1024]{1,0:T(8,128)}, f32[128,1024]{1,0:T(8,128)S(1)}, u32[]{:S(2)}) copy-start(f32[128,1024]{1,0:T(8,128)S(1)} %get-tuple-element.49) | copy-start | bytes 1572868
  244.4 148.8 %copy-start.37 = (bf16[4,512,64]{1,2,0:T(8,128)(2,1)}, bf16[4,512,64]{1,2,0:T(8,128)(2,1)S(1)}, u32[]{:S(2)}) copy-start(bf16[4,512,64]{1,2,0:T(8,128)(2,1)S(1)} %convolution_convert_fusion.14) | copy-start | bytes 786436
  313.1 165.9 %reduce-scatter.7.cloned.1.call-start = ((), (), s32[]{:S(2)}) async-start(), calls=%async_computation.15 | async-start | bytes 2359296 | tf_op jit(solution)/shard_map/reduce_scatter | solution.py:290
  313.5 28.3 %copy-start.46 = (bf16[4,256,1024]{2,1,0:T(8,128)(2,1)S(1)}, bf16[4,256,1024]{2,1,0:T(8,128)(2,1)}, u32[]{:S(2)}) copy-start(bf16[4,256,1024]{2,1,0:T(8,128)(2,1)} %copy-done.45) | copy-start | bytes 6291460
  313.5 28.3 %copy-start.93 = (bf16[512,1024]{1,0:T(8,128)(2,1)S(1)}, bf16[512,1024]{1,0:T(8,128)(2,1)}, u32[]{:S(2)}) copy-start(bf16[512,1024]{1,0:T(8,128)(2,1)} %copy-done.92) | copy-start | bytes 3145732
  401.6 117.0 %all-gather.18.cloned.1.call-start = ((), (), s32[]{:S(2)}) async-start(), calls=%async_computation.16 | async-start | bytes 4718592 | tf_op jit(solution)/shard_map/all_gather | solution.py:299
  418.7 143.4 %reduce-scatter.9.cloned.1.call-start = ((), (), s32[]{:S(2)}) async-start(), calls=%async_computation.17 | async-start | bytes 4718592 | tf_op jit(solution)/shard_map/reduce_scatter | solution.py:290
  421.4 45.5 %copy-start.89 = (f32[512,1024]{1,0:T(8,128)S(1)}, f32[512,1024]{1,0:T(8,128)}, u32[]{:S(2)}) copy-start(f32[512,1024]{1,0:T(8,128)} %copy-done.88) | copy-start | bytes 6291460
  480.7 13.3 %all-to-all-start.4 = ((bf16[4,32,768]{2,1,0:T(8,128)(2,1)}), bf16[4,32,768]{2,1,0:T(8,128)(2,1)S(1)}, u32[]{:S(2)}, u32[]{:S(2)}) async-start(bf16[4,32,768]{2,1,0:T(8,128)(2,1)} %bitcast.341), calls=%async_computation.8 | async-start | bytes 393216 | tf_op jit(solution)/shard_map/all_to_all | solution.py:231
  487.7 91.7 %all-gather.22.cloned.1.call-start = ((), (), s32[]{:S(2)}) async-start(), calls=%async_computation.20 | async-start | bytes 2359296 | tf_op jit(solution)/shard_map/all_gather | solution.py:299
  495.2 144.4 %reduce-scatter.11.cloned.1.call-start = ((), (), s32[]{:S(2)}) async-start(), calls=%async_computation.18 | async-start | bytes 2359296 | tf_op jit(solution)/shard_map/reduce_scatter | solution.py:290
  562.0 93.0 %all-gather.24.cloned.1.call-start = ((), (), s32[]{:S(2)}) async-start(), calls=%async_computation.21 | async-start | bytes 4718592 | tf_op jit(solution)/shard_map/all_gather | solution.py:299
  586.5 52.0 %copy-start.29 = (f32[128,1024]{1,0:T(8,128)S(1)}, f32[128,1024]{1,0:T(8,128)}, u32[]{:S(2)}) copy-start(f32[128,1024]{1,0:T(8,128)} %copy-done.28) | copy-start | bytes 1572868
  641.2 10.9 %all-to-all-start.3 = ((bf16[4,32,768]{2,1,0:T(8,128)(2,1)}), bf16[4,32,768]{2,1,0:T(8,128)(2,1)S(1)}, u32[]{:S(2)}, u32[]{:S(2)}) async-start(bf16[4,32,768]{2,1,0:T(8,128)(2,1)} %bitcast.343), calls=%async_computation.7 | async-start | bytes 393216 | tf_op jit(solution)/shard_map/all_to_all | solution.py:231
  645.8 37.9 %all-gather.20.cloned.1.call-start = ((), (), s32[]{:S(2)}) async-start(), calls=%async_computation.19 | async-start | bytes 2359296 | tf_op jit(solution)/shard_map/all_gather | solution.py:299
  (86 other events, 670.6 us)
Sparse Core Ops, SparseCore 0:
  23.7 24.6 all-gather.9
  50.9 25.5 all-gather.13
  79.0 27.7 all-gather.11
  109.1 31.1 all-gather.15
  313.2 54.5 reduce-scatter.4
  401.8 44.4 reduce-scatter.6
  448.7 36.5 all-gather.17
  489.3 51.1 reduce-scatter.8
  542.3 27.7 all-gather.21
  573.9 41.0 reduce-scatter.10
  617.5 36.6 all-gather.23
  655.9 27.7 all-gather.19
where the time goes:
time: 704 us; the launch traced here: 698 us
  Pallas kernels  377 us (54%)
  blocking collectives  99.7 us (14%)
  local copies, waits for them, and re-layouts  84.2 us (12%)
  matrix products  53.4 us (8%)
  other arithmetic  29.7 us (4%)
  waiting for transfers between devices  24.7 us (4%)
  between operations  16.6 us (2%)
  starting transfers between devices  13.3 us (2%)
    pallas_call x8, Pallas kernels, gather_rows(): pl.pallas_call(functools.partial(gather_kernel, groups), out_shape=jax.Sh...  189 us
    pallas_call x9, Pallas kernels, scatter_rows(): pl.pallas_call(functools.partial(scatter_kernel, groups), out_shape=jax.S...  187 us
    all_to_all x4, blocking collectives, exchange(): lax.all_to_all(block, 'group', split_axis=0, concat_axis=0, tiled=True)  63.7 us
    unnamed x230, local copies, waits for them, and re-layouts  43 us
    psum x1, blocking collectives, local(): total = lax.psum(flat, 'replica').reshape(-1)  22.8 us
    all_gather x4, waiting for transfers between devices, share_pair(): return lax.all_gather(mine, 'replica', axis=0, tiled=True)  17.9 us
    dot_general x8, matrix products, dot_nt(): lax.dot_general(a, b, (((1,), (1,)), ((), ())), preferred_element_type=F32)  15.6 us
  transfers between devices with their start and end apart: 14, of which 3 were waited for; matrix products, arithmetic and copies ran while one was open for 17% of the time, Pallas kernels for 54%

commit v1 on v0

v1 whole, which is shorter than its diff:
```python
import functools

import jax
import jax.numpy as jnp
from jax import lax
from jax.experimental import pallas as pl
from jax.experimental.pallas import tpu as pltpu
from jax.sharding import PartitionSpec as P

HEADS = 16
HEAD_DIM = 64

EPS = 1e-05
NEG = -1e30
GELU_C = 0.7978845608028654
GELU_A = 0.044715
F32 = jnp.float32
B16 = jnp.bfloat16
MESH = pl.DeviceIdType.MESH
CH = 2

VMEM = pl.BlockSpec(memory_space=pltpu.VMEM)
ANY = pl.BlockSpec(memory_space=pl.ANY)


def norm_apply(values_in, gain_row, bias_row):
    row_mean = jnp.mean(values_in, axis=-1, keepdims=True)
    centered = values_in - row_mean
    variance = jnp.mean(centered * centered, axis=-1, keepdims=True)
    inverse = lax.rsqrt(variance + EPS)
    normed = centered * inverse
    return (normed * gain_row + bias_row, normed, inverse)


def norm_back(grad_in, normed, inverse, gain_row):
    scaled = grad_in * gain_row
    return inverse * (
        scaled
        - jnp.mean(scaled, axis=-1, keepdims=True)
        - normed * jnp.mean(scaled * normed, axis=-1, keepdims=True)
    )


def gelu_parts(pre_act):
    tanh_val = jnp.tanh(GELU_C * (pre_act + GELU_A * pre_act * pre_act * pre_act))
    gelu_value = 0.5 * pre_act * (1.0 + tanh_val)
    gelu_slope = 0.5 * (1.0 + tanh_val) + 0.5 * pre_act * (1.0 - tanh_val * tanh_val) * GELU_C * (
        1.0 + 3.0 * GELU_A * pre_act * pre_act
    )
    return (gelu_value, gelu_slope)


def dot(a, b):
    return jnp.dot(a, b, preferred_element_type=F32)


def dot_nt(a, b):
    return lax.dot_general(a, b, (((1,), (1,)), ((), ())), preferred_element_type=F32)


def dot_tn(a, b):
    return lax.dot_general(a, b, (((0,), (0,)), ((), ())), preferred_element_type=F32)


def greet_line(n, me):
    barrier = pltpu.get_barrier_semaphore()
    for there, peer in ((me > 0, me - 1), (me < n - 1, me + 1)):

        @pl.when(there)
        def _():
            pl.semaphore_signal(barrier, inc=1, device_id={"group": peer}, device_id_type=MESH)

    beside_me = (me > 0).astype(jnp.int32) + (me < n - 1).astype(jnp.int32)
    pl.semaphore_wait(barrier, beside_me)


def beside(way, me):
    return me + 1 if way == 0 else me - 1


def line_gather(n, me, buf, rows, send_sems, recv_sems, on_block):
    part = rows // CH

    def copy(way, step, chunk, block):
        here = pl.ds(pl.multiple_of(block * rows + chunk * part, part), part)
        return pltpu.make_async_remote_copy(
            src_ref=buf.at[here],
            dst_ref=buf.at[here],
            send_sem=send_sems.at[way, step, chunk],
            recv_sem=recv_sems.at[way, step, chunk],
            device_id={"group": beside(way, me)},
            device_id_type=MESH,
        )

    def block_of(way, step):
        return me - step if way == 0 else me + step

    def have(way, step):
        return me - step >= 0 if way == 0 else me + step < n

    def onward(way):
        return me < n - 1 if way == 0 else me > 0

    for chunk in range(CH):
        for way in (0, 1):

            @pl.when(onward(way))
            def _():
                copy(way, 0, chunk, me).start()

    on_block(me)

    def advance(step, carry):
        for chunk in range(CH):
            for way in (0, 1):

                @pl.when(have(way, step))
                def _():
                    copy(way, step - 1, chunk, block_of(way, step)).wait_recv()

                @pl.when(have(way, step) & onward(way) & (step < n - 1))
                def _():
                    copy(way, step, chunk, block_of(way, step)).start()

        for way in (0, 1):

            @pl.when(have(way, step))
            def _():
                on_block(block_of(way, step))

        return carry

    lax.fori_loop(1, n, advance, 0)

    def drain(step, carry):
        for way in (0, 1):

            @pl.when(have(way, step) & onward(way))
            def _():
                for chunk in range(CH):
                    copy(way, step, chunk, block_of(way, step)).wait_send()

        return carry

    lax.fori_loop(0, n - 1, drain, 0)


def line_scatter(n, me, part, hold, recv, send, final, send_sems, recv_sems):
    def copy(way, step, chunk):
        return pltpu.make_async_remote_copy(
            src_ref=send.at[way, step, chunk],
            dst_ref=recv.at[way, step, chunk],
            send_sem=send_sems.at[way, step, chunk],
            recv_sem=recv_sems.at[way, step, chunk],
            device_id={"group": beside(way, me)},
            device_id_type=MESH,
        )

    def goal(way, step):
        return n - 1 - step if way == 0 else step

    def onward(way, step):
        return goal(way, step) > me if way == 0 else goal(way, step) < me

    def fed(way):
        return me > 0 if way == 0 else me < n - 1

    def advance(step, carry):
        for way in (0, 1):
            on = onward(way, step)

            @pl.when(on)
            def _():
                part(goal(way, step), hold)
                for chunk in range(CH):

                    @pl.when(fed(way))
                    def _():
                        copy(way, step, chunk).wait_recv()
                        send[way, step, chunk] = (hold[chunk] + recv[way, step, chunk].astype(F32)).astype(B16)

                    @pl.when(jnp.logical_not(fed(way)))
                    def _():
                        send[way, step, chunk] = hold[chunk].astype(B16)

                    copy(way, step, chunk).start()

        return carry

    lax.fori_loop(0, n - 1, advance, 0)
    part(me, final)

    def collect(step, carry):
        for way in (0, 1):

            @pl.when((goal(way, step) == me) & fed(way))
            def _():
                for chunk in range(CH):
                    copy(way, step, chunk).wait_recv()
                    final[chunk] = final[chunk] + recv[way, step, chunk].astype(F32)

            @pl.when(onward(way, step))
            def _():
                for chunk in range(CH):
                    copy(way, step, chunk).wait_send()

        return carry

    lax.fori_loop(0, n - 1, collect, 0)


def line_sems(n):
    return [pltpu.SemaphoreType.DMA((2, n - 1, CH)) for _ in range(2)]


def scatter_scratch(n, rows, width):
    cols = width // CH
    return [
        pltpu.VMEM((CH, rows, cols), F32),
        pltpu.VMEM((2, n - 1, CH, rows, cols), B16),
        pltpu.VMEM((2, n - 1, CH, rows, cols), B16),
        pltpu.VMEM((CH, rows, cols), F32),
    ] + line_sems(n)


def rows_at(block, rows):
    return pl.ds(pl.multiple_of(block * rows, rows), rows)


def joined(final):
    return jnp.concatenate([final[chunk] for chunk in range(CH)], axis=1)


def weight_scratch(raw):
    outer, inner, piece, cols = raw.shape
    return [pltpu.VMEM((inner, outer, piece, cols), raw.dtype), pltpu.SemaphoreType.DMA((inner,))]


def weight_copies(raw, held, sems):
    return [
        pltpu.make_async_copy(raw.at[:, i], held.at[i], sems.at[i]) for i in range(held.shape[0])
    ]


def weight_cols(held, lo, size):
    inner, outer, piece, _ = held.shape
    return held[:, :, :, pl.ds(lo, size)].reshape(inner * outer * piece, size)


def weight_rows(held, chunk):
    inner, outer, piece, cols = held.shape
    if inner % CH == 0:
        take = inner // CH
        return held[chunk * take : (chunk + 1) * take].reshape(take * outer * piece, cols)
    take = piece // CH
    return held[0, 0, chunk * take : (chunk + 1) * take, :]


def params(collective_id):
    return pltpu.CompilerParams(
        collective_id=collective_id, has_side_effects=True, vmem_limit_bytes=48 * 1024 * 1024
    )


def cost(us):
    return pl.CostEstimate(flops=0, bytes_accessed=int(us * 3.3e6), transcendentals=0)


STEP_COLS = 256


def forward_kernel(n, layer, mode, *refs):
    refs = list(refs)
    lhs, w_any, res, vec = refs[:4]
    del refs[:4]
    raw = bias = None
    if mode:
        raw, bias = refs[:2]
        del refs[:2]
    after = refs.pop(0)
    y_ref = refs.pop(0)
    outs = []
    if mode:
        count = 3 if mode == "gelu" else 2
        outs = refs[:count]
        del refs[:count]
    w, w_sem, hold, recv, send, final, s_send, s_recv = refs[:8]
    del refs[:8]
    me = lax.axis_index("group")
    rows = res.shape[0]
    w_copy = pltpu.make_async_copy(w_any.at[layer], w, w_sem)
    w_copy.start()
    if mode:
        g_send, g_recv, held, h_sems = refs
        others = weight_copies(raw, held, h_sems)
        for other in others:
            other.start()
    greet_line(n, me)
    w_copy.wait()
    cols = w.shape[1] // CH

    def part(block, into):
        mine = lhs[rows_at(block, rows), :]
        for chunk in range(CH):
            into[chunk] = dot(mine, w[:, chunk * cols : (chunk + 1) * cols])

    line_scatter(n, me, part, hold, recv, send, final, s_send, s_recv)
    y = res[...] + joined(final) + vec[0:1, :]
    y_ref[...] = y
    if not mode:
        return
    all_ref = outs[0]
    all_ref[rows_at(me, rows), :] = norm_apply(y, vec[1:2, :], vec[2:3, :])[0].astype(B16)
    wide = held.shape[-1]
    size = STEP_COLS if wide % STEP_COLS == 0 else wide
    waited = []

    def on_block(block):
        if not waited:
            for other in others:
                other.wait()
            waited.append(True)
        here = rows_at(block, rows)

        def column(i, carry):
            lo = pl.multiple_of(i * size, size)
            value = dot(all_ref[here, :], weight_cols(held, lo, size)) + bias[:, pl.ds(lo, size)]
            if mode == "gelu":
                value, slope = gelu_parts(value)
                outs[2][here, pl.ds(lo, size)] = slope
            outs[1][here, pl.ds(lo, size)] = value.astype(B16)
            return carry

        lax.fori_loop(0, wide // size, column, 0)

    line_gather(n, me, all_ref, rows, g_send, g_recv, on_block)


def forward_step(lhs, w_all, layer, res, vec, collective_id, mode=None, raw=None, bias=None, after=None):
    n = lax.axis_size("group")
    rows, width = res.shape
    depth = w_all.shape[1]
    ins = [lhs, w_all, res, vec]
    specs = [VMEM, ANY, VMEM, VMEM]
    outs = [jax.ShapeDtypeStruct((rows, width), F32)]
    scratch = [pltpu.VMEM((depth, width), B16), pltpu.SemaphoreType.DMA] + scatter_scratch(n, rows, width)
    us = 21.0
    if mode:
        us = 42.0
        ins += [raw, bias]
        specs += [ANY, VMEM]
        wide = raw.shape[-1]
        outs += [
            jax.ShapeDtypeStruct((n * rows, width), B16),
            jax.ShapeDtypeStruct((n * rows, wide), B16),
        ]
        if mode == "gelu":
            outs.append(jax.ShapeDtypeStruct((n * rows, wide), F32))
        scratch += line_sems(n) + weight_scratch(raw)
    ins.append(lhs if after is None else after)
    specs.append(ANY)
    return pl.pallas_call(
        functools.partial(forward_kernel, n, layer, mode),
        out_shape=outs,
        in_specs=specs,
        out_specs=[VMEM] * len(outs),
        scratch_shapes=scratch,
        compiler_params=params(collective_id),
        cost_estimate=cost(us),
        name=f"forward_{mode}_{layer}",
    )(*ins)


def backward_kernel(n, layer, mode, *refs):
    refs = list(refs)
    lhs, raw, xin, gain, res = refs[:5]
    del refs[:5]
    if mode:
        w_any = refs.pop(0)
    if mode == "gelu":
        slope = refs.pop(0)
    after = refs.pop(0)
    g_ref, small_ref = refs[:2]
    del refs[:2]
    if mode:
        all_ref, t_ref = refs[:2]
        del refs[:2]
    if mode == "gelu":
        sum_ref = refs.pop(0)
    held, h_sems, hold, recv, send, final, s_send, s_recv = refs[:8]
    del refs[:8]
    me = lax.axis_index("group")
    rows = res.shape[0]
    others = weight_copies(raw, held, h_sems)
    for other in others:
        other.start()
    if mode:
        g_send, g_recv, w, w_sem = refs
        w_copy = pltpu.make_async_copy(w_any.at[layer], w, w_sem)
        w_copy.start()
    greet_line(n, me)
    for other in others:
        other.wait()

    def part(block, into):
        mine = lhs[rows_at(block, rows), :]
        for chunk in range(CH):
            into[chunk] = dot_nt(mine, weight_rows(held, chunk))

    line_scatter(n, me, part, hold, recv, send, final, s_send, s_recv)
    grad = joined(final)
    _, normed, inverse = norm_apply(xin[...], gain[...], gain[...])
    result = res[...] + norm_back(grad, normed, inverse, gain[...])
    g_ref[...] = result
    small_ref[0:1, :] = jnp.sum(grad * normed, axis=0, keepdims=True)
    small_ref[1:2, :] = jnp.sum(grad, axis=0, keepdims=True)
    small_ref[2:3, :] = jnp.sum(result, axis=0, keepdims=True)
    if not mode:
        return
    all_ref[rows_at(me, rows), :] = result.astype(B16)
    wide = w.shape[0]
    size = STEP_COLS if wide % STEP_COLS == 0 else wide
    if mode == "gelu":
        sum_ref[...] = jnp.zeros_like(sum_ref)
    waited = []

    def on_block(block):
        if not waited:
            w_copy.wait()
            waited.append(True)
        here = rows_at(block, rows)

        def column(i, carry):
            lo = pl.multiple_of(i * size, size)
            value = dot_nt(all_ref[here, :], w[pl.ds(lo, size), :])
            if mode == "gelu":
                value = value * slope[here, pl.ds(lo, size)]
                sum_ref[:, pl.ds(lo, size)] += jnp.sum(value, axis=0, keepdims=True)
            t_ref[here, pl.ds(lo, size)] = value.astype(B16)
            return carry

        lax.fori_loop(0, wide // size, column, 0)

    line_gather(n, me, all_ref, rows, g_send, g_recv, on_block)


def backward_step(lhs, raw, xin, gain, res, collective_id, mode=None, w_all=None, layer=0, slope=None, after=None):
    n = lax.axis_size("group")
    rows, width = res.shape
    ins = [lhs, raw, xin, gain, res]
    specs = [VMEM, ANY, VMEM, VMEM, VMEM]
    outs = [jax.ShapeDtypeStruct((rows, width), F32), jax.ShapeDtypeStruct((8, width), F32)]
    scratch = weight_scratch(raw) + scatter_scratch(n, rows, width)
    us = 21.0
    if mode:
        us = 42.0
        ins.append(w_all)
        specs.append(ANY)
        wide = w_all.shape[1]
        outs += [
            jax.ShapeDtypeStruct((n * rows, width), B16),
            jax.ShapeDtypeStruct((n * rows, wide), B16),
        ]
        scratch += line_sems(n) + [pltpu.VMEM((wide, width), B16), pltpu.SemaphoreType.DMA]
    if mode == "gelu":
        ins.append(slope)
        specs.append(VMEM)
        outs.append(jax.ShapeDtypeStruct((1, wide), F32))
    ins.append(lhs if after is None else after)
    specs.append(ANY)
    return pl.pallas_call(
        functools.partial(backward_kernel, n, layer, mode),
        out_shape=outs,
        in_specs=specs,
        out_specs=[VMEM] * len(outs),
        scratch_shapes=scratch,
        compiler_params=params(collective_id),
        cost_estimate=cost(us),
        name=f"backward_{mode}_{layer}",
    )(*ins)


def first_kernel(n, normed, x_ref, vec, after, all_ref, g_send, g_recv):
    me = lax.axis_index("group")
    rows = x_ref.shape[0]
    greet_line(n, me)
    value = x_ref[...]
    if normed:
        value = norm_apply(value.astype(F32), vec[0:1, :], vec[1:2, :])[0].astype(B16)
    all_ref[rows_at(me, rows), :] = value
    line_gather(n, me, all_ref, rows, g_send, g_recv, lambda block: None)


def first_gather(x, vec, collective_id, normed, after):
    n = lax.axis_size("group")
    rows, width = x.shape
    return pl.pallas_call(
        functools.partial(first_kernel, n, normed),
        out_shape=jax.ShapeDtypeStruct((n * rows, width), B16),
        in_specs=[VMEM, VMEM, ANY],
        out_specs=VMEM,
        scratch_shapes=line_sems(n),
        compiler_params=params(collective_id),
        cost_estimate=cost(21.0),
        name="first_gather" if normed else "cot_gather",
    )(x, vec, after)


def swap_kernel(n, count, *refs):
    ins, outs = refs[:count], refs[count + 1 : 2 * count + 1]
    send_sems, recv_sems, own_sems = refs[2 * count + 1 :]
    me = lax.axis_index("group")
    peers = [lax.rem(me + step, n) for step in range(1, n)]
    barrier = pltpu.get_barrier_semaphore()
    for peer in peers:
        pl.semaphore_signal(barrier, inc=1, device_id={"group": peer}, device_id_type=MESH)
    pl.semaphore_wait(barrier, n - 1)
    copies = []
    for k in range(count):
        for step, peer in enumerate(peers):
            copy = pltpu.make_async_remote_copy(
                src_ref=ins[k].at[peer],
                dst_ref=outs[k].at[me],
                send_sem=send_sems.at[k, step],
                recv_sem=recv_sems.at[k, step],
                device_id={"group": peer},
                device_id_type=MESH,
            )
            copy.start()
            copies.append(copy)
        own = pltpu.make_async_copy(ins[k].at[me], outs[k].at[me], own_sems.at[k])
        own.start()
        copies.append(own)
    for copy in copies:
        copy.wait()


def swap(blocks, collective_id, after=None, us=8.0):
    n = lax.axis_size("group")
    count = len(blocks)
    return pl.pallas_call(
        functools.partial(swap_kernel, n, count),
        out_shape=[jax.ShapeDtypeStruct(b.shape, b.dtype) for b in blocks],
        in_specs=[VMEM] * count + [ANY],
        out_specs=[VMEM] * count,
        scratch_shapes=[pltpu.SemaphoreType.DMA((count, n - 1)) for _ in range(2)]
        + [pltpu.SemaphoreType.DMA((count,))],
        compiler_params=params(collective_id),
        cost_estimate=cost(us),
        name=f"swap_{collective_id}",
    )(*blocks, blocks[0] if after is None else after)


def grads_kernel(n, a_ref, b_ref, c_ref, d_ref, o_ref, held, sems):
    own = held.shape[0]
    cols, width = b_ref.shape[1], d_ref.shape[1]
    folds = c_ref.shape[1] // own
    copies = []
    for i in range(n + folds):
        if i < n:
            lo, size = i * cols, cols
            value = dot_tn(a_ref[:, i * own : (i + 1) * own], b_ref[...])
        else:
            lo, size = n * cols + (i - n) * width, width
            value = dot_tn(c_ref[:, (i - n) * own : (i - n + 1) * own], d_ref[...])
        held[:, lo : lo + size] = value.astype(B16)
        copy = pltpu.make_async_copy(
            held.at[:, pl.ds(lo, size)], o_ref.at[:, pl.ds(lo, size)], sems.at[i]
        )
        copy.start()
        copies.append(copy)
    for copy in copies:
        copy.wait()


def grads_pair(a, b, c, d):
    n = lax.axis_size("group")
    own = a.shape[1] // n
    folds = c.shape[1] // own
    total = n * b.shape[1] + folds * d.shape[1]
    return pl.pallas_call(
        functools.partial(grads_kernel, n),
        out_shape=jax.ShapeDtypeStruct((own, total), B16),
        in_specs=[VMEM] * 4,
        out_specs=ANY,
        scratch_shapes=[pltpu.VMEM((own, total), B16), pltpu.SemaphoreType.DMA((n + folds,))],
        compiler_params=pltpu.CompilerParams(vmem_limit_bytes=32 * 1024 * 1024),
        cost_estimate=cost(4.0),
        name="weight_grads",
    )(a, b, c, d)


def attention(q, k, v, first_head, heads_here):
    tokens = q.shape[0]
    split = lambda m: m.reshape(tokens, heads_here, HEAD_DIM).transpose(1, 0, 2)
    q, k, v = split(q), split(k), split(v)
    head_ids = (first_head + jnp.arange(heads_here, dtype=jnp.int32)).astype(F32)
    slopes = 2.0 ** (-8.0 * (head_ids + 1.0) / HEADS)
    pos = jnp.arange(tokens, dtype=jnp.int32)
    offset = (pos[:, None] - pos[None, :]).astype(F32)
    raw = jnp.einsum("hqd,hkd->hqk", q, k, preferred_element_type=F32)
    scores = raw * HEAD_DIM ** (-0.5) - slopes[:, None, None] * offset[None]
    scores = jnp.where((offset >= 0.0)[None], scores, NEG)
    row_top = jnp.max(scores, axis=-1, keepdims=True)
    exps_raw = jnp.exp(scores - row_top)
    row_total = jnp.sum(exps_raw, axis=-1, keepdims=True)
    probs = (exps_raw * (1.0 / row_total)).astype(B16)
    context = jnp.einsum("hqk,hkd->hqd", probs, v, preferred_element_type=F32).astype(B16)
    return context.transpose(1, 0, 2).reshape(tokens, -1), (q, k, v, probs, context)


def attention_back(d_context, saved):
    q, k, v, probs, context = saved
    heads_here, tokens, _ = q.shape
    dc = d_context.reshape(tokens, heads_here, HEAD_DIM).transpose(1, 0, 2)
    d_probs = jnp.einsum("hqd,hkd->hqk", dc, v, preferred_element_type=F32)
    delta = jnp.sum(dc.astype(F32) * context.astype(F32), axis=-1, keepdims=True)
    ds = (probs.astype(F32) * (d_probs - delta)).astype(B16)
    scale = HEAD_DIM ** (-0.5)
    dq = jnp.einsum("hqk,hkd->hqd", ds, k, preferred_element_type=F32) * scale
    dk = jnp.einsum("hqk,hqd->hkd", ds, q, preferred_element_type=F32) * scale
    dv = jnp.einsum("hqk,hqd->hkd", probs, dc, preferred_element_type=F32)
    sums = (jnp.sum(dq, axis=1).reshape(-1), jnp.sum(dv, axis=1).reshape(-1))
    join = lambda m: m.astype(B16).transpose(1, 0, 2).reshape(tokens, -1)
    return jnp.concatenate([join(dq), join(dk), join(dv)], axis=1), sums


def local(
    inputs,
    cotangent,
    norm_gain,
    norm_bias,
    w_qkv,
    bias_qv,
    w_out,
    bias_out,
    w_up,
    bias_up,
    w_down,
    bias_down,
):
    groups = lax.axis_size("group")
    replicas = lax.axis_size("replica")
    me = lax.axis_index("group")
    copy_idx = lax.axis_index("replica")
    layers, own, _ = w_qkv.shape
    width = own * groups
    ff_own = w_down.shape[1]
    heads_here = HEADS // groups
    piece = own // replicas

    qkv_piece = lax.dynamic_slice_in_dim(w_qkv, copy_idx * piece, piece, axis=1)
    qkv_piece = qkv_piece.reshape(layers, piece, 3, groups, own).transpose(0, 3, 1, 2, 4)
    qkv_piece = qkv_piece.reshape(layers, groups, piece, 3 * own)
    up_piece = lax.dynamic_slice_in_dim(w_up, copy_idx * piece, piece, axis=1)
    up_piece = up_piece.reshape(layers, piece, groups, ff_own).transpose(0, 2, 1, 3)

    def share(block):
        full = lax.all_gather(block, "replica", axis=0)
        if piece % 16:
            full = full.transpose(1, 0, 2, 3).reshape(1, 1, width, -1)
        return full

    small = jnp.concatenate(
        [norm_gain, norm_bias, bias_qv.reshape(layers, 2, own), bias_out[:, None], bias_down[:, None]],
        axis=1,
    ).reshape(layers * 8, own)
    small = jnp.broadcast_to(small[None], (groups,) + small.shape)
    small, wq_first = swap([small, qkv_piece[0]], 0)
    wq = [share(wq_first)] + [None] * (layers - 1)
    wu = [None] * layers

    small = small.reshape(groups, layers, 8, own).astype(F32)
    rows_of = lambda i: small[:, :, i].transpose(1, 0, 2).reshape(layers, width)
    gains = [rows_of(0), rows_of(1)]
    shifts = [rows_of(2), rows_of(3)]
    qv_full = small[:, :, 4:6].transpose(1, 0, 2, 3).reshape(layers, 2 * width)
    q_bias = lax.dynamic_slice_in_dim(qv_full, me * own, own, axis=1)
    v_bias = lax.dynamic_slice_in_dim(qv_full, width + me * own, own, axis=1)
    qkv_bias = jnp.concatenate([q_bias, jnp.zeros_like(q_bias), v_bias], axis=1)
    out_bias, down_bias = rows_of(6), rows_of(7)
    up_bias = bias_up.astype(F32)

    x = inputs[0].astype(F32)
    vec0 = jnp.stack([gains[0][0], shifts[0][0]])
    a1_all = first_gather(inputs[0], vec0, 1, True, wq_first)
    later = [up_piece[l] for l in range(layers)] + [qkv_piece[l] for l in range(1, layers)]
    later = swap(later, 2, a1_all, 24.0)
    for l in range(layers):
        wu[l] = share(later[l])
        if l:
            wq[l] = share(later[layers + l - 1])
    cot_all = first_gather(cotangent[0], vec0, 3, False, later[0])

    full0 = wq[0].transpose(1, 0, 2, 3).reshape(width, 3 * own)
    proj = (dot(a1_all, full0) + qkv_bias[0]).astype(B16)
    kept = []
    for l in range(layers):
        cut = lambda i: proj[:, i * own : (i + 1) * own]
        context, attn_saved = attention(cut(0), cut(1), cut(2), me * heads_here, heads_here)
        vec = jnp.stack([out_bias[l], gains[1][l], shifts[1][l]])
        h, a2_all, hidden, slope = forward_step(
            context, w_out, l, x, vec, 10 + 4 * l, "gelu", wu[l], up_bias[l][None]
        )
        saved = (x, a1_all, attn_saved, context, h, a2_all, slope, hidden)
        if l + 1 < layers:
            vec = jnp.stack([down_bias[l], gains[0][l + 1], shifts[0][l + 1]])
            x, a1_all, proj = forward_step(
                hidden, w_down, l, h, vec, 11 + 4 * l, "bias", wq[l + 1], qkv_bias[l + 1][None]
            )
        else:
            vec = jnp.stack([down_bias[l], down_bias[l], down_bias[l]])
            (x,) = forward_step(hidden, w_down, l, h, vec, 11 + 4 * l)
        kept.append(saved)
    outputs = x.astype(B16)[None]

    def reduce_pair(grads):
        return lax.psum_scatter(grads, "replica", scatter_dimension=0, tiled=True)

    def share_pair(mine, cols, minor, collective_id, after=None):
        cut = groups * cols
        left = mine[:, :cut].reshape(piece, groups, cols).transpose(1, 0, 2)
        (left,) = swap([left], collective_id, after)
        left = left.reshape(groups, piece, minor, cols // minor).transpose(1, 2, 0, 3)
        mine = jnp.concatenate([left.reshape(piece, cut), mine[:, cut:]], axis=1)
        return lax.all_gather(mine, "replica", axis=0, tiled=True)

    def unpack_pair(full, cols):
        cut = groups * cols
        folds = (full.shape[1] - cut) // width
        rows = [full[:, cut + i * width : cut + (i + 1) * width] for i in range(folds)]
        return full[:, :cut].astype(F32), jnp.concatenate(rows, axis=0).astype(F32)

    g = cotangent[0].astype(F32)
    g_sum = jnp.sum(g, axis=0)
    g_all = cot_all
    smalls = [None] * layers
    ffn_sum = [None] * layers
    attn_sum = [None] * layers
    ffn_full = [None] * layers
    attn_full = [None] * layers
    zeros_qv = jnp.zeros((2 * width,), F32)
    pre = up_sum = None
    for l in reversed(range(layers)):
        x_in, a1_all, attn_saved, context, h, a2_all, slope, hidden = kept[l]
        if pre is None:
            d_pre = dot_nt(g_all, w_down[l]) * slope
            up_sum = jnp.sum(d_pre, axis=0)
            pre = d_pre.astype(B16)
        ffn_grads = grads_pair(a2_all, pre, hidden, g_all)
        ffn_sum[l] = reduce_pair(ffn_grads)
        down_sum = g_sum
        dh, small1, dh_all, dc = backward_step(
            pre, wu[l], h, gains[1][l][None], g, 30 + 4 * l, "plain", w_out, l
        )
        d_proj, (dq_sum, dv_sum) = attention_back(dc, attn_saved)
        attn_grads = grads_pair(a1_all, d_proj, context, dh_all)
        attn_sum[l] = reduce_pair(attn_grads)
        ffn_full[l] = share_pair(ffn_sum[l], ff_own, 1, 60 + 4 * l)
        ups = up_sum
        if l:
            below = kept[l - 1]
            g, small0, g_all, pre, up_sum = backward_step(
                d_proj, wq[l], x_in, gains[0][l][None], dh, 31 + 4 * l, "gelu", w_down, l - 1, below[6],
                after=attn_grads,
            )
            g_sum, up_sum = small0[2], up_sum[0]
        else:
            g, small0 = backward_step(
                d_proj, wq[l], x_in, gains[0][l][None], dh, 31 + 4 * l, after=attn_grads
            )
        attn_full[l] = share_pair(attn_sum[l], 3 * own, 3, 61 + 4 * l)
        qv = lax.dynamic_update_slice_in_dim(zeros_qv, dq_sum, me * own, axis=0)
        qv = lax.dynamic_update_slice_in_dim(qv, dv_sum, width + me * own, axis=0)
        smalls[l] = (
            jnp.concatenate([small0[0], small1[0], small0[1], small1[1], qv, small1[2], down_sum]),
            ups,
        )

    grads = [unpack_pair(attn_full[l], 3 * own) + unpack_pair(ffn_full[l], ff_own) for l in range(layers)]

    wide = jnp.stack([s[0] for s in smalls])
    per_owner = lambda lo, n: wide[:, lo * width : (lo + n) * width].reshape(layers, n, groups, own)
    gain_bias = per_owner(0, 4).transpose(2, 0, 1, 3)
    qv = wide[:, 4 * width : 6 * width].reshape(layers, groups, 2, own).transpose(1, 0, 2, 3)
    dense = per_owner(6, 2).transpose(2, 0, 1, 3)
    wide = jnp.concatenate([gain_bias, qv, dense], axis=2)
    (mine,) = swap([wide.reshape(groups, layers * 8, own)], 5)
    mine = jnp.sum(mine, axis=0)
    ups = jnp.stack([s[1] for s in smalls])
    flat = jnp.concatenate([mine.reshape(-1), ups.reshape(-1)]).reshape(-1, 128)
    total = lax.psum(flat, "replica").reshape(-1)
    cut = layers * 8 * own
    own_cols = total[:cut].reshape(layers, 8, own)
    up_total = total[cut:].reshape(layers, ff_own)
    qv_total = own_cols[:, 4:6].reshape(layers, 2 * own)
    stack = lambda i: jnp.stack([grads[l][i] for l in range(layers)])
    return (
        outputs,
        g[None],
        own_cols[:, 0:2],
        own_cols[:, 2:4],
        stack(0),
        qv_total,
        stack(1),
        own_cols[:, 6],
        stack(2),
        up_total,
        stack(3),
        own_cols[:, 7],
    )


def solution(mesh):
    rows = P("replica", "group", None)
    vec = P(None, None, "group")
    mat = P(None, "group", None)
    bias = P(None, "group")
    params_in = (vec, vec, mat, bias, mat, bias, mat, bias, mat, bias)
    return jax.shard_map(
        local,
        mesh=mesh,
        in_specs=(rows, rows) + params_in,
        out_specs=(rows, rows) + params_in,
        check_vma=False,
    )
```

time: 704 us -> 780 us (1.11)
  waiting for transfers between devices: 24.7 us -> 169 us
  blocking collectives: 99.7 us -> 22.7 us
  Pallas kernels: 377 us -> 424 us
  matrix products: 53.4 us -> 30.4 us
  starting transfers between devices: 13.3 us -> 0.74 us
    reduce_scatter x4, waiting for transfers between devices: 0.06 us -> 110 us  [reduce_pair(): return lax.psum_scatter(grads, 'replica', scatter_dimension=0, tiled=True)]
    all_to_all x4 -> x0, blocking collectives: 63.7 us -> none  [exchange(): lax.all_to_all(block, 'group', split_axis=0, concat_axis=0, tiled=True)]
    pallas_call x17 -> x21, Pallas kernels: 377 us -> 424 us  [the longest x4 153 us: forward_step(): pl.pallas_call(functools.partial(forward_kernel, n, layer, mode), out_sha...]
    all_gather x4, waiting for transfers between devices: 17.9 us -> 57.5 us  [share_pair(): return lax.all_gather(mine, 'replica', axis=0, tiled=True)]
    all_gather x1 -> x0, blocking collectives: 13.1 us -> none  [local(): small = lax.all_gather(small, 'group', axis=0).astype(F32)]
    all_to_all x2 -> x0, starting transfers between devices: 11.7 us -> none  [exchange(): lax.all_to_all(block, 'group', split_axis=0, concat_axis=0, tiled=True)]
    dot_general x8 -> x1, matrix products: 15.6 us -> 4.03 us  [dot_nt(): lax.dot_general(a, b, (((1,), (1,)), ((), ())), preferred_element_type=F32)]
    dot_general x8 -> x1, matrix products: 12.2 us -> 0.99 us  [dot(): return jnp.dot(a, b, preferred_element_type=F32)]
  transfers between devices with their start and end apart: 14 -> 12, of which waited for: 3 -> 6; matrix products, arithmetic and copies ran while one was open for 17% -> 7% of each run, Pallas kernels for 54% -> 31%
where the time goes in v1:
time: 780 us; the launch traced here: 771 us
  Pallas kernels  424 us (54%)
  waiting for transfers between devices  169 us (22%)
  local copies, waits for them, and re-layouts  78.6 us (10%)
  matrix products  30.4 us (4%)
  other arithmetic  29.8 us (4%)
  blocking collectives  22.7 us (3%)
  between operations  16.3 us (2%)
    pallas_call x4, Pallas kernels, forward_step(): pl.pallas_call(functools.partial(forward_kernel, n, layer, mode), out_sha...  153 us
    pallas_call x4, Pallas kernels, backward_step(): pl.pallas_call(functools.partial(backward_kernel, n, layer, mode), out_sh...  152 us
    reduce_scatter x4, waiting for transfers between devices, reduce_pair(): return lax.psum_scatter(grads, 'replica', scatter_dimension=0, tiled=True)  110 us
    pallas_call x7, Pallas kernels, swap(): pl.pallas_call(functools.partial(swap_kernel, n, count), out_shape=[jax.S...  66.9 us
    all_gather x4, waiting for transfers between devices, share_pair(): return lax.all_gather(mine, 'replica', axis=0, tiled=True)  57.5 us
    unnamed x207, local copies, waits for them, and re-layouts  50.2 us
    pallas_call x2, Pallas kernels, first_gather(): pl.pallas_call(functools.partial(first_kernel, n, normed), out_shape=jax....  38.6 us
    psum x1, blocking collectives, local(): total = lax.psum(flat, 'replica').reshape(-1)  22.7 us
  transfers between devices with their start and end apart: 12, of which 6 were waited for; matrix products, arithmetic and copies ran while one was open for 7% of the time, Pallas kernels for 31%

profile of v1, /device:TPU:0, one launch (start us, length us, event | category | flops | bytes accessed | tf_op | source)
XLA Modules:
  0.0 771.4 jit_solution(17714439750457128465)
XLA Ops:
  11.1 10.7 %swap_0.1 = (bf16[4,16,256]{2,1,0:T(8,128)(2,1)S(1)}, bf16[4,32,768]{2,1,0:T(8,128)(2,1)}) custom-call(bf16[4,16,256]{2,1,0:T(8,128)(2,1)S(1)} %broadcast_in_dim.63.refs_0_.refs_2_, bf16[4,32,768]{2,1,0:T(8,128)(2,1)S(1)} %squeeze.81.refs_1_, bf16[4,16,256]{2,1,0:T(8,128)(2,1)S(1)} %broadcast_in_dim.63.refs_0_.refs_2_), custom_call_target="tpu_custom_call" | custom-call | bytes 26400000 | tf_op jit(solution)/shard_map/swap_0/pallas_call | solution.py:541
  23.5 20.1 %first_gather.1.refs_3_.a_ref = bf16[512,1024]{1,0:T(8,128)(2,1)S(1)} custom-call(bf16[128,1024]{1,0:T(8,128)(2,1)S(1)} %bitcast.306, f32[2,1024]{1,0:T(2,128)S(1)} %pad_maximum_fusion.11.vec, bf16[4,32,768]{2,1,0:T(8,128)(2,1)} %get-tuple-element.44.after), custom_call_target="tpu_custom_call" | custom-call | bytes 69300000 | tf_op jit(solution)/shard_map/first_gather/pallas_call | solution.py:497
  44.6 17.6 %swap_2.1 = (bf16[4,32,1024]{2,1,0:T(8,128)(2,1)}, bf16[4,32,1024]{2,1,0:T(8,128)(2,1)}, bf16[4,32,768]{2,1,0:T(8,128)(2,1)}) custom-call(bf16[4,32,1024]{2,1,0:T(8,128)(2,1)S(1)} %get-tuple-element.115.refs_0_, bf16[4,32,1024]{2,1,0:T(8,128)(2,1)S(1)} %get-tuple-element.114.refs_1_, bf16[4,32,768]{2,1,0:T(8,128)(2,1)S(1)} %squeeze.89.refs_2_, ...), custom_call_target="tpu_custom_call" | custom-call | bytes 79200000 | tf_op jit(solution)/shard_map/swap_2/pallas_call | solution.py:541
  66.9 18.5 %cot_gather.1.d_ref = bf16[512,1024]{1,0:T(8,128)(2,1)S(1)} custom-call(bf16[128,1024]{1,0:T(8,128)(2,1)S(1)} %bitcast.299, f32[2,1024]{1,0:T(2,128)S(1)} %pad_maximum_fusion.11.vec, bf16[4,32,1024]{2,1,0:T(8,128)(2,1)} %get-tuple-element.45.after), custom_call_target="tpu_custom_call" | custom-call | bytes 69300000 | tf_op jit(solution)/shard_map/cot_gather/pallas_call | solution.py:497
  100.7 41.8 %forward_gelu_0.1 = (f32[128,1024]{1,0:T(8,128)S(1)}, bf16[512,1024]{1,0:T(8,128)(2,1)S(1)}, bf16[512,1024]{1,0:T(8,128)(2,1)S(1)}, f32[512,1024]{1,0:T(8,128)}) custom-call(bf16[512,256]{1,0:T(8,128)(2,1)S(1)} %copy.185.refs_0_.refs_6_.c_ref, bf16[2,256,1024]{2,1,0:T(8,128)(2,1)S(1)} %copy-done.4, f32[128,1024]{1,0:T(8,128)S(1)} %copy-done.27, ...), custom_call_target="tpu_custom_call" | custom-call | bytes 138600000 | tf_op jit(solution)/shard_map/forward_gelu_0/pallas_call | solution.py:362
  149.1 44.1 %forward_bias_0.1 = (f32[128,1024]{1,0:T(8,128)S(1)}, bf16[512,1024]{1,0:T(8,128)(2,1)S(1)}, bf16[512,768]{1,0:T(8,128)(2,1)S(1)}) custom-call(bf16[512,1024]{1,0:T(8,128)(2,1)S(1)} %copy-done.14, bf16[2,1024,1024]{2,1,0:T(8,128)(2,1)} %refs_5_.4, f32[128,1024]{1,0:T(8,128)S(1)} %copy-done.37, f32[3,1024]{1,0:T(4,128)S(1)} %pad_maximum_fusion.9.refs_3_, ...), custom_call_target="tpu_custom_call" | custom-call | bytes 138600000 | tf_op jit(solution)/shard_map/forward_bias_0/pallas_call | solution.py:362
  206.5 42.5 %forward_gelu_1.1 = (f32[128,1024]{1,0:T(8,128)S(1)}, bf16[512,1024]{1,0:T(8,128)(2,1)S(1)}, bf16[512,1024]{1,0:T(8,128)(2,1)S(1)}, f32[512,1024]{1,0:T(8,128)}) custom-call(bf16[512,256]{1,0:T(8,128)(2,1)S(1)} %copy-done.29, bf16[2,256,1024]{2,1,0:T(8,128)(2,1)S(1)} %copy-done.5, f32[128,1024]{1,0:T(8,128)S(1)} %copy-done.41, ...), custom_call_target="tpu_custom_call" | custom-call | bytes 138600000 | tf_op jit(solution)/shard_map/forward_gelu_1/pallas_call | solution.py:362
  255.0 40.8 %backward_plain_1.1 = (f32[128,1024]{1,0:T(8,128)S(1)}, f32[8,1024]{1,0:T(8,128)S(1)}, bf16[512,1024]{1,0:T(8,128)(2,1)S(1)}, bf16[512,256]{1,0:T(8,128)(2,1)S(1)}) custom-call(bf16[512,1024]{1,0:T(8,128)(2,1)S(1)} %get-tuple-element.95.refs_0_.refs_6_.b_ref, bf16[8,4,32,1024]{3,2,1,0:T(8,128)(2,1)} %bitcast.321, f32[128,1024]{1,0:T(8,128)S(1)} %get-tuple-element.53.refs_2_, ...), custom_call_target="tpu_custom_call" | custom-call | bytes 138600000 | tf_op jit(solution)/shard_map/backward_plain_1/pallas_call | solution.py:471
  316.6 45.1 %backward_gelu_0.1 = (f32[128,1024]{1,0:T(8,128)S(1)}, f32[8,1024]{1,0:T(8,128)S(1)}, bf16[512,1024]{1,0:T(8,128)(2,1)S(1)}, bf16[512,1024]{1,0:T(8,128)(2,1)S(1)}, f32[1,1024]{1,0:T(1,128)S(1)}) custom-call(bf16[512,768]{1,0:T(8,128)(2,1)S(1)} %copy-done.23, bf16[8,4,32,768]{3,2,1,0:T(8,128)(2,1)S(1)} %bitcast.294, f32[128,1024]{1,0:T(8,128)S(1)} %copy-done.42, ...), custom_call_target="tpu_custom_call" | custom-call | bytes 138600000 | tf_op jit(solution)/shard_map/backward_gelu_0/pallas_call | solution.py:471
  362.7 38.0 %backward_plain_0.1 = (f32[128,1024]{1,0:T(8,128)S(1)}, f32[8,1024]{1,0:T(8,128)S(1)}, bf16[512,1024]{1,0:T(8,128)(2,1)S(1)}, bf16[512,256]{1,0:T(8,128)(2,1)S(1)}) custom-call(bf16[512,1024]{1,0:T(8,128)(2,1)S(1)} %get-tuple-element.60.refs_0_.refs_6_.b_ref, bf16[8,4,32,1024]{3,2,1,0:T(8,128)(2,1)} %bitcast.319, f32[128,1024]{1,0:T(8,128)S(1)} %copy-done.38, ...), custom_call_target="tpu_custom_call" | custom-call | bytes 138600000 | tf_op jit(solution)/shard_map/backward_plain_0/pallas_call | solution.py:471
  438.4 20.1 %reduce-scatter.5.cloned.1.call-done = bf16[32,4096]{1,0:T(8,128)(2,1)} async-done(((bf16[256,4096]{1,0:T(8,128)(2,1)}), bf16[32,4096]{1,0:T(8,128)(2,1)}) %reduce-scatter.5.cloned.1.call-update) | async-done | bytes 262160 | tf_op jit(solution)/shard_map/reduce_scatter | solution.py:718
  459.4 7.6 swap_61.1
  469.1 34.2 %reduce-scatter.7.cloned.1.call-done = bf16[32,4096]{1,0:T(8,128)(2,1)} async-done(((bf16[256,4096]{1,0:T(8,128)(2,1)}), bf16[32,4096]{1,0:T(8,128)(2,1)}) %reduce-scatter.7.cloned.1.call-update) | async-done | bytes 262160 | tf_op jit(solution)/shard_map/reduce_scatter | solution.py:718
  504.3 7.6 swap_65.1
  514.0 44.5 %reduce-scatter.11.cloned.1.call-done = bf16[32,8192]{1,0:T(8,128)(2,1)} async-done(((bf16[256,8192]{1,0:T(8,128)(2,1)}), bf16[32,8192]{1,0:T(8,128)(2,1)}) %reduce-scatter.11.cloned.1.call-update) | async-done | bytes 524304 | tf_op jit(solution)/shard_map/reduce_scatter | solution.py:718
  559.6 8.5 %swap_64.1 = bf16[4,32,1024]{2,1,0:T(8,128)(2,1)S(1)} custom-call(bf16[4,32,1024]{2,1,0:T(8,128)(2,1)S(1)} %bitcast.295, bf16[4,32,1024]{2,1,0:T(8,128)(2,1)S(1)} %bitcast.296), custom_call_target="tpu_custom_call" | custom-call | bytes 26400000 | tf_op jit(solution)/shard_map/swap_64/pallas_call | solution.py:541
  573.1 28.5 %backward_None_0.1 = (f32[128,1024]{1,0:T(8,128)S(1)}, f32[8,1024]{1,0:T(8,128)S(1)}) custom-call(bf16[512,768]{1,0:T(8,128)(2,1)S(1)} %copy-done.21, bf16[8,4,32,768]{3,2,1,0:T(8,128)(2,1)S(1)} %bitcast.292, f32[128,1024]{1,0:T(8,128)S(1)} %copy-done.28, f32[1,1024]{1,0:T(1,128)S(1)} %bitcast.313, f32[128,1024]{1,0:T(8,128)S(1)} %copy-done.57, ...), custom_call_target="tpu_custom_call" | custom-call | bytes 69300000 | tf_op jit(solution)/shard_map/backward_None_0/pallas_call | solution.py:471
  602.4 11.2 %reduce-scatter.9.cloned.1.call-done = bf16[32,8192]{1,0:T(8,128)(2,1)} async-done(((bf16[256,8192]{1,0:T(8,128)(2,1)}), bf16[32,8192]{1,0:T(8,128)(2,1)}) %reduce-scatter.9.cloned.1.call-update) | async-done | bytes 524304 | tf_op jit(solution)/shard_map/reduce_scatter | solution.py:718
  614.7 8.5 %swap_60.1 = bf16[4,32,1024]{2,1,0:T(8,128)(2,1)S(1)} custom-call(bf16[4,32,1024]{2,1,0:T(8,128)(2,1)S(1)} %bitcast.297, bf16[4,32,1024]{2,1,0:T(8,128)(2,1)S(1)} %bitcast.298), custom_call_target="tpu_custom_call" | custom-call | bytes 26400000 | tf_op jit(solution)/shard_map/swap_60/pallas_call | solution.py:541
  626.0 6.4 swap_5.1
  632.4 22.7 %psum.7 = f32[48,128]{1,0:T(8,128)S(1)} all-reduce(f32[48,128]{1,0:T(8,128)S(1)} %maximum_bitcast_fusion), channel_id=1, replica_groups=mesh['group'=4,'replica'=8] {'replica'}, use_global_device_ids=true, to_apply=%region_13.14 | all-reduce | flops 6144 | bytes 49152 | tf_op jit(solution)/shard_map/psum | solution.py:792
  656.4 24.4 %forward_None_1.1 = f32[128,1024]{1,0:T(8,128)S(1)} custom-call(bf16[512,1024]{1,0:T(8,128)(2,1)S(1)} %copy-done.12, bf16[2,1024,1024]{2,1,0:T(8,128)(2,1)} %refs_5_.4, f32[128,1024]{1,0:T(8,128)S(1)} %copy-done.35, f32[3,1024]{1,0:T(4,128)S(1)} %stack.84.refs_3_, bf16[512,1024]{1,0:T(8,128)(2,1)S(1)} %copy-done.12), custom_call_target="tpu_custom_call" | custom-call | bytes 69300000 | tf_op jit(solution)/shard_map/forward_None_1/pallas_call | solution.py:362
  691.8 20.3 %all-gather.19.cloned.1.call-done = bf16[256,8192]{1,0:T(8,128)(2,1)} async-done(((bf16[32,8192]{1,0:T(8,128)(2,1)}), bf16[256,8192]{1,0:T(8,128)(2,1)}) %all-gather.19.cloned.1.call-update) | async-done | bytes 4194320 | tf_op jit(solution)/shard_map/all_gather | solution.py:726
  713.9 37.1 %all-gather.17.cloned.1.call-done = bf16[256,8192]{1,0:T(8,128)(2,1)} async-done(((bf16[32,8192]{1,0:T(8,128)(2,1)}), bf16[256,8192]{1,0:T(8,128)(2,1)}) %all-gather.17.cloned.1.call-update) | async-done | bytes 4194320 | tf_op jit(solution)/shard_map/all_gather | solution.py:726
  (388 shorter events, 154.3 us)
Async XLA Ops:
  7.2 79.1 %all-gather.21.cloned.1.call-start = ((), (), s32[]{:S(2)}) async-start(), calls=%async_computation.12 | async-start | bytes 1769472 | tf_op jit(solution)/shard_map/all_gather | solution.py:659
  21.8 77.3 %all-gather.23.cloned.1.call-start = ((), (), s32[]{:S(2)}) async-start(), calls=%async_computation.13 | async-start | bytes 2359296 | tf_op jit(solution)/shard_map/all_gather | solution.py:659
  23.4 43.1 %copy-start.81 = (bf16[2,1024]{1,0:T(2,128)(2,1)S(1)}, bf16[2,1024]{1,0:T(2,128)(2,1)}, u32[]{:S(2)}) copy-start(bf16[2,1024]{1,0:T(2,128)(2,1)} %param.21) | copy-start | bytes 12292
  23.4 43.5 %copy-start.33 = (bf16[1,128,1024]{2,1,0:T(8,128)(2,1)S(1)}, bf16[1,128,1024]{2,1,0:T(8,128)(2,1)}, u32[]{:S(2)}) copy-start(bf16[1,128,1024]{2,1,0:T(8,128)(2,1)} %param.13) | copy-start | bytes 786436
  62.2 83.2 %all-gather.25.cloned.1.call-start = ((), (), s32[]{:S(2)}) async-start(), calls=%async_computation.14 | async-start | bytes 1769472 | tf_op jit(solution)/shard_map/all_gather | solution.py:659
  62.9 142.5 %all-gather.27.cloned.1.call-start = ((), (), s32[]{:S(2)}) async-start(), calls=%async_computation.15 | async-start | bytes 2359296 | tf_op jit(solution)/shard_map/all_gather | solution.py:659
  63.5 395.0 %reduce-scatter.5.cloned.1.call-start = ((), (), s32[]{:S(2)}) async-start(), calls=%async_computation.4 | async-start | bytes 2359296 | tf_op jit(solution)/shard_map/reduce_scatter | solution.py:718
  206.5 44.5 %copy-start.62 = (bf16[2,1024,1024]{2,1,0:T(8,128)(2,1)S(1)}, bf16[2,1024,1024]{2,1,0:T(8,128)(2,1)}, u32[]{:S(2)}) copy-start(bf16[2,1024,1024]{2,1,0:T(8,128)(2,1)} %refs_5_.4) | copy-start | bytes 12582916
  250.9 44.9 %copy-start.34 = (f32[128,1024]{1,0:T(8,128)}, f32[128,1024]{1,0:T(8,128)S(1)}, u32[]{:S(2)}) copy-start(f32[128,1024]{1,0:T(8,128)S(1)} %get-tuple-element.53.refs_2_) | copy-start | bytes 1572868
  255.0 46.3 %copy-start.16 = (bf16[512,1024]{1,0:T(8,128)(2,1)}, bf16[512,1024]{1,0:T(8,128)(2,1)S(1)}, u32[]{:S(2)}) copy-start(bf16[512,1024]{1,0:T(8,128)(2,1)S(1)} %get-tuple-element.95.refs_0_.refs_6_.b_ref) | copy-start | bytes 3145732
  316.6 46.1 %copy-start.6 = (bf16[2,256,1024]{2,1,0:T(8,128)(2,1)S(1)}, bf16[2,256,1024]{2,1,0:T(8,128)(2,1)}, u32[]{:S(2)}) copy-start(bf16[2,256,1024]{2,1,0:T(8,128)(2,1)} %refs_5_.5) | copy-start | bytes 3145732
  316.6 46.1 %copy-start.38 = (f32[128,1024]{1,0:T(8,128)S(1)}, f32[128,1024]{1,0:T(8,128)}, u32[]{:S(2)}) copy-start(f32[128,1024]{1,0:T(8,128)} %copy-done.36) | copy-start | bytes 1572868
  362.7 38.1 %copy-start.18 = (bf16[512,1024]{1,0:T(8,128)(2,1)}, bf16[512,1024]{1,0:T(8,128)(2,1)S(1)}, u32[]{:S(2)}) copy-start(bf16[512,1024]{1,0:T(8,128)(2,1)S(1)} %get-tuple-element.60.refs_0_.refs_6_.b_ref) | copy-start | bytes 3145732
  418.4 85.0 %reduce-scatter.7.cloned.1.call-start = ((), (), s32[]{:S(2)}) async-start(), calls=%async_computation.6 | async-start | bytes 2359296 | tf_op jit(solution)/shard_map/reduce_scatter | solution.py:718
  418.9 139.5 %reduce-scatter.11.cloned.1.call-start = ((), (), s32[]{:S(2)}) async-start(), calls=%async_computation.10 | async-start | bytes 4718592 | tf_op jit(solution)/shard_map/reduce_scatter | solution.py:718
  428.6 184.9 %reduce-scatter.9.cloned.1.call-start = ((), (), s32[]{:S(2)}) async-start(), calls=%async_computation.8 | async-start | bytes 4718592 | tf_op jit(solution)/shard_map/reduce_scatter | solution.py:718
  438.1 246.4 %all-gather.13.cloned.1.call-start = ((), (), s32[]{:S(2)}) async-start(), calls=%async_computation.5 | async-start | bytes 2359296 | tf_op jit(solution)/shard_map/all_gather | solution.py:726
  469.1 216.6 %all-gather.15.cloned.1.call-start = ((), (), s32[]{:S(2)}) async-start(), calls=%async_computation.7 | async-start | bytes 2359296 | tf_op jit(solution)/shard_map/all_gather | solution.py:726
  504.3 65.1 %copy-start.21 = (bf16[512,768]{1,0:T(8,128)(2,1)S(1)}, bf16[512,768]{1,0:T(8,128)(2,1)}, u32[]{:S(2)}) copy-start(bf16[512,768]{1,0:T(8,128)(2,1)} %copy-done.20) | copy-start | bytes 2359300
  514.0 198.1 %all-gather.19.cloned.1.call-start = ((), (), s32[]{:S(2)}) async-start(), calls=%async_computation.11 | async-start | bytes 4718592 | tf_op jit(solution)/shard_map/all_gather | solution.py:726
  569.2 181.8 %all-gather.17.cloned.1.call-start = ((), (), s32[]{:S(2)}) async-start(), calls=%async_computation.9 | async-start | bytes 4718592 | tf_op jit(solution)/shard_map/all_gather | solution.py:726
  573.1 51.2 %copy-start.83 = (f32[1024]{0:T(1024)S(1)}, f32[1024]{0:T(1024)}, u32[]{:S(2)}) copy-start(f32[1024]{0:T(1024)} %get-tuple-element.94) | copy-start | bytes 12292
  573.1 51.4 %copy-start.82 = (f32[4,64]{1,0:T(4,128)S(1)}, f32[4,64]{1,0:T(4,128)}, u32[]{:S(2)}) copy-start(f32[4,64]{1,0:T(4,128)} %get-tuple-element.108) | copy-start | bytes 3076
  602.4 52.8 %copy-start.35 = (f32[128,1024]{1,0:T(8,128)S(1)}, f32[128,1024]{1,0:T(8,128)}, u32[]{:S(2)}) copy-start(f32[128,1024]{1,0:T(8,128)} %copy-done.34) | copy-start | bytes 1572868
  (72 other events, 219.3 us)
Sparse Core Ops, SparseCore 0:
  21.9 26.6 all-gather.20
  62.3 28.2 all-gather.22
  92.5 25.5 all-gather.24
  119.8 27.7 all-gather.26
  418.5 39.9 reduce-scatter.4
  462.2 41.1 reduce-scatter.6
  507.3 51.1 reduce-scatter.10
  562.4 51.1 reduce-scatter.8
  615.5 27.8 all-gather.12
  645.1 27.8 all-gather.14
  675.5 36.5 all-gather.18
  714.4 36.5 all-gather.16

commit v2 on v1

--- a/solution.py
+++ b/solution.py
@@ -269,7 +269,7 @@
 STEP_COLS = 256
 
 
-def forward_kernel(n, layer, mode, *refs):
+def forward_kernel(n, layer, mode, waits, *refs):
     refs = list(refs)
     lhs, w_any, res, vec = refs[:4]
     del refs[:4]
@@ -277,7 +277,7 @@
     if mode:
         raw, bias = refs[:2]
         del refs[:2]
-    after = refs.pop(0)
+    del refs[:waits]
     y_ref = refs.pop(0)
     outs = []
     if mode:
@@ -336,7 +336,7 @@
     line_gather(n, me, all_ref, rows, g_send, g_recv, on_block)
 
 
-def forward_step(lhs, w_all, layer, res, vec, collective_id, mode=None, raw=None, bias=None, after=None):
+def forward_step(lhs, w_all, layer, res, vec, collective_id, mode=None, raw=None, bias=None, after=()):
     n = lax.axis_size("group")
     rows, width = res.shape
     depth = w_all.shape[1]
@@ -357,10 +357,10 @@
         if mode == "gelu":
             outs.append(jax.ShapeDtypeStruct((n * rows, wide), F32))
         scratch += line_sems(n) + weight_scratch(raw)
-    ins.append(lhs if after is None else after)
-    specs.append(ANY)
+    ins += list(after)
+    specs += [ANY] * len(after)
     return pl.pallas_call(
-        functools.partial(forward_kernel, n, layer, mode),
+        functools.partial(forward_kernel, n, layer, mode, len(after)),
         out_shape=outs,
         in_specs=specs,
         out_specs=[VMEM] * len(outs),
@@ -371,7 +371,7 @@
     )(*ins)
 
 
-def backward_kernel(n, layer, mode, *refs):
+def backward_kernel(n, layer, mode, waits, *refs):
     refs = list(refs)
     lhs, raw, xin, gain, res = refs[:5]
     del refs[:5]
@@ -379,7 +379,7 @@
         w_any = refs.pop(0)
     if mode == "gelu":
         slope = refs.pop(0)
-    after = refs.pop(0)
+    del refs[:waits]
     g_ref, small_ref = refs[:2]
     del refs[:2]
     if mode:
@@ -444,7 +444,7 @@
     line_gather(n, me, all_ref, rows, g_send, g_recv, on_block)
 
 
-def backward_step(lhs, raw, xin, gain, res, collective_id, mode=None, w_all=None, layer=0, slope=None, after=None):
+def backward_step(lhs, raw, xin, gain, res, collective_id, mode=None, w_all=None, layer=0, slope=None, after=()):
     n = lax.axis_size("group")
     rows, width = res.shape
     ins = [lhs, raw, xin, gain, res]
@@ -466,10 +466,10 @@
         ins.append(slope)
         specs.append(VMEM)
         outs.append(jax.ShapeDtypeStruct((1, wide), F32))
-    ins.append(lhs if after is None else after)
-    specs.append(ANY)
+    ins += list(after)
+    specs += [ANY] * len(after)
     return pl.pallas_call(
-        functools.partial(backward_kernel, n, layer, mode),
+        functools.partial(backward_kernel, n, layer, mode, len(after)),
         out_shape=outs,
         in_specs=specs,
         out_specs=[VMEM] * len(outs),
@@ -590,6 +590,285 @@
     )(a, b, c, d)
 
 
+def digit(value, place):
+    return (value // 2**place) % 2
+
+
+def with_digit(value, place, wanted):
+    return value + (wanted - digit(value, place)) * 2**place
+
+
+def flipped(value, place):
+    return value + (1 - 2 * digit(value, place)) * 2**place
+
+
+def reduce_share_kernel(n, replicas, cols, minor, g_ref, after, o_ref, *refs):
+    own_half, first_in, acc, flow_in, landed = refs[:5]
+    sems = refs[5:]
+    pair_send, pair_recv, flow_send, flow_recv, swap_send, swap_recv = sems[:6]
+    out_send, out_recv, side_send, side_recv, load_sems = sems[6:]
+    me = lax.axis_index("group")
+    mine = lax.axis_index("replica")
+    core = digit(mine, 0)
+    spot = mine // 2
+    halves = replicas // 2
+    bits = halves.bit_length() - 1
+    total = g_ref.shape[2]
+    flow_cols = total // 2
+    orders = (list(range(bits)), list(range(bits))[::-1])
+    sibling = flipped(mine, 0)
+    peers = [lax.rem(me + step, n) for step in range(1, n)]
+    barrier = pltpu.get_barrier_semaphore()
+    for place in range(bits + 1):
+        pl.semaphore_signal(
+            barrier, inc=1, device_id={"replica": flipped(mine, place)}, device_id_type=MESH
+        )
+    for peer in peers:
+        pl.semaphore_signal(barrier, inc=1, device_id={"group": peer}, device_id_type=MESH)
+    loads = []
+    for q in range(halves):
+        load = pltpu.make_async_copy(g_ref.at[2 * q + core], own_half.at[q], load_sems.at[q])
+        load.start()
+        loads.append(load)
+    pl.semaphore_wait(barrier, bits + n)
+
+    def to_replica(src, dst, send_sem, recv_sem, target):
+        copy = pltpu.make_async_remote_copy(
+            src_ref=src,
+            dst_ref=dst,
+            send_sem=send_sem,
+            recv_sem=recv_sem,
+            device_id={"replica": target},
+            device_id_type=MESH,
+        )
+        copy.start()
+        return copy
+
+    sent = []
+    paired = []
+    for q in range(halves):
+        copy = to_replica(
+            g_ref.at[2 * q + 1 - core], first_in.at[q], pair_send.at[q], pair_recv.at[q], sibling
+        )
+        paired.append(copy)
+    sent += paired
+    for q in range(halves):
+        loads[q].wait()
+        paired[q].wait_recv()
+        acc[q] = (own_half[q].astype(F32) + first_in[q].astype(F32)).astype(B16)
+
+    def chosen(order, count, index):
+        spot_of = spot
+        for i in range(count):
+            spot_of = with_digit(spot_of, order[i], (index >> i) % 2)
+        return spot_of
+
+    slot = 0
+    for stage in range(bits):
+        started = []
+        for flow in (0, 1):
+            lanes = pl.ds(flow * flow_cols, flow_cols)
+            place = orders[flow][stage]
+            free = orders[flow][stage + 1 :]
+            for t in range(2 ** len(free)):
+                keep = chosen(free, len(free), t)
+                copy = to_replica(
+                    acc.at[flipped(keep, place), :, lanes],
+                    flow_in.at[flow, slot + t],
+                    flow_send.at[flow, slot + t],
+                    flow_recv.at[flow, slot + t],
+                    flipped(mine, place + 1),
+                )
+                started.append((copy, flow, slot + t, keep))
+        for copy, flow, at, keep in started:
+            copy.wait_recv()
+            lanes = slice(flow * flow_cols, (flow + 1) * flow_cols)
+            acc[keep, :, lanes] = (
+                acc[keep, :, lanes].astype(F32) + flow_in[flow, at].astype(F32)
+            ).astype(B16)
+            sent.append(copy)
+        slot += 2 ** (bits - 1 - stage)
+
+    swaps = []
+    for step, peer in enumerate(peers):
+        copy = pltpu.make_async_remote_copy(
+            src_ref=acc.at[spot, :, pl.ds(pl.multiple_of(peer * cols, 128), cols)],
+            dst_ref=landed.at[me],
+            send_sem=swap_send.at[step],
+            recv_sem=swap_recv.at[step],
+            device_id={"group": peer},
+            device_id_type=MESH,
+        )
+        copy.start()
+        swaps.append(copy)
+    landed[me] = acc[spot, :, pl.ds(pl.multiple_of(me * cols, 128), cols)]
+    o_ref[mine, :, n * cols :] = acc[spot, :, n * cols :]
+    for copy in swaps:
+        copy.wait_recv()
+    sent += swaps
+    inner = cols // minor
+    for src in range(n):
+        for m in range(minor):
+            lo = (m * n + src) * inner
+            o_ref[mine, :, lo : lo + inner] = landed[src, :, m * inner : (m + 1) * inner]
+
+    def place_out(spot_of, flow):
+        return o_ref.at[2 * spot_of + core, :, pl.ds(flow * flow_cols, flow_cols)]
+
+    sides = []
+
+    def to_side(spot_of, flow, index):
+        here = place_out(spot_of, flow)
+        sides.append(
+            to_replica(here, here, side_send.at[flow, index], side_recv.at[flow, index], sibling)
+        )
+
+    slot = 0
+    for stage in range(bits):
+        started = []
+        for flow in (0, 1):
+            order = orders[flow][::-1]
+            place = order[stage]
+            for t in range(2**stage):
+                here = place_out(chosen(order, stage, t), flow)
+                copy = to_replica(
+                    here,
+                    here,
+                    out_send.at[flow, slot + t],
+                    out_recv.at[flow, slot + t],
+                    flipped(mine, place + 1),
+                )
+                started.append((copy, flow, t))
+        if stage == 0:
+            for flow in (0, 1):
+                to_side(spot, flow, 0)
+        for copy, flow, t in started:
+            order = orders[flow][::-1]
+            copy.wait_recv()
+            to_side(flipped(chosen(order, stage, t), order[stage]), flow, 2**stage + t)
+            sent.append(copy)
+        slot += 2**stage
+    for copy in sides:
+        copy.wait_recv()
+    for copy in sent + sides:
+        copy.wait_send()
+
+
+def reduce_share(grads, cols, minor, collective_id, after):
+    n, replicas = lax.axis_size("group"), lax.axis_size("replica")
+    own, total = grads.shape
+    piece, halves = own // replicas, replicas // 2
+    dma = lambda *shape: pltpu.SemaphoreType.DMA(shape)
+    full = pl.pallas_call(
+        functools.partial(reduce_share_kernel, n, replicas, cols, minor),
+        out_shape=jax.ShapeDtypeStruct((replicas, piece, total), B16),
+        in_specs=[ANY, ANY],
+        out_specs=VMEM,
+        scratch_shapes=[
+            pltpu.VMEM((halves, piece, total), B16),
+            pltpu.VMEM((halves, piece, total), B16),
+            pltpu.VMEM((halves, piece, total), B16),
+            pltpu.VMEM((2, halves - 1, piece, total // 2), B16),
+            pltpu.VMEM((n, piece, cols), B16),
+            dma(halves),
+            dma(halves),
+            dma(2, halves),
+            dma(2, halves),
+            dma(n - 1),
+            dma(n - 1),
+            dma(2, halves),
+            dma(2, halves),
+            dma(2, halves),
+            dma(2, halves),
+            dma(halves),
+        ],
+        compiler_params=params(collective_id),
+        cost_estimate=cost(35.0),
+        name="reduce_share",
+    )(grads.reshape(replicas, piece, total), after)
+    return full.reshape(own, total)
+
+
+def small_sums_kernel(n, replicas, wide, ups, o_ref, landed, both, spread, *sems):
+    a_send, a_recv, b_send, b_recv = sems
+    me = lax.axis_index("group")
+    mine = lax.axis_index("replica")
+    rows = landed.shape[1]
+    peers = [lax.rem(me + step, n) for step in range(1, n)]
+    mates = [lax.rem(mine + step, replicas) for step in range(1, replicas)]
+    barrier = pltpu.get_barrier_semaphore()
+    for peer in peers:
+        pl.semaphore_signal(barrier, inc=1, device_id={"group": peer}, device_id_type=MESH)
+    for mate in mates:
+        pl.semaphore_signal(barrier, inc=1, device_id={"replica": mate}, device_id_type=MESH)
+    pl.semaphore_wait(barrier, n + replicas - 2)
+    copies = []
+    for step, peer in enumerate(peers):
+        copy = pltpu.make_async_remote_copy(
+            src_ref=wide.at[peer],
+            dst_ref=landed.at[me],
+            send_sem=a_send.at[step],
+            recv_sem=a_recv.at[step],
+            device_id={"group": peer},
+            device_id_type=MESH,
+        )
+        copy.start()
+        copies.append(copy)
+    landed[me] = wide[me]
+    for copy in copies:
+        copy.wait_recv()
+    total = landed[0]
+    for i in range(1, n):
+        total = total + landed[i]
+    both[0:rows, :] = total
+    both[rows:, :] = ups[...]
+    spread[mine] = both[...]
+    others = []
+    for step, mate in enumerate(mates):
+        copy = pltpu.make_async_remote_copy(
+            src_ref=both,
+            dst_ref=spread.at[mine],
+            send_sem=b_send.at[step],
+            recv_sem=b_recv.at[step],
+            device_id={"replica": mate},
+            device_id_type=MESH,
+        )
+        copy.start()
+        others.append(copy)
+    for copy in others:
+        copy.wait_recv()
+    total = spread[0]
+    for i in range(1, replicas):
+        total = total + spread[i]
+    o_ref[...] = total
+    for copy in copies + others:
+        copy.wait_send()
+
+
+def small_sums(wide, ups, collective_id):
+    n, replicas = lax.axis_size("group"), lax.axis_size("replica")
+    _, rows, own = wide.shape
+    lines = rows + ups.shape[0]
+    return pl.pallas_call(
+        functools.partial(small_sums_kernel, n, replicas),
+        out_shape=jax.ShapeDtypeStruct((lines, own), F32),
+        in_specs=[VMEM, VMEM],
+        out_specs=VMEM,
+        scratch_shapes=[
+            pltpu.VMEM((n, rows, own), F32),
+            pltpu.VMEM((lines, own), F32),
+            pltpu.VMEM((replicas, lines, own), F32),
+            pltpu.SemaphoreType.DMA((n - 1,)),
+            pltpu.SemaphoreType.DMA((n - 1,)),
+            pltpu.SemaphoreType.DMA((replicas - 1,)),
+            pltpu.SemaphoreType.DMA((replicas - 1,)),
+        ],
+        compiler_params=params(collective_id),
+        cost_estimate=cost(9.0),
+        name="small_sums",
+    )(wide, ups)
+
+
 def attention(q, k, v, first_head, heads_here):
     tokens = q.shape[0]
     split = lambda m: m.reshape(tokens, heads_here, HEAD_DIM).transpose(1, 0, 2)
@@ -717,10 +996,13 @@
     def reduce_pair(grads):
         return lax.psum_scatter(grads, "replica", scatter_dimension=0, tiled=True)
 
-    def share_pair(mine, cols, minor, collective_id, after=None):
+    def swap_pair(mine, cols, collective_id, after=None):
         cut = groups * cols
         left = mine[:, :cut].reshape(piece, groups, cols).transpose(1, 0, 2)
-        (left,) = swap([left], collective_id, after)
+        return swap([left], collective_id, after)[0]
+
+    def share_pair(left, mine, cols, minor):
+        cut = groups * cols
         left = left.reshape(groups, piece, minor, cols // minor).transpose(1, 2, 0, 3)
         mine = jnp.concatenate([left.reshape(piece, cut), mine[:, cut:]], axis=1)
         return lax.all_gather(mine, "replica", axis=0, tiled=True)
@@ -741,6 +1023,7 @@
     attn_full = [None] * layers
     zeros_qv = jnp.zeros((2 * width,), F32)
     pre = up_sum = None
+    waits = ()
     for l in reversed(range(layers)):
         x_in, a1_all, attn_saved, context, h, a2_all, slope, hidden = kept[l]
         if pre is None:
@@ -749,27 +1032,31 @@
             pre = d_pre.astype(B16)
         ffn_grads = grads_pair(a2_all, pre, hidden, g_all)
         ffn_sum[l] = reduce_pair(ffn_grads)
-        down_sum = g_sum
+        down_sum, ups = g_sum, up_sum
         dh, small1, dh_all, dc = backward_step(
-            pre, wu[l], h, gains[1][l][None], g, 30 + 4 * l, "plain", w_out, l
+            pre, wu[l], h, gains[1][l][None], g, 30 + 4 * l, "plain", w_out, l, after=(ffn_grads,) + waits
         )
         d_proj, (dq_sum, dv_sum) = attention_back(dc, attn_saved)
         attn_grads = grads_pair(a1_all, d_proj, context, dh_all)
-        attn_sum[l] = reduce_pair(attn_grads)
-        ffn_full[l] = share_pair(ffn_sum[l], ff_own, 1, 60 + 4 * l)
-        ups = up_sum
         if l:
-            below = kept[l - 1]
+            attn_sum[l] = reduce_pair(attn_grads)
+            ffn_left = swap_pair(ffn_sum[l], ff_own, 60 + 4 * l, attn_grads)
+            ffn_full[l] = share_pair(ffn_left, ffn_sum[l], ff_own, 1)
             g, small0, g_all, pre, up_sum = backward_step(
-                d_proj, wq[l], x_in, gains[0][l][None], dh, 31 + 4 * l, "gelu", w_down, l - 1, below[6],
-                after=attn_grads,
+                d_proj, wq[l], x_in, gains[0][l][None], dh, 31 + 4 * l, "gelu", w_down, l - 1, kept[l - 1][6],
+                after=(attn_grads, ffn_left),
             )
+            attn_left = swap_pair(attn_sum[l], 3 * own, 61 + 4 * l, small0)
+            attn_full[l] = share_pair(attn_left, attn_sum[l], 3 * own, 3)
+            waits = (attn_left,)
             g_sum, up_sum = small0[2], up_sum[0]
         else:
             g, small0 = backward_step(
-                d_proj, wq[l], x_in, gains[0][l][None], dh, 31 + 4 * l, after=attn_grads
+                d_proj, wq[l], x_in, gains[0][l][None], dh, 31 + 4 * l, after=(attn_grads,)
             )
-        attn_full[l] = share_pair(attn_sum[l], 3 * own, 3, 61 + 4 * l)
+            ffn_left = swap_pair(ffn_sum[l], ff_own, 60 + 4 * l, small0)
+            ffn_full[l] = share_pair(ffn_left, ffn_sum[l], ff_own, 1)
+            attn_full[l] = reduce_share(attn_grads, 3 * own, 3, 70, ffn_left)
         qv = lax.dynamic_update_slice_in_dim(zeros_qv, dq_sum, me * own, axis=0)
         qv = lax.dynamic_update_slice_in_dim(qv, dv_sum, width + me * own, axis=0)
         smalls[l] = (
@@ -785,14 +1072,10 @@
     qv = wide[:, 4 * width : 6 * width].reshape(layers, groups, 2, own).transpose(1, 0, 2, 3)
     dense = per_owner(6, 2).transpose(2, 0, 1, 3)
     wide = jnp.concatenate([gain_bias, qv, dense], axis=2)
-    (mine,) = swap([wide.reshape(groups, layers * 8, own)], 5)
-    mine = jnp.sum(mine, axis=0)
-    ups = jnp.stack([s[1] for s in smalls])
-    flat = jnp.concatenate([mine.reshape(-1), ups.reshape(-1)]).reshape(-1, 128)
-    total = lax.psum(flat, "replica").reshape(-1)
-    cut = layers * 8 * own
-    own_cols = total[:cut].reshape(layers, 8, own)
-    up_total = total[cut:].reshape(layers, ff_own)
+    ups = jnp.stack([s[1] for s in smalls]).reshape(-1, own)
+    total = small_sums(wide.reshape(groups, layers * 8, own), ups, 5)
+    own_cols = total[: layers * 8].reshape(layers, 8, own)
+    up_total = total[layers * 8 :].reshape(layers, ff_own)
     qv_total = own_cols[:, 4:6].reshape(layers, 2 * own)
     stack = lambda i: jnp.stack([grads[l][i] for l in range(layers)])
     return (

time: 780 us -> 631 us (0.81)
  waiting for transfers between devices: 169 us -> 1.44 us
  Pallas kernels: 424 us -> 453 us
  blocking collectives: 22.7 us -> 0 us
  local copies, waits for them, and re-layouts: 78.6 us -> 86.4 us
    reduce_scatter x4 -> x3, waiting for transfers between devices: 110 us -> 0.06 us  [reduce_pair(): return lax.psum_scatter(grads, 'replica', scatter_dimension=0, tiled=True)]
    all_gather x4 -> x3, waiting for transfers between devices: 57.5 us -> 0.02 us  [share_pair(): return lax.all_gather(mine, 'replica', axis=0, tiled=True)]
    pallas_call x8 -> x10, Pallas kernels: 305 us -> 351 us  [the longest x4 150 us: forward_step(): pl.pallas_call(functools.partial(forward_kernel, n, layer, mode, len(afte...]
    psum x1 -> x0, blocking collectives: 22.7 us -> none  [local(): total = lax.psum(flat, 'replica').reshape(-1)]
    pallas_call x7 -> x5, Pallas kernels: 66.9 us -> 49.3 us  [swap(): pl.pallas_call(functools.partial(swap_kernel, n, count), out_shape=[jax.S...]
    unnamed x207 -> x215, local copies, waits for them, and re-layouts: 50.2 us -> 50.2 us
  transfers between devices with their start and end apart: 12 -> 10, of which waited for: 6 -> 0; matrix products, arithmetic and copies ran while one was open for 7% -> 14% of each run, Pallas kernels for 31% -> 63%
where the time goes in v2:
time: 631 us; the launch traced here: 623 us
  Pallas kernels  453 us (72%)
  local copies, waits for them, and re-layouts  86.4 us (14%)
  matrix products  37.1 us (6%)
  other arithmetic  28.2 us (4%)
  between operations  16.3 us (3%)
    pallas_call x4, Pallas kernels, forward_step(): pl.pallas_call(functools.partial(forward_kernel, n, layer, mode, len(afte...  150 us
    pallas_call x4, Pallas kernels, backward_step(): pl.pallas_call(functools.partial(backward_kernel, n, layer, mode, len(aft...  146 us
    unnamed x215, local copies, waits for them, and re-layouts  50.2 us
    pallas_call x5, Pallas kernels, swap(): pl.pallas_call(functools.partial(swap_kernel, n, count), out_shape=[jax.S...  49.3 us
    pallas_call x1, Pallas kernels, reduce_share(): pl.pallas_call(functools.partial(reduce_share_kernel, n, replicas, cols,...  42.5 us
    pallas_call x2, Pallas kernels, first_gather(): pl.pallas_call(functools.partial(first_kernel, n, normed), out_shape=jax....  38.6 us
    pallas_call x4, Pallas kernels, grads_pair(): pl.pallas_call(functools.partial(grads_kernel, n), out_shape=jax.ShapeDty...  13.4 us
    pallas_call x1, Pallas kernels, small_sums(): pl.pallas_call(functools.partial(small_sums_kernel, n, replicas), out_sha...  12.7 us
  transfers between devices with their start and end apart: 10, of which 0 were waited for; matrix products, arithmetic and copies ran while one was open for 14% of the time, Pallas kernels for 63%

profile of v2, /device:TPU:0, one launch (start us, length us, event | category | flops | bytes accessed | tf_op | source)
XLA Modules:
  0.0 622.7 jit_solution(8126119441297967869)
XLA Ops:
  14.4 10.7 %swap_0.1 = (bf16[4,16,256]{2,1,0:T(8,128)(2,1)S(1)}, bf16[4,32,768]{2,1,0:T(8,128)(2,1)}) custom-call(bf16[4,16,256]{2,1,0:T(8,128)(2,1)S(1)} %broadcast_in_dim.63.refs_0_.refs_2_, bf16[4,32,768]{2,1,0:T(8,128)(2,1)S(1)} %squeeze.81.refs_1_, bf16[4,16,256]{2,1,0:T(8,128)(2,1)S(1)} %broadcast_in_dim.63.refs_0_.refs_2_), custom_call_target="tpu_custom_call" | custom-call | bytes 26400000 | tf_op jit(solution)/shard_map/swap_0/pallas_call | solution.py:541
  26.9 20.1 %first_gather.1.refs_3_.a_ref = bf16[512,1024]{1,0:T(8,128)(2,1)S(1)} custom-call(bf16[128,1024]{1,0:T(8,128)(2,1)S(1)} %bitcast.289, f32[2,1024]{1,0:T(2,128)S(1)} %pad_maximum_fusion.10.vec, bf16[4,32,768]{2,1,0:T(8,128)(2,1)} %get-tuple-element.44.after), custom_call_target="tpu_custom_call" | custom-call | bytes 69300000 | tf_op jit(solution)/shard_map/first_gather/pallas_call | solution.py:497
  47.9 17.6 %swap_2.1 = (bf16[4,32,1024]{2,1,0:T(8,128)(2,1)}, bf16[4,32,1024]{2,1,0:T(8,128)(2,1)}, bf16[4,32,768]{2,1,0:T(8,128)(2,1)}) custom-call(bf16[4,32,1024]{2,1,0:T(8,128)(2,1)S(1)} %get-tuple-element.103.refs_0_, bf16[4,32,1024]{2,1,0:T(8,128)(2,1)S(1)} %get-tuple-element.102.refs_1_, bf16[4,32,768]{2,1,0:T(8,128)(2,1)S(1)} %squeeze.89.refs_2_, ...), custom_call_target="tpu_custom_call" | custom-call | bytes 79200000 | tf_op jit(solution)/shard_map/swap_2/pallas_call | solution.py:541
  69.4 18.5 %cot_gather.1.d_ref = bf16[512,1024]{1,0:T(8,128)(2,1)S(1)} custom-call(bf16[128,1024]{1,0:T(8,128)(2,1)S(1)} %bitcast.287, f32[2,1024]{1,0:T(2,128)S(1)} %pad_maximum_fusion.10.vec, bf16[4,32,1024]{2,1,0:T(8,128)(2,1)} %get-tuple-element.45.after), custom_call_target="tpu_custom_call" | custom-call | bytes 69300000 | tf_op jit(solution)/shard_map/cot_gather/pallas_call | solution.py:497
  91.9 5.0 fusion.54
  103.5 41.8 %forward_gelu_0.1 = (f32[128,1024]{1,0:T(8,128)S(1)}, bf16[512,1024]{1,0:T(8,128)(2,1)S(1)}, bf16[512,1024]{1,0:T(8,128)(2,1)S(1)}, f32[512,1024]{1,0:T(8,128)}) custom-call(bf16[512,256]{1,0:T(8,128)(2,1)S(1)} %copy.181.refs_0_.c_ref, bf16[2,256,1024]{2,1,0:T(8,128)(2,1)S(1)} %copy-done.6, f32[128,1024]{1,0:T(8,128)S(1)} %copy-done.17, ...), custom_call_target="tpu_custom_call" | custom-call | bytes 138600000 | tf_op jit(solution)/shard_map/forward_gelu_0/pallas_call | solution.py:362
  151.7 44.2 %forward_bias_0.1 = (f32[128,1024]{1,0:T(8,128)S(1)}, bf16[512,1024]{1,0:T(8,128)(2,1)S(1)}, bf16[512,768]{1,0:T(8,128)(2,1)S(1)}) custom-call(bf16[512,1024]{1,0:T(8,128)(2,1)S(1)} %copy-done.28, bf16[2,1024,1024]{2,1,0:T(8,128)(2,1)} %refs_5_.4, f32[128,1024]{1,0:T(8,128)S(1)} %copy-done.38, f32[3,1024]{1,0:T(4,128)S(1)} %pad_maximum_fusion.8.refs_3_, ...), custom_call_target="tpu_custom_call" | custom-call | bytes 138600000 | tf_op jit(solution)/shard_map/forward_bias_0/pallas_call | solution.py:362
  198.9 5.3 fusion.55
  212.2 42.5 %forward_gelu_1.1 = (f32[128,1024]{1,0:T(8,128)S(1)}, bf16[512,1024]{1,0:T(8,128)(2,1)S(1)}, bf16[512,1024]{1,0:T(8,128)(2,1)S(1)}, f32[512,1024]{1,0:T(8,128)}) custom-call(bf16[512,256]{1,0:T(8,128)(2,1)S(1)} %copy-done.30, bf16[2,256,1024]{2,1,0:T(8,128)(2,1)S(1)} %copy-done.7, f32[128,1024]{1,0:T(8,128)S(1)} %copy-done.44, ...), custom_call_target="tpu_custom_call" | custom-call | bytes 138600000 | tf_op jit(solution)/shard_map/forward_gelu_1/pallas_call | solution.py:362
  254.8 4.4 fusion.36
  259.3 4.3 weight_grads.4.refs_6_
  269.2 40.5 %backward_plain_1.1 = (f32[128,1024]{1,0:T(8,128)S(1)}, f32[8,1024]{1,0:T(8,128)S(1)}, bf16[512,1024]{1,0:T(8,128)(2,1)S(1)}, bf16[512,256]{1,0:T(8,128)(2,1)S(1)}) custom-call(bf16[512,1024]{1,0:T(8,128)(2,1)S(1)} %copy-done.22, bf16[8,4,32,1024]{3,2,1,0:T(8,128)(2,1)} %bitcast.305, f32[128,1024]{1,0:T(8,128)S(1)} %copy-done.41, f32[1,1024]{1,0:T(1,128)S(1)} %bitcast.299, ...), custom_call_target="tpu_custom_call" | custom-call | bytes 138600000 | tf_op jit(solution)/shard_map/backward_plain_1/pallas_call | solution.py:471
  331.7 7.1 %swap_64.1.refs_8_ = bf16[4,32,1024]{2,1,0:T(8,128)(2,1)S(1)} custom-call(bf16[4,32,1024]{2,1,0:T(8,128)(2,1)S(1)} %bitcast.288, bf16[256,4096]{1,0:T(8,128)(2,1)} %weight_grads.5.refs_1_.refs_7_), custom_call_target="tpu_custom_call" | custom-call | bytes 26400000 | tf_op jit(solution)/shard_map/swap_64/pallas_call | solution.py:541
  341.0 45.4 %backward_gelu_0.1 = (f32[128,1024]{1,0:T(8,128)S(1)}, f32[8,1024]{1,0:T(8,128)S(1)}, bf16[512,1024]{1,0:T(8,128)(2,1)S(1)}, bf16[512,1024]{1,0:T(8,128)(2,1)S(1)}, f32[1,1024]{1,0:T(1,128)S(1)}) custom-call(bf16[512,768]{1,0:T(8,128)(2,1)S(1)} %copy-done.14, bf16[8,4,32,768]{3,2,1,0:T(8,128)(2,1)} %bitcast.283, f32[128,1024]{1,0:T(8,128)S(1)} %copy-done.45, ...), custom_call_target="tpu_custom_call" | custom-call | bytes 138600000 | tf_op jit(solution)/shard_map/backward_gelu_0/pallas_call | solution.py:471
  387.3 4.3 weight_grads.6.refs_6_
  396.6 6.6 %swap_65.1.refs_7_ = bf16[4,32,768]{2,1,0:T(8,128)(2,1)S(1)} custom-call(bf16[4,32,768]{2,1,0:T(8,128)(2,1)S(1)} %bitcast.291, f32[8,1024]{1,0:T(8,128)S(1)} %get-tuple-element.65.refs_1_), custom_call_target="tpu_custom_call" | custom-call | bytes 26400000 | tf_op jit(solution)/shard_map/swap_65/pallas_call | solution.py:541
  407.5 21.6 %forward_None_1.1 = f32[128,1024]{1,0:T(8,128)S(1)} custom-call(bf16[512,1024]{1,0:T(8,128)(2,1)S(1)} %copy-done.26, bf16[2,1024,1024]{2,1,0:T(8,128)(2,1)} %refs_5_.4, f32[128,1024]{1,0:T(8,128)S(1)} %copy-done.42, f32[3,1024]{1,0:T(4,128)S(1)} %stack.84.refs_3_), custom_call_target="tpu_custom_call" | custom-call | bytes 69300000 | tf_op jit(solution)/shard_map/forward_None_1/pallas_call | solution.py:362
  435.9 38.0 %backward_plain_0.1 = (f32[128,1024]{1,0:T(8,128)S(1)}, f32[8,1024]{1,0:T(8,128)S(1)}, bf16[512,1024]{1,0:T(8,128)(2,1)S(1)}, bf16[512,256]{1,0:T(8,128)(2,1)S(1)}) custom-call(bf16[512,1024]{1,0:T(8,128)(2,1)S(1)} %copy-done.20, bf16[8,4,32,1024]{3,2,1,0:T(8,128)(2,1)} %bitcast.303, f32[128,1024]{1,0:T(8,128)S(1)} %copy-done.39, f32[1,1024]{1,0:T(1,128)S(1)} %bitcast.295, ...), custom_call_target="tpu_custom_call" | custom-call | bytes 138600000 | tf_op jit(solution)/shard_map/backward_plain_0/pallas_call | solution.py:471
  498.5 22.2 %backward_None_0.1 = (f32[128,1024]{1,0:T(8,128)S(1)}, f32[8,1024]{1,0:T(8,128)S(1)}) custom-call(bf16[512,768]{1,0:T(8,128)(2,1)S(1)} %pad_maximum_fusion.1.b_ref.refs_0_, bf16[8,4,32,768]{3,2,1,0:T(8,128)(2,1)S(1)} %bitcast.282, f32[128,1024]{1,0:T(8,128)S(1)} %copy-done.18, f32[1,1024]{1,0:T(1,128)S(1)} %bitcast.301, f32[128,1024]{1,0:T(8,128)S(1)} %copy-done.62, ...), custom_call_target="tpu_custom_call" | custom-call | bytes 69300000 | tf_op jit(solution)/shard_map/backward_None_0/pallas_call | solution.py:471
  523.3 7.4 %swap_60.1.after = bf16[4,32,1024]{2,1,0:T(8,128)(2,1)S(1)} custom-call(bf16[4,32,1024]{2,1,0:T(8,128)(2,1)S(1)} %bitcast.290, f32[8,1024]{1,0:T(8,128)S(1)} %get-tuple-element.70.refs_1_), custom_call_target="tpu_custom_call" | custom-call | bytes 26400000 | tf_op jit(solution)/shard_map/swap_60/pallas_call | solution.py:541
  532.8 12.7 %small_sums.1 = f32[24,256]{1,0:T(8,128)S(1)} custom-call(f32[4,16,256]{2,1,0:T(8,128)S(1)} %bitcast.293, f32[8,256]{1,0:T(8,128)S(1)} %reshape.369.ups), custom_call_target="tpu_custom_call" | custom-call | bytes 29700000 | tf_op jit(solution)/shard_map/small_sums/pallas_call | solution.py:852
  552.7 42.5 %reduce_share.1 = bf16[8,32,4096]{2,1,0:T(8,128)(2,1)S(1)} custom-call(bf16[8,32,4096]{2,1,0:T(8,128)(2,1)S(1)} %bitcast.278, bf16[4,32,1024]{2,1,0:T(8,128)(2,1)S(1)} %swap_60.1.after), custom_call_target="tpu_custom_call" | custom-call | bytes 115500000 | tf_op jit(solution)/shard_map/reduce_share/pallas_call | solution.py:762
  605.1 4.2 maximum_convert_fusion
  610.7 3.9 maximum_convert_fusion.1
  (380 shorter events, 135.9 us)
Async XLA Ops:
  7.2 19.7 %copy-start.54 = (bf16[1,128,1024]{2,1,0:T(8,128)(2,1)S(1)}, bf16[1,128,1024]{2,1,0:T(8,128)(2,1)}, u32[]{:S(2)}) copy-start(bf16[1,128,1024]{2,1,0:T(8,128)(2,1)} %param.12) | copy-start | bytes 786436
  7.2 81.6 %all-gather.18.cloned.1.call-start = ((), (), s32[]{:S(2)}) async-start(), calls=%async_computation.9 | async-start | bytes 1769472 | tf_op jit(solution)/shard_map/all_gather | solution.py:938
  25.2 77.2 %all-gather.20.cloned.1.call-start = ((), (), s32[]{:S(2)}) async-start(), calls=%async_computation.10 | async-start | bytes 2359296 | tf_op jit(solution)/shard_map/all_gather | solution.py:938
  25.7 43.5 %copy-start.88 = (bf16[2,1024]{1,0:T(2,128)(2,1)S(1)}, bf16[2,1024]{1,0:T(2,128)(2,1)}, u32[]{:S(2)}) copy-start(bf16[2,1024]{1,0:T(2,128)(2,1)} %param.21) | copy-start | bytes 12292
  26.8 42.6 %copy-start.34 = (bf16[1,128,1024]{2,1,0:T(8,128)(2,1)S(1)}, bf16[1,128,1024]{2,1,0:T(8,128)(2,1)}, u32[]{:S(2)}) copy-start(bf16[1,128,1024]{2,1,0:T(8,128)(2,1)} %param.13) | copy-start | bytes 786436
  65.5 24.9 %copy-start.11 = (bf16[512,1024]{1,0:T(8,128)(2,1)S(1)}, bf16[512,1024]{1,0:T(8,128)(2,1)}, u32[]{:S(2)}) copy-start(bf16[512,1024]{1,0:T(8,128)(2,1)} %copy-done.10) | copy-start | bytes 3145732
  65.5 82.5 %all-gather.22.cloned.1.call-start = ((), (), s32[]{:S(2)}) async-start(), calls=%async_computation.11 | async-start | bytes 1769472 | tf_op jit(solution)/shard_map/all_gather | solution.py:938
  66.3 144.0 %all-gather.24.cloned.1.call-start = ((), (), s32[]{:S(2)}) async-start(), calls=%async_computation.12 | async-start | bytes 2359296 | tf_op jit(solution)/shard_map/all_gather | solution.py:938
  66.9 263.0 %reduce-scatter.4.cloned.1.call-start = ((), (), s32[]{:S(2)}) async-start(), calls=%async_computation.3 | async-start | bytes 4718592 | tf_op jit(solution)/shard_map/reduce_scatter | solution.py:997
  266.6 128.2 %reduce-scatter.6.cloned.1.call-start = ((), (), s32[]{:S(2)}) async-start(), calls=%async_computation.4 | async-start | bytes 2359296 | tf_op jit(solution)/shard_map/reduce_scatter | solution.py:997
  329.7 192.3 %reduce-scatter.8.cloned.1.call-start = ((), (), s32[]{:S(2)}) async-start(), calls=%async_computation.5 | async-start | bytes 4718592 | tf_op jit(solution)/shard_map/reduce_scatter | solution.py:997
  329.8 8.9 %copy-start.14 = (bf16[512,768]{1,0:T(8,128)(2,1)S(1)}, bf16[512,768]{1,0:T(8,128)(2,1)}, u32[]{:S(2)}) copy-start(bf16[512,768]{1,0:T(8,128)(2,1)} %copy-done.13) | copy-start | bytes 2359300
  338.8 47.7 %copy-start.32 = (bf16[4,32,1024]{2,1,0:T(8,128)(2,1)}, bf16[4,32,1024]{2,1,0:T(8,128)(2,1)S(1)}, u32[]{:S(2)}) copy-start(bf16[4,32,1024]{2,1,0:T(8,128)(2,1)S(1)} %swap_64.1.refs_8_) | copy-start | bytes 786436
  341.0 46.3 %copy-start.29 = (bf16[512,1024]{1,0:T(8,128)(2,1)S(1)}, bf16[512,1024]{1,0:T(8,128)(2,1)}, u32[]{:S(2)}) copy-start(bf16[512,1024]{1,0:T(8,128)(2,1)} %copy-done.27) | copy-start | bytes 3145732
  341.0 46.3 %copy-start.56 = (bf16[512,1024]{1,0:T(8,128)(2,1)S(1)}, bf16[512,1024]{1,0:T(8,128)(2,1)}, u32[]{:S(2)}) copy-start(bf16[512,1024]{1,0:T(8,128)(2,1)} %copy-done.55) | copy-start | bytes 3145732
  394.6 10.1 %copy-start.33 = (bf16[4,32,1024]{2,1,0:T(8,128)(2,1)S(1)}, bf16[4,32,1024]{2,1,0:T(8,128)(2,1)}, u32[]{:S(2)}) copy-start(bf16[4,32,1024]{2,1,0:T(8,128)(2,1)} %copy-done.32) | copy-start | bytes 786436
  394.6 10.4 %copy-start.87 = (bf16[32,4096]{1,0:T(8,128)(2,1)S(1)}, bf16[32,4096]{1,0:T(8,128)(2,1)}, u32[]{:S(2)}) copy-start(bf16[32,4096]{1,0:T(8,128)(2,1)} %get-tuple-element.92) | copy-start | bytes 786436
  394.6 11.4 %copy-start.36 = (bf16[1,128,1024]{2,1,0:T(8,128)(2,1)S(1)}, bf16[1,128,1024]{2,1,0:T(8,128)(2,1)}, u32[]{:S(2)}) copy-start(bf16[1,128,1024]{2,1,0:T(8,128)(2,1)} %param.13) | copy-start | bytes 786436
  394.6 11.6 %copy-start.42 = (f32[128,1024]{1,0:T(8,128)S(1)}, f32[128,1024]{1,0:T(8,128)}, u32[]{:S(2)}) copy-start(f32[128,1024]{1,0:T(8,128)} %copy-done.40) | copy-start | bytes 1572868
  394.7 153.8 %all-gather.12.cloned.1.call-start = ((), (), s32[]{:S(2)}) async-start(), calls=%async_computation.6 | async-start | bytes 2359296 | tf_op jit(solution)/shard_map/all_gather | solution.py:1008
  404.4 195.4 %all-gather.16.cloned.1.call-start = ((), (), s32[]{:S(2)}) async-start(), calls=%async_computation.8 | async-start | bytes 4718592 | tf_op jit(solution)/shard_map/all_gather | solution.py:1008
  405.9 197.4 %all-gather.14.cloned.1.call-start = ((), (), s32[]{:S(2)}) async-start(), calls=%async_computation.7 | async-start | bytes 4718592 | tf_op jit(solution)/shard_map/all_gather | solution.py:1008
  482.7 9.6 %copy-start.12 = (bf16[512,1024]{1,0:T(8,128)(2,1)S(1)}, bf16[512,1024]{1,0:T(8,128)(2,1)}, u32[]{:S(2)}) copy-start(bf16[512,1024]{1,0:T(8,128)(2,1)} %copy-done.10) | copy-start | bytes 3145732
  482.7 9.6 %copy-start.51 = (bf16[512,1024]{1,0:T(8,128)(2,1)S(1)}, bf16[512,1024]{1,0:T(8,128)(2,1)}, u32[]{:S(2)}) copy-start(bf16[512,1024]{1,0:T(8,128)(2,1)} %copy-done.50) | copy-start | bytes 3145732
  (75 other events, 181.7 us)
Sparse Core Ops, SparseCore 0:
  25.3 26.6 all-gather.17
  65.7 28.2 all-gather.19
  95.9 25.5 all-gather.21
  123.2 27.8 all-gather.23
  266.7 49.7 reduce-scatter.3
  329.9 40.2 reduce-scatter.5
  394.8 49.3 reduce-scatter.7
  446.1 27.7 all-gather.11
  475.8 36.5 all-gather.15
  531.9 43.6 all-gather.13

commit v3 on v2

--- a/solution.py
+++ b/solution.py
@@ -145,7 +145,7 @@
     lax.fori_loop(0, n - 1, drain, 0)
 
 
-def line_scatter(n, me, part, hold, recv, send, final, send_sems, recv_sems):
+def line_scatter(n, me, part, hold, recv, send, final, send_sems, recv_sems, hook=None):
     def copy(way, step, chunk):
         return pltpu.make_async_remote_copy(
             src_ref=send.at[way, step, chunk],
@@ -187,7 +187,12 @@
 
         return carry
 
-    lax.fori_loop(0, n - 1, advance, 0)
+    if hook is None:
+        lax.fori_loop(0, n - 1, advance, 0)
+    else:
+        for step in range(n - 1):
+            advance(step, 0)
+            hook(step)
     part(me, final)
 
     def collect(step, carry):
@@ -535,6 +540,69 @@
         copy.wait()
 
 
+def weight_swap_kernel(n, jobs, count, *refs):
+    piece = refs[len(jobs) + count + 1].shape[1] if jobs else 0
+    srcs, plain = refs[: len(jobs)], refs[len(jobs) : len(jobs) + count]
+    outs = refs[len(jobs) + count + 1 : 2 * (len(jobs) + count) + 1]
+    send_sems, recv_sems, own_sems = refs[2 * (len(jobs) + count) + 1 :]
+    me = lax.axis_index("group")
+    mine = lax.axis_index("replica")
+    peers = [lax.rem(me + step, n) for step in range(1, n)]
+    barrier = pltpu.get_barrier_semaphore()
+    for peer in peers:
+        pl.semaphore_signal(barrier, inc=1, device_id={"group": peer}, device_id_type=MESH)
+    pl.semaphore_wait(barrier, n - 1)
+    copies = []
+    line = [0]
+
+    def move(block, spot):
+        for step, peer in enumerate(peers):
+            copy = pltpu.make_async_remote_copy(
+                src_ref=block(peer),
+                dst_ref=spot(me),
+                send_sem=send_sems.at[line[0], step],
+                recv_sem=recv_sems.at[line[0], step],
+                device_id={"group": peer},
+                device_id_type=MESH,
+            )
+            copy.start()
+            copies.append(copy)
+        own = pltpu.make_async_copy(block(me), spot(me), own_sems.at[line[0]])
+        own.start()
+        copies.append(own)
+        line[0] += 1
+
+    for k in range(count):
+        move(lambda i: plain[k].at[i], lambda i: outs[len(jobs) + k].at[i])
+    for j, (layer, minor, cols) in enumerate(jobs):
+        here = pl.ds(pl.multiple_of(mine * piece, piece), piece)
+        for m in range(minor):
+            move(
+                lambda i: srcs[j].at[layer, here, pl.ds(pl.multiple_of((m * n + i) * cols, 128), cols)],
+                lambda i: outs[j].at[i, :, pl.ds(m * cols, cols)],
+            )
+    for copy in copies:
+        copy.wait()
+
+
+def weight_swap(weights, jobs, plain, collective_id, after, us):
+    n, replicas = lax.axis_size("group"), lax.axis_size("replica")
+    piece = weights[0].shape[1] // replicas
+    lines = sum(job[1] for job in jobs) + len(plain)
+    return pl.pallas_call(
+        functools.partial(weight_swap_kernel, n, jobs, len(plain)),
+        out_shape=[jax.ShapeDtypeStruct((n, piece, job[1] * job[2]), B16) for job in jobs]
+        + [jax.ShapeDtypeStruct(b.shape, b.dtype) for b in plain],
+        in_specs=[ANY] * len(jobs) + [VMEM] * len(plain) + [ANY],
+        out_specs=[VMEM] * (len(jobs) + len(plain)),
+        scratch_shapes=[pltpu.SemaphoreType.DMA((lines, n - 1)) for _ in range(2)]
+        + [pltpu.SemaphoreType.DMA((lines,))],
+        compiler_params=params(collective_id),
+        cost_estimate=cost(us),
+        name=f"weight_swap_{collective_id}",
+    )(*weights, *plain, after)
+
+
 def swap(blocks, collective_id, after=None, us=8.0):
     n = lax.axis_size("group")
     count = len(blocks)
@@ -551,7 +619,8 @@
     )(*blocks, blocks[0] if after is None else after)
 
 
-def grads_kernel(n, a_ref, b_ref, c_ref, d_ref, o_ref, held, sems):
+def grads_kernel(n, a_ref, b_ref, c_ref, d_ref, *refs):
+    o_ref, held, sems = refs[-3:]
     own = held.shape[0]
     cols, width = b_ref.shape[1], d_ref.shape[1]
     folds = c_ref.shape[1] // own
@@ -573,7 +642,7 @@
         copy.wait()
 
 
-def grads_pair(a, b, c, d):
+def grads_pair(a, b, c, d, after=()):
     n = lax.axis_size("group")
     own = a.shape[1] // n
     folds = c.shape[1] // own
@@ -581,13 +650,13 @@
     return pl.pallas_call(
         functools.partial(grads_kernel, n),
         out_shape=jax.ShapeDtypeStruct((own, total), B16),
-        in_specs=[VMEM] * 4,
-        out_specs=ANY,
+        in_specs=[VMEM] * 4 + [ANY] * len(after),
+        out_specs=pl.BlockSpec(memory_space=pltpu.HBM),
         scratch_shapes=[pltpu.VMEM((own, total), B16), pltpu.SemaphoreType.DMA((n + folds,))],
         compiler_params=pltpu.CompilerParams(vmem_limit_bytes=32 * 1024 * 1024),
         cost_estimate=cost(4.0),
         name="weight_grads",
-    )(a, b, c, d)
+    )(a, b, c, d, *after)
 
 
 def digit(value, place):
@@ -602,40 +671,26 @@
     return value + (1 - 2 * digit(value, place)) * 2**place
 
 
-def reduce_share_kernel(n, replicas, cols, minor, g_ref, after, o_ref, *refs):
-    own_half, first_in, acc, flow_in, landed = refs[:5]
-    sems = refs[5:]
-    pair_send, pair_recv, flow_send, flow_recv, swap_send, swap_recv = sems[:6]
-    out_send, out_recv, side_send, side_recv, load_sems = sems[6:]
+def exchange_steps(n, cols, minor, src, o_ref, held, sems, reduce):
+    replicas = o_ref.shape[0]
     me = lax.axis_index("group")
     mine = lax.axis_index("replica")
     core = digit(mine, 0)
     spot = mine // 2
     halves = replicas // 2
     bits = halves.bit_length() - 1
-    total = g_ref.shape[2]
+    total = o_ref.shape[2]
     flow_cols = total // 2
     orders = (list(range(bits)), list(range(bits))[::-1])
     sibling = flipped(mine, 0)
     peers = [lax.rem(me + step, n) for step in range(1, n)]
-    barrier = pltpu.get_barrier_semaphore()
-    for place in range(bits + 1):
-        pl.semaphore_signal(
-            barrier, inc=1, device_id={"replica": flipped(mine, place)}, device_id_type=MESH
-        )
-    for peer in peers:
-        pl.semaphore_signal(barrier, inc=1, device_id={"group": peer}, device_id_type=MESH)
-    loads = []
-    for q in range(halves):
-        load = pltpu.make_async_copy(g_ref.at[2 * q + core], own_half.at[q], load_sems.at[q])
-        load.start()
-        loads.append(load)
-    pl.semaphore_wait(barrier, bits + n)
-
-    def to_replica(src, dst, send_sem, recv_sem, target):
+    landed = held[0]
+    swap_send, swap_recv, out_send, out_recv, side_send, side_recv = sems[:6]
+
+    def to_replica(src_ref, dst_ref, send_sem, recv_sem, target):
         copy = pltpu.make_async_remote_copy(
-            src_ref=src,
-            dst_ref=dst,
+            src_ref=src_ref,
+            dst_ref=dst_ref,
             send_sem=send_sem,
             recv_sem=recv_sem,
             device_id={"replica": target},
@@ -644,55 +699,68 @@
         copy.start()
         return copy
 
-    sent = []
-    paired = []
-    for q in range(halves):
-        copy = to_replica(
-            g_ref.at[2 * q + 1 - core], first_in.at[q], pair_send.at[q], pair_recv.at[q], sibling
-        )
-        paired.append(copy)
-    sent += paired
-    for q in range(halves):
-        loads[q].wait()
-        paired[q].wait_recv()
-        acc[q] = (own_half[q].astype(F32) + first_in[q].astype(F32)).astype(B16)
-
     def chosen(order, count, index):
         spot_of = spot
         for i in range(count):
             spot_of = with_digit(spot_of, order[i], (index >> i) % 2)
         return spot_of
 
-    slot = 0
-    for stage in range(bits):
-        started = []
-        for flow in (0, 1):
-            lanes = pl.ds(flow * flow_cols, flow_cols)
-            place = orders[flow][stage]
-            free = orders[flow][stage + 1 :]
-            for t in range(2 ** len(free)):
-                keep = chosen(free, len(free), t)
-                copy = to_replica(
-                    acc.at[flipped(keep, place), :, lanes],
-                    flow_in.at[flow, slot + t],
-                    flow_send.at[flow, slot + t],
-                    flow_recv.at[flow, slot + t],
-                    flipped(mine, place + 1),
+    sent = []
+    if reduce:
+        own_half, first_in, acc, flow_in = held[1:]
+        pair_send, pair_recv, flow_send, flow_recv, load_sems = sems[6:]
+        loads = []
+        for q in range(halves):
+            load = pltpu.make_async_copy(src.at[2 * q + core], own_half.at[q], load_sems.at[q])
+            load.start()
+            loads.append(load)
+        paired = []
+        for q in range(halves):
+            paired.append(
+                to_replica(
+                    src.at[2 * q + 1 - core], first_in.at[q], pair_send.at[q], pair_recv.at[q], sibling
                 )
-                started.append((copy, flow, slot + t, keep))
-        for copy, flow, at, keep in started:
-            copy.wait_recv()
-            lanes = slice(flow * flow_cols, (flow + 1) * flow_cols)
-            acc[keep, :, lanes] = (
-                acc[keep, :, lanes].astype(F32) + flow_in[flow, at].astype(F32)
-            ).astype(B16)
-            sent.append(copy)
-        slot += 2 ** (bits - 1 - stage)
+            )
+        sent += paired
+        yield
+        for q in range(halves):
+            loads[q].wait()
+            paired[q].wait_recv()
+            acc[q] = (own_half[q].astype(F32) + first_in[q].astype(F32)).astype(B16)
+        slot = 0
+        for stage in range(bits):
+            started = []
+            for flow in (0, 1):
+                lanes = pl.ds(flow * flow_cols, flow_cols)
+                place = orders[flow][stage]
+                free = orders[flow][stage + 1 :]
+                for t in range(2 ** len(free)):
+                    keep = chosen(free, len(free), t)
+                    copy = to_replica(
+                        acc.at[flipped(keep, place), :, lanes],
+                        flow_in.at[flow, slot + t],
+                        flow_send.at[flow, slot + t],
+                        flow_recv.at[flow, slot + t],
+                        flipped(mine, place + 1),
+                    )
+                    started.append((copy, flow, slot + t, keep))
+            yield
+            for copy, flow, at, keep in started:
+                copy.wait_recv()
+                lanes = slice(flow * flow_cols, (flow + 1) * flow_cols)
+                acc[keep, :, lanes] = (
+                    acc[keep, :, lanes].astype(F32) + flow_in[flow, at].astype(F32)
+                ).astype(B16)
+                sent.append(copy)
+            slot += 2 ** (bits - 1 - stage)
+        whole = acc.at[spot]
+    else:
+        whole = src
 
     swaps = []
     for step, peer in enumerate(peers):
         copy = pltpu.make_async_remote_copy(
-            src_ref=acc.at[spot, :, pl.ds(pl.multiple_of(peer * cols, 128), cols)],
+            src_ref=whole.at[:, pl.ds(pl.multiple_of(peer * cols, 128), cols)],
             dst_ref=landed.at[me],
             send_sem=swap_send.at[step],
             recv_sem=swap_recv.at[step],
@@ -701,16 +769,17 @@
         )
         copy.start()
         swaps.append(copy)
-    landed[me] = acc[spot, :, pl.ds(pl.multiple_of(me * cols, 128), cols)]
-    o_ref[mine, :, n * cols :] = acc[spot, :, n * cols :]
+    landed[me] = whole[:, pl.ds(pl.multiple_of(me * cols, 128), cols)]
+    o_ref[mine, :, n * cols :] = whole[:, n * cols :]
+    yield
     for copy in swaps:
         copy.wait_recv()
     sent += swaps
     inner = cols // minor
-    for src in range(n):
+    for origin in range(n):
         for m in range(minor):
-            lo = (m * n + src) * inner
-            o_ref[mine, :, lo : lo + inner] = landed[src, :, m * inner : (m + 1) * inner]
+            lo = (m * n + origin) * inner
+            o_ref[mine, :, lo : lo + inner] = landed[origin, :, m * inner : (m + 1) * inner]
 
     def place_out(spot_of, flow):
         return o_ref.at[2 * spot_of + core, :, pl.ds(flow * flow_cols, flow_cols)]
@@ -742,51 +811,143 @@
         if stage == 0:
             for flow in (0, 1):
                 to_side(spot, flow, 0)
+        yield
         for copy, flow, t in started:
             order = orders[flow][::-1]
             copy.wait_recv()
             to_side(flipped(chosen(order, stage, t), order[stage]), flow, 2**stage + t)
             sent.append(copy)
         slot += 2**stage
+    yield
     for copy in sides:
         copy.wait_recv()
     for copy in sent + sides:
         copy.wait_send()
 
 
-def reduce_share(grads, cols, minor, collective_id, after):
+def exchange_scratch(n, replicas, piece, total, cols, reduce):
+    halves = replicas // 2
+    dma = lambda *shape: pltpu.SemaphoreType.DMA(shape)
+    held = [pltpu.VMEM((n, piece, cols), B16)]
+    sems = [dma(n - 1), dma(n - 1)] + [dma(2, halves) for _ in range(4)]
+    if reduce:
+        held += [pltpu.VMEM((halves, piece, total), B16) for _ in range(3)]
+        held.append(pltpu.VMEM((2, halves - 1, piece, total // 2), B16))
+        sems += [dma(halves), dma(halves), dma(2, halves), dma(2, halves), dma(halves)]
+    return held + sems
+
+
+def closing_kernel(n, replicas, layer, attn_cols, ffn_cols, *refs):
+    refs = list(refs)
+
+    def take(count):
+        some = refs[:count]
+        del refs[:count]
+        return some
+
+    lhs, raw, xin, gain, res, f_lhs, w_any, f_res, bias, attn_src, ffn_src = take(11)
+    take(1)
+    g_ref, small_ref, y_ref, attn_out, ffn_out = take(5)
+    held, h_sems, w, w_sem = take(4)
+    line_b, line_f = take(6), take(6)
+    attn_held, attn_sems = take(5), take(11)
+    ffn_held, ffn_sems = take(1), take(6)
+    me = lax.axis_index("group")
+    mine = lax.axis_index("replica")
+    rows = res.shape[0]
+    bits = (replicas // 2).bit_length() - 1
+    others = weight_copies(raw, held, h_sems)
+    for other in others:
+        other.start()
+    w_copy = pltpu.make_async_copy(w_any.at[layer], w, w_sem)
+    w_copy.start()
+    barrier = pltpu.get_barrier_semaphore()
+    for place in range(bits + 1):
+        pl.semaphore_signal(
+            barrier, inc=1, device_id={"replica": flipped(mine, place)}, device_id_type=MESH
+        )
+    for step in range(1, n):
+        pl.semaphore_signal(
+            barrier, inc=1, device_id={"group": lax.rem(me + step, n)}, device_id_type=MESH
+        )
+    pl.semaphore_wait(barrier, bits + n)
+
+    attn = exchange_steps(n, attn_cols, 3, attn_src, attn_out, attn_held, attn_sems, True)
+    ffn = exchange_steps(n, ffn_cols, 1, ffn_src, ffn_out, ffn_held, ffn_sems, False)
+    next(attn)
+    for other in others:
+        other.wait()
+
+    def part(block, into):
+        own = lhs[rows_at(block, rows), :]
+        for chunk in range(CH):
+            into[chunk] = dot_nt(own, weight_rows(held, chunk))
+
+    def early(step):
+        if step == 0:
+            next(attn, None)
+            next(ffn, None)
+        else:
+            next(ffn, None)
+        if step == n - 2:
+            next(attn, None)
+
+    line_scatter(n, me, part, *line_b, hook=early)
+    grad = joined(line_b[3])
+    _, normed, inverse = norm_apply(xin[...], gain[...], gain[...])
+    result = res[...] + norm_back(grad, normed, inverse, gain[...])
+    g_ref[...] = result
+    small_ref[0:1, :] = jnp.sum(grad * normed, axis=0, keepdims=True)
+    small_ref[1:2, :] = jnp.sum(grad, axis=0, keepdims=True)
+    small_ref[2:3, :] = jnp.sum(result, axis=0, keepdims=True)
+    next(attn, None)
+    w_copy.wait()
+    cols = w.shape[1] // CH
+
+    def f_part(block, into):
+        own = f_lhs[rows_at(block, rows), :]
+        for chunk in range(CH):
+            into[chunk] = dot(own, w[:, chunk * cols : (chunk + 1) * cols])
+
+    def late(step):
+        next(attn, None)
+        if step:
+            next(ffn, None)
+
+    line_scatter(n, me, f_part, *line_f, hook=late)
+    y_ref[...] = f_res[...] + joined(line_f[3]) + bias[...]
+    for steps in (attn, ffn):
+        for _ in steps:
+            pass
+
+
+def closing_step(lhs, raw, xin, gain, res, f_lhs, w_all, layer, f_res, bias, attn_grads, ffn_mine, attn_cols, ffn_cols, after):
     n, replicas = lax.axis_size("group"), lax.axis_size("replica")
-    own, total = grads.shape
-    piece, halves = own // replicas, replicas // 2
-    dma = lambda *shape: pltpu.SemaphoreType.DMA(shape)
-    full = pl.pallas_call(
-        functools.partial(reduce_share_kernel, n, replicas, cols, minor),
-        out_shape=jax.ShapeDtypeStruct((replicas, piece, total), B16),
-        in_specs=[ANY, ANY],
-        out_specs=VMEM,
-        scratch_shapes=[
-            pltpu.VMEM((halves, piece, total), B16),
-            pltpu.VMEM((halves, piece, total), B16),
-            pltpu.VMEM((halves, piece, total), B16),
-            pltpu.VMEM((2, halves - 1, piece, total // 2), B16),
-            pltpu.VMEM((n, piece, cols), B16),
-            dma(halves),
-            dma(halves),
-            dma(2, halves),
-            dma(2, halves),
-            dma(n - 1),
-            dma(n - 1),
-            dma(2, halves),
-            dma(2, halves),
-            dma(2, halves),
-            dma(2, halves),
-            dma(halves),
-        ],
-        compiler_params=params(collective_id),
-        cost_estimate=cost(35.0),
-        name="reduce_share",
-    )(grads.reshape(replicas, piece, total), after)
-    return full.reshape(own, total)
+    rows, width = res.shape
+    own, attn_total = attn_grads.shape
+    piece, ffn_total = ffn_mine.shape
+    full = lambda total: jax.ShapeDtypeStruct((replicas, piece, total), B16)
+    flat = jax.ShapeDtypeStruct((rows, width), F32)
+    outs = pl.pallas_call(
+        functools.partial(closing_kernel, n, replicas, layer, attn_cols, ffn_cols),
+        out_shape=[flat, jax.ShapeDtypeStruct((8, width), F32), flat, full(attn_total), full(ffn_total)],
+        in_specs=[VMEM, ANY, VMEM, VMEM, VMEM, VMEM, ANY, VMEM, VMEM, ANY, VMEM, ANY],
+        out_specs=[VMEM] * 5,
+        scratch_shapes=weight_scratch(raw)
+        + [pltpu.VMEM(w_all.shape[1:], B16), pltpu.SemaphoreType.DMA]
+        + scatter_scratch(n, rows, width)
+        + scatter_scratch(n, rows, width)
+        + exchange_scratch(n, replicas, piece, attn_total, attn_cols, True)
+        + exchange_scratch(n, replicas, piece, ffn_total, ffn_cols, False),
+        compiler_params=params(70),
+        cost_estimate=cost(50.0),
+        name="closing",
+    )(
+        lhs, raw, xin, gain, res, f_lhs, w_all, f_res, bias,
+        attn_grads.reshape(replicas, piece, attn_total), ffn_mine, after,
+    )
+    g, small, y, attn_full, ffn_full = outs
+    return g, small, y, attn_full.reshape(own, attn_total), ffn_full.reshape(own, ffn_total)
 
 
 def small_sums_kernel(n, replicas, wide, ups, o_ref, landed, both, spread, *sems):
@@ -869,6 +1030,42 @@
     )(wide, ups)
 
 
+def widen_kernel(lead, *refs):
+    full, cols_out, rows_out = refs[0], refs[-2], refs[-1]
+    step = pl.program_id(0)
+
+    @pl.when(step < lead)
+    def _():
+        cols_out[0] = full[...].astype(F32)
+
+    @pl.when(step >= lead)
+    def _():
+        rows_out[0] = full[...].astype(F32)
+
+
+def widen(full, cut, width, layer, layers, before):
+    own, total = full.shape
+    lead, folds = cut // width, (total - cut) // width
+    block = (1, own, width)
+    return pl.pallas_call(
+        functools.partial(widen_kernel, lead),
+        grid=(lead + folds,),
+        out_shape=[
+            jax.ShapeDtypeStruct((layers, own, cut), F32),
+            jax.ShapeDtypeStruct((layers, own * folds, width), F32),
+        ],
+        in_specs=[pl.BlockSpec((own, width), lambda j: (0, j))] + [ANY] * len(before),
+        out_specs=[
+            pl.BlockSpec(block, lambda j: (layer, 0, jnp.minimum(j, lead - 1))),
+            pl.BlockSpec(block, lambda j: (layer, jnp.maximum(j - lead, 0), 0)),
+        ],
+        input_output_aliases={1: 0, 2: 1} if before else {},
+        compiler_params=pltpu.CompilerParams(vmem_limit_bytes=24 * 1024 * 1024),
+        cost_estimate=cost(own * total * 6 / 3.3e6),
+        name=f"widen_{layer}",
+    )(full, *before)
+
+
 def attention(q, k, v, first_head, heads_here):
     tokens = q.shape[0]
     split = lambda m: m.reshape(tokens, heads_here, HEAD_DIM).transpose(1, 0, 2)
@@ -928,12 +1125,6 @@
     heads_here = HEADS // groups
     piece = own // replicas
 
-    qkv_piece = lax.dynamic_slice_in_dim(w_qkv, copy_idx * piece, piece, axis=1)
-    qkv_piece = qkv_piece.reshape(layers, piece, 3, groups, own).transpose(0, 3, 1, 2, 4)
-    qkv_piece = qkv_piece.reshape(layers, groups, piece, 3 * own)
-    up_piece = lax.dynamic_slice_in_dim(w_up, copy_idx * piece, piece, axis=1)
-    up_piece = up_piece.reshape(layers, piece, groups, ff_own).transpose(0, 2, 1, 3)
-
     def share(block):
         full = lax.all_gather(block, "replica", axis=0)
         if piece % 16:
@@ -945,7 +1136,7 @@
         axis=1,
     ).reshape(layers * 8, own)
     small = jnp.broadcast_to(small[None], (groups,) + small.shape)
-    small, wq_first = swap([small, qkv_piece[0]], 0)
+    wq_first, small = weight_swap([w_qkv], [(0, 3, own)], [small], 0, bias_up, 9.0)
     wq = [share(wq_first)] + [None] * (layers - 1)
     wu = [None] * layers
 
@@ -963,8 +1154,8 @@
     x = inputs[0].astype(F32)
     vec0 = jnp.stack([gains[0][0], shifts[0][0]])
     a1_all = first_gather(inputs[0], vec0, 1, True, wq_first)
-    later = [up_piece[l] for l in range(layers)] + [qkv_piece[l] for l in range(1, layers)]
-    later = swap(later, 2, a1_all, 24.0)
+    jobs = [(l, 1, ff_own) for l in range(layers)] + [(l, 3, own) for l in range(1, layers)]
+    later = weight_swap([w_up] * layers + [w_qkv] * (layers - 1), jobs, [], 2, a1_all, 18.0)
     for l in range(layers):
         wu[l] = share(later[l])
         if l:
@@ -987,11 +1178,7 @@
             x, a1_all, proj = forward_step(
                 hidden, w_down, l, h, vec, 11 + 4 * l, "bias", wq[l + 1], qkv_bias[l + 1][None]
             )
-        else:
-            vec = jnp.stack([down_bias[l], down_bias[l], down_bias[l]])
-            (x,) = forward_step(hidden, w_down, l, h, vec, 11 + 4 * l)
         kept.append(saved)
-    outputs = x.astype(B16)[None]
 
     def reduce_pair(grads):
         return lax.psum_scatter(grads, "replica", scatter_dimension=0, tiled=True)
@@ -1006,12 +1193,6 @@
         left = left.reshape(groups, piece, minor, cols // minor).transpose(1, 2, 0, 3)
         mine = jnp.concatenate([left.reshape(piece, cut), mine[:, cut:]], axis=1)
         return lax.all_gather(mine, "replica", axis=0, tiled=True)
-
-    def unpack_pair(full, cols):
-        cut = groups * cols
-        folds = (full.shape[1] - cut) // width
-        rows = [full[:, cut + i * width : cut + (i + 1) * width] for i in range(folds)]
-        return full[:, :cut].astype(F32), jnp.concatenate(rows, axis=0).astype(F32)
 
     g = cotangent[0].astype(F32)
     g_sum = jnp.sum(g, axis=0)
@@ -1037,7 +1218,7 @@
             pre, wu[l], h, gains[1][l][None], g, 30 + 4 * l, "plain", w_out, l, after=(ffn_grads,) + waits
         )
         d_proj, (dq_sum, dv_sum) = attention_back(dc, attn_saved)
-        attn_grads = grads_pair(a1_all, d_proj, context, dh_all)
+        attn_grads = grads_pair(a1_all, d_proj, context, dh_all, (ffn_sum[l],) if l else ())
         if l:
             attn_sum[l] = reduce_pair(attn_grads)
             ffn_left = swap_pair(ffn_sum[l], ff_own, 60 + 4 * l, attn_grads)
@@ -1051,12 +1232,12 @@
             waits = (attn_left,)
             g_sum, up_sum = small0[2], up_sum[0]
         else:
-            g, small0 = backward_step(
-                d_proj, wq[l], x_in, gains[0][l][None], dh, 31 + 4 * l, after=(attn_grads,)
+            last = kept[layers - 1]
+            g, small0, x, attn_full[l], ffn_full[l] = closing_step(
+                d_proj, wq[l], x_in, gains[0][l][None], dh, last[7], w_down, layers - 1, last[4],
+                down_bias[layers - 1][None], attn_grads, ffn_sum[l], 3 * own, ff_own, attn_grads,
             )
-            ffn_left = swap_pair(ffn_sum[l], ff_own, 60 + 4 * l, small0)
-            ffn_full[l] = share_pair(ffn_left, ffn_sum[l], ff_own, 1)
-            attn_full[l] = reduce_share(attn_grads, 3 * own, 3, 70, ffn_left)
+            outputs = x.astype(B16)[None]
         qv = lax.dynamic_update_slice_in_dim(zeros_qv, dq_sum, me * own, axis=0)
         qv = lax.dynamic_update_slice_in_dim(qv, dv_sum, width + me * own, axis=0)
         smalls[l] = (
@@ -1064,7 +1245,10 @@
             ups,
         )
 
-    grads = [unpack_pair(attn_full[l], 3 * own) + unpack_pair(ffn_full[l], ff_own) for l in range(layers)]
+    ffn_out, attn_out = (), ()
+    for l in reversed(range(layers)):
+        ffn_out = tuple(widen(ffn_full[l], groups * ff_own, width, l, layers, ffn_out))
+        attn_out = tuple(widen(attn_full[l], 3 * width, width, l, layers, attn_out))
 
     wide = jnp.stack([s[0] for s in smalls])
     per_owner = lambda lo, n: wide[:, lo * width : (lo + n) * width].reshape(layers, n, groups, own)
@@ -1077,19 +1261,18 @@
     own_cols = total[: layers * 8].reshape(layers, 8, own)
     up_total = total[layers * 8 :].reshape(layers, ff_own)
     qv_total = own_cols[:, 4:6].reshape(layers, 2 * own)
-    stack = lambda i: jnp.stack([grads[l][i] for l in range(layers)])
     return (
         outputs,
         g[None],
         own_cols[:, 0:2],
         own_cols[:, 2:4],
-        stack(0),
+        attn_out[0],
         qv_total,
-        stack(1),
+        attn_out[1],
         own_cols[:, 6],
-        stack(2),
+        ffn_out[0],
         up_total,
-        stack(3),
+        ffn_out[1],
         own_cols[:, 7],
     )
 

time: 631 us -> 618 us (0.979)
  Pallas kernels: 453 us -> 466 us
  other arithmetic: 28.2 us -> 15.7 us
  local copies, waits for them, and re-layouts: 86.4 us -> 78.4 us
    pallas_call x1 -> x7, Pallas kernels: 42.5 us -> 129 us  [the longest x1 85 us: closing_step(): pl.pallas_call(functools.partial(closing_kernel, n, replicas, layer, attn...]
    pallas_call x5 -> x2, Pallas kernels: 49.3 us -> 13.2 us  [swap(): pl.pallas_call(functools.partial(swap_kernel, n, count), out_shape=[jax.S...]
    pallas_call x4 -> x3, Pallas kernels: 150 us -> 128 us  [forward_step(): pl.pallas_call(functools.partial(forward_kernel, n, layer, mode, len(afte...]
    pallas_call x4 -> x3, Pallas kernels: 146 us -> 128 us  [backward_step(): pl.pallas_call(functools.partial(backward_kernel, n, layer, mode, len(aft...]
    another operation x4 -> x0, other arithmetic: 12.6 us -> none  [local(): stack = lambda i: jnp.stack([grads[l][i] for l in range(layers)])]
    unnamed x215 -> x202, local copies, waits for them, and re-layouts: 50.2 us -> 54.9 us
  transfers between devices with their start and end apart: 10 -> 9, of which waited for: 0 -> 0; matrix products, arithmetic and copies ran while one was open for 14% -> 11% of each run, Pallas kernels for 63% -> 65%
where the time goes in v3:
time: 618 us; the launch traced here: 611 us
  Pallas kernels  466 us (75%)
  local copies, waits for them, and re-layouts  78.4 us (13%)
  matrix products  33.2 us (5%)
  between operations  15.8 us (3%)
  other arithmetic  15.7 us (3%)
    pallas_call x3, Pallas kernels, forward_step(): pl.pallas_call(functools.partial(forward_kernel, n, layer, mode, len(afte...  128 us
    pallas_call x3, Pallas kernels, backward_step(): pl.pallas_call(functools.partial(backward_kernel, n, layer, mode, len(aft...  128 us
    pallas_call x1, Pallas kernels, closing_step(): pl.pallas_call(functools.partial(closing_kernel, n, replicas, layer, attn...  85 us
    unnamed x202, local copies, waits for them, and re-layouts  54.9 us
    pallas_call x2, Pallas kernels, first_gather(): pl.pallas_call(functools.partial(first_kernel, n, normed), out_shape=jax....  37.5 us
    pallas_call x2, Pallas kernels, weight_swap(): pl.pallas_call(functools.partial(weight_swap_kernel, n, jobs, len(plain))...  28.5 us
    pallas_call x4, Pallas kernels, widen(): pl.pallas_call(functools.partial(widen_kernel, lead), grid=(lead + folds,...  16 us
    pallas_call x1, Pallas kernels, small_sums(): pl.pallas_call(functools.partial(small_sums_kernel, n, replicas), out_sha...  15.7 us
  transfers between devices with their start and end apart: 9, of which 0 were waited for; matrix products, arithmetic and copies ran while one was open for 11% of the time, Pallas kernels for 65%

profile of v3, /device:TPU:0, one launch (start us, length us, event | category | flops | bytes accessed | tf_op | source)
XLA Modules:
  0.0 611.2 jit_solution(10768717698792387510)
XLA Ops:
  12.6 10.9 %weight_swap_0.1 = (bf16[4,32,768]{2,1,0:T(8,128)(2,1)S(1)}, bf16[4,16,256]{2,1,0:T(8,128)(2,1)S(1)}) custom-call(bf16[2,256,3072]{2,1,0:T(8,128)(2,1)S(1)} %copy-done.4, bf16[4,16,256]{2,1,0:T(8,128)(2,1)S(1)} %broadcast_in_dim.63.refs_1_, bf16[2,1024]{1,0:T(2,128)(2,1)S(1)} %copy-done.66), custom_call_target="tpu_custom_call" | custom-call | bytes 29700000 | tf_op jit(solution)/shard_map/weight_swap_0/pallas_call | solution.py:592
  25.4 19.5 %first_gather.1.refs_3_.a_ref = bf16[512,1024]{1,0:T(8,128)(2,1)S(1)} custom-call(bf16[128,1024]{1,0:T(8,128)(2,1)S(1)} %bitcast.233, f32[2,1024]{1,0:T(2,128)S(1)} %pad_maximum_fusion.9.vec, bf16[4,32,768]{2,1,0:T(8,128)(2,1)S(1)} %copy-done.54), custom_call_target="tpu_custom_call" | custom-call | bytes 69300000 | tf_op jit(solution)/shard_map/first_gather/pallas_call | solution.py:502
  44.9 17.6 %weight_swap_2.1 = (bf16[4,32,1024]{2,1,0:T(8,128)(2,1)S(1)}, bf16[4,32,1024]{2,1,0:T(8,128)(2,1)S(1)}, bf16[4,32,768]{2,1,0:T(8,128)(2,1)S(1)}) custom-call(bf16[2,256,4096]{2,1,0:T(8,128)(2,1)} %refs_1_.4, bf16[2,256,4096]{2,1,0:T(8,128)(2,1)} %refs_1_.4, bf16[2,256,3072]{2,1,0:T(8,128)(2,1)S(1)} %copy-done.5, bf16[512,1024]{1,0:T(8,128)(2,1)S(1)} %first_gather.1.refs_3_.a_ref), custom_call_target="tpu_custom_call" | custom-call | bytes 59400000 | tf_op jit(solution)/shard_map/weight_swap_2/pallas_call | solution.py:592
  67.8 18.0 %cot_gather.1.d_ref = bf16[512,1024]{1,0:T(8,128)(2,1)S(1)} custom-call(bf16[128,1024]{1,0:T(8,128)(2,1)S(1)} %bitcast.230, f32[2,1024]{1,0:T(2,128)S(1)} %pad_maximum_fusion.9.vec, bf16[4,32,1024]{2,1,0:T(8,128)(2,1)S(1)} %copy-done.46), custom_call_target="tpu_custom_call" | custom-call | bytes 69300000 | tf_op jit(solution)/shard_map/cot_gather/pallas_call | solution.py:502
  90.0 5.3 fusion.52
  95.3 2.8 multiply_convert_fusion.3
  100.1 42.4 %forward_gelu_0.1 = (f32[128,1024]{1,0:T(8,128)S(1)}, bf16[512,1024]{1,0:T(8,128)(2,1)S(1)}, bf16[512,1024]{1,0:T(8,128)(2,1)S(1)}, f32[512,1024]{1,0:T(8,128)}) custom-call(bf16[512,256]{1,0:T(8,128)(2,1)S(1)} %copy.128.refs_0_.c_ref, bf16[2,256,1024]{2,1,0:T(8,128)(2,1)S(1)} %copy-done.3, f32[128,1024]{1,0:T(8,128)S(1)} %bitcast_convert_fusion.2.refs_2_, ...), custom_call_target="tpu_custom_call" | custom-call | bytes 138600000 | tf_op jit(solution)/shard_map/forward_gelu_0/pallas_call | solution.py:367
  148.9 43.6 %forward_bias_0.1 = (f32[128,1024]{1,0:T(8,128)S(1)}, bf16[512,1024]{1,0:T(8,128)(2,1)S(1)}, bf16[512,768]{1,0:T(8,128)(2,1)S(1)}) custom-call(bf16[512,1024]{1,0:T(8,128)(2,1)S(1)} %copy-done.20, bf16[2,1024,1024]{2,1,0:T(8,128)(2,1)} %refs_6_.1, f32[128,1024]{1,0:T(8,128)S(1)} %copy-done.35, f32[3,1024]{1,0:T(4,128)S(1)} %pad_maximum_fusion.7.refs_3_, ...), custom_call_target="tpu_custom_call" | custom-call | bytes 138600000 | tf_op jit(solution)/shard_map/forward_bias_0/pallas_call | solution.py:367
  198.2 5.3 fusion.53
  210.0 42.5 %forward_gelu_1.1 = (f32[128,1024]{1,0:T(8,128)S(1)}, bf16[512,1024]{1,0:T(8,128)(2,1)S(1)}, bf16[512,1024]{1,0:T(8,128)(2,1)S(1)}, f32[512,1024]{1,0:T(8,128)}) custom-call(bf16[512,256]{1,0:T(8,128)(2,1)S(1)} %copy.134.refs_0_.c_ref, bf16[2,256,1024]{2,1,0:T(8,128)(2,1)S(1)} %copy-done.3, f32[128,1024]{1,0:T(8,128)S(1)} %copy-done.38, ...), custom_call_target="tpu_custom_call" | custom-call | bytes 138600000 | tf_op jit(solution)/shard_map/forward_gelu_1/pallas_call | solution.py:367
  252.6 4.1 fusion.36
  256.7 4.3 weight_grads.4.refs_6_
  266.4 40.5 %backward_plain_1.1 = (f32[128,1024]{1,0:T(8,128)S(1)}, f32[8,1024]{1,0:T(8,128)S(1)}, bf16[512,1024]{1,0:T(8,128)(2,1)S(1)}, bf16[512,256]{1,0:T(8,128)(2,1)S(1)}) custom-call(bf16[512,1024]{1,0:T(8,128)(2,1)S(1)} %copy-done.16, bf16[8,4,32,1024]{3,2,1,0:T(8,128)(2,1)} %bitcast.249, f32[128,1024]{1,0:T(8,128)S(1)} %copy-done.32, f32[1,1024]{1,0:T(1,128)S(1)} %bitcast.242, ...), custom_call_target="tpu_custom_call" | custom-call | bytes 138600000 | tf_op jit(solution)/shard_map/backward_plain_1/pallas_call | solution.py:476
  331.2 7.1 %swap_64.1.refs_8_ = bf16[4,32,1024]{2,1,0:T(8,128)(2,1)S(1)} custom-call(bf16[4,32,1024]{2,1,0:T(8,128)(2,1)S(1)} %bitcast.232, bf16[256,4096]{1,0:T(8,128)(2,1)} %weight_grads.5.refs_1_.refs_7_), custom_call_target="tpu_custom_call" | custom-call | bytes 26400000 | tf_op jit(solution)/shard_map/swap_64/pallas_call | solution.py:609
  338.3 45.6 %backward_gelu_0.1 = (f32[128,1024]{1,0:T(8,128)S(1)}, f32[8,1024]{1,0:T(8,128)S(1)}, bf16[512,1024]{1,0:T(8,128)(2,1)S(1)}, bf16[512,1024]{1,0:T(8,128)(2,1)S(1)}, f32[1,1024]{1,0:T(1,128)S(1)}) custom-call(bf16[512,768]{1,0:T(8,128)(2,1)S(1)} %pad_maximum_fusion.b_ref.refs_0_, bf16[8,4,32,768]{3,2,1,0:T(8,128)(2,1)} %bitcast.226, ...), custom_call_target="tpu_custom_call" | custom-call | bytes 138600000 | tf_op jit(solution)/shard_map/backward_gelu_0/pallas_call | solution.py:476
  384.7 4.3 weight_grads.6.refs_6_
  393.1 6.1 swap_65.1.refs_7_
  411.9 42.4 %backward_plain_0.1 = (f32[128,1024]{1,0:T(8,128)S(1)}, f32[8,1024]{1,0:T(8,128)S(1)}, bf16[512,1024]{1,0:T(8,128)(2,1)S(1)}, bf16[512,256]{1,0:T(8,128)(2,1)S(1)}) custom-call(bf16[512,1024]{1,0:T(8,128)(2,1)S(1)} %copy-done.14, bf16[8,4,32,1024]{3,2,1,0:T(8,128)(2,1)} %bitcast.247, f32[128,1024]{1,0:T(8,128)S(1)} %copy-done.36, f32[1,1024]{1,0:T(1,128)S(1)} %bitcast.238, ...), custom_call_target="tpu_custom_call" | custom-call | bytes 138600000 | tf_op jit(solution)/shard_map/backward_plain_0/pallas_call | solution.py:476
  478.1 85.0 %closing.1 = (f32[128,1024]{1,0:T(8,128)S(1)}, f32[8,1024]{1,0:T(8,128)S(1)}, f32[128,1024]{1,0:T(8,128)S(1)}, bf16[8,32,4096]{2,1,0:T(8,128)(2,1)}, bf16[8,32,8192]{2,1,0:T(8,128)(2,1)}) custom-call(bf16[512,768]{1,0:T(8,128)(2,1)S(1)} %pad_maximum_fusion.1.b_ref.refs_0_, bf16[8,4,32,768]{3,2,1,0:T(8,128)(2,1)} %bitcast.251, ...), custom_call_target="tpu_custom_call" | custom-call | bytes 165000000 | tf_op jit(solution)/shard_map/closing/pallas_call | solution.py:931
  564.2 15.7 %small_sums.1 = f32[24,256]{1,0:T(8,128)S(1)} custom-call(f32[4,16,256]{2,1,0:T(8,128)S(1)} %bitcast.236, f32[8,256]{1,0:T(8,128)S(1)} %reshape.239.ups), custom_call_target="tpu_custom_call" | custom-call | bytes 29700000 | tf_op jit(solution)/shard_map/small_sums/pallas_call | solution.py:1013
  585.3 2.9 widen_1.2
  588.2 2.9 widen_0.2
  593.2 5.1 widen_1.3
  598.3 5.1 widen_0.3
  (339 shorter events, 116.6 us)
Async XLA Ops:
  7.2 79.6 %all-gather.15.cloned.1.call-start = ((), (), s32[]{:S(2)}) async-start(), calls=%async_computation.8 | async-start | bytes 1769472 | tf_op jit(solution)/shard_map/all_gather | solution.py:1129
  12.6 11.8 %copy-start.44 = (bf16[1,128,1024]{2,1,0:T(8,128)(2,1)S(1)}, bf16[1,128,1024]{2,1,0:T(8,128)(2,1)}, u32[]{:S(2)}) copy-start(bf16[1,128,1024]{2,1,0:T(8,128)(2,1)} %param.12) | copy-start | bytes 786436
  12.6 32.3 %copy-start.5 = (bf16[2,256,3072]{2,1,0:T(8,128)(2,1)S(1)}, bf16[2,256,3072]{2,1,0:T(8,128)(2,1)}, u32[]{:S(2)}) copy-start(bf16[2,256,3072]{2,1,0:T(8,128)(2,1)} %refs_2_.3) | copy-start | bytes 9437188
  24.2 75.4 %all-gather.17.cloned.1.call-start = ((), (), s32[]{:S(2)}) async-start(), calls=%async_computation.9 | async-start | bytes 2359296 | tf_op jit(solution)/shard_map/all_gather | solution.py:1129
  44.9 17.6 %copy-start.6 = (bf16[512,1024]{1,0:T(8,128)(2,1)}, bf16[512,1024]{1,0:T(8,128)(2,1)S(1)}, u32[]{:S(2)}) copy-start(bf16[512,1024]{1,0:T(8,128)(2,1)S(1)} %first_gather.1.refs_3_.a_ref) | copy-start | bytes 3145732
  44.9 22.4 %copy-start.67 = (bf16[2,1024]{1,0:T(2,128)(2,1)S(1)}, bf16[2,1024]{1,0:T(2,128)(2,1)}, u32[]{:S(2)}) copy-start(bf16[2,1024]{1,0:T(2,128)(2,1)} %refs_2_.2) | copy-start | bytes 12292
  64.6 80.7 %all-gather.19.cloned.1.call-start = ((), (), s32[]{:S(2)}) async-start(), calls=%async_computation.10 | async-start | bytes 1769472 | tf_op jit(solution)/shard_map/all_gather | solution.py:1129
  65.3 143.6 %all-gather.21.cloned.1.call-start = ((), (), s32[]{:S(2)}) async-start(), calls=%async_computation.11 | async-start | bytes 2359296 | tf_op jit(solution)/shard_map/all_gather | solution.py:1129
  65.9 256.7 %reduce-scatter.4.cloned.1.call-start = ((), (), s32[]{:S(2)}) async-start(), calls=%async_computation.3 | async-start | bytes 4718592 | tf_op jit(solution)/shard_map/reduce_scatter | solution.py:1184
  67.3 22.7 %copy-start.82 = (pred[512,512]{0,1:T(8,128)(4,1)}, pred[512,512]{0,1:T(8,128)(4,1)S(1)}, u32[]{:S(2)}) copy-start(pred[512,512]{0,1:T(8,128)(4,1)S(1)} %broadcast_compare_fusion) | copy-start | bytes 786436
  99.4 43.1 %copy-start.74 = (bf16[4,512,64]{1,2,0:T(8,128)(2,1)}, bf16[4,512,64]{1,2,0:T(8,128)(2,1)S(1)}, u32[]{:S(2)}) copy-start(bf16[4,512,64]{1,2,0:T(8,128)(2,1)S(1)} %convolution_convert_fusion.1) | copy-start | bytes 786436
  99.6 93.0 %copy-start.22 = (bf16[512,256]{1,0:T(8,128)(2,1)}, bf16[512,256]{1,0:T(8,128)(2,1)S(1)}, u32[]{:S(2)}) copy-start(bf16[512,256]{1,0:T(8,128)(2,1)S(1)} %copy.128.refs_0_.c_ref) | copy-start | bytes 786436
  208.9 47.8 %copy-start.24 = (bf16[512,256]{1,0:T(8,128)(2,1)}, bf16[512,256]{1,0:T(8,128)(2,1)S(1)}, u32[]{:S(2)}) copy-start(bf16[512,256]{1,0:T(8,128)(2,1)S(1)} %copy.134.refs_0_.c_ref) | copy-start | bytes 786436
  208.9 43.7 %copy-start.18 = (bf16[512,1024]{1,0:T(8,128)(2,1)S(1)}, bf16[512,1024]{1,0:T(8,128)(2,1)}, u32[]{:S(2)}) copy-start(bf16[512,1024]{1,0:T(8,128)(2,1)} %copy-done.17) | copy-start | bytes 3145732
  264.0 128.1 %reduce-scatter.6.cloned.1.call-start = ((), (), s32[]{:S(2)}) async-start(), calls=%async_computation.4 | async-start | bytes 2359296 | tf_op jit(solution)/shard_map/reduce_scatter | solution.py:1184
  329.2 145.5 %reduce-scatter.8.cloned.1.call-start = ((), (), s32[]{:S(2)}) async-start(), calls=%async_computation.5 | async-start | bytes 4718592 | tf_op jit(solution)/shard_map/reduce_scatter | solution.py:1184
  338.3 45.7 %copy-start.26 = (bf16[4,32,1024]{2,1,0:T(8,128)(2,1)}, bf16[4,32,1024]{2,1,0:T(8,128)(2,1)S(1)}, u32[]{:S(2)}) copy-start(bf16[4,32,1024]{2,1,0:T(8,128)(2,1)S(1)} %swap_64.1.refs_8_) | copy-start | bytes 786436
  338.3 46.4 %copy-start.21 = (bf16[512,1024]{1,0:T(8,128)(2,1)S(1)}, bf16[512,1024]{1,0:T(8,128)(2,1)}, u32[]{:S(2)}) copy-start(bf16[512,1024]{1,0:T(8,128)(2,1)} %copy-done.19) | copy-start | bytes 3145732
  338.3 46.4 %copy-start.52 = (bf16[512,1024]{1,0:T(8,128)(2,1)S(1)}, bf16[512,1024]{1,0:T(8,128)(2,1)}, u32[]{:S(2)}) copy-start(bf16[512,1024]{1,0:T(8,128)(2,1)} %copy-done.51) | copy-start | bytes 3145732
  392.0 13.6 %copy-start.27 = (bf16[4,32,1024]{2,1,0:T(8,128)(2,1)S(1)}, bf16[4,32,1024]{2,1,0:T(8,128)(2,1)}, u32[]{:S(2)}) copy-start(bf16[4,32,1024]{2,1,0:T(8,128)(2,1)} %copy-done.26) | copy-start | bytes 786436
  392.0 191.7 %all-gather.11.cloned.1.call-start = ((), (), s32[]{:S(2)}) async-start(), calls=%async_computation.6 | async-start | bytes 2359296 | tf_op jit(solution)/shard_map/all_gather | solution.py:1195
  405.3 185.7 %all-gather.13.cloned.1.call-start = ((), (), s32[]{:S(2)}) async-start(), calls=%async_computation.7 | async-start | bytes 4718592 | tf_op jit(solution)/shard_map/all_gather | solution.py:1195
  411.9 45.4 %copy-start.73 = (bf16[512,256]{0,1:T(8,128)(2,1)S(1)}, bf16[512,256]{0,1:T(8,128)(2,1)}, u32[]{:S(2)}) copy-start(bf16[512,256]{0,1:T(8,128)(2,1)} %copy-done.72) | copy-start | bytes 786436
  563.9 24.2 %copy-start.30 = (bf16[8,32,4096]{2,1,0:T(8,128)(2,1)S(1)}, bf16[8,32,4096]{2,1,0:T(8,128)(2,1)}, u32[]{:S(2)}) copy-start(bf16[8,32,4096]{2,1,0:T(8,128)(2,1)} %get-tuple-element.86) | copy-start | bytes 6291460
  (69 other events, 164.0 us)
Sparse Core Ops, SparseCore 0:
  24.4 25.8 all-gather.14
  64.7 26.9 all-gather.16
  93.6 25.5 all-gather.18
  121.0 27.8 all-gather.20
  264.1 49.8 reduce-scatter.3
  329.4 40.2 reduce-scatter.5
  392.1 50.5 reduce-scatter.7
  444.6 27.7 all-gather.10
  474.3 47.6 all-gather.12

commit v4 on v3

--- a/solution.py
+++ b/solution.py
@@ -17,7 +17,7 @@
 F32 = jnp.float32
 B16 = jnp.bfloat16
 MESH = pl.DeviceIdType.MESH
-CH = 2
+CH = 4
 
 VMEM = pl.BlockSpec(memory_space=pltpu.VMEM)
 ANY = pl.BlockSpec(memory_space=pl.ANY)

time: 618 us -> 615 us (level)
  no operation moved by 1% of the time
where the time goes in v4:
time: 615 us; the launch traced here: 606 us
  Pallas kernels  461 us (75%)
  local copies, waits for them, and re-layouts  78.3 us (13%)
  matrix products  33.1 us (5%)
  between operations  15.8 us (3%)
  other arithmetic  15.7 us (3%)
    pallas_call x3, Pallas kernels, forward_step(): pl.pallas_call(functools.partial(forward_kernel, n, layer, mode, len(afte...  126 us
    pallas_call x3, Pallas kernels, backward_step(): pl.pallas_call(functools.partial(backward_kernel, n, layer, mode, len(aft...  126 us
    pallas_call x1, Pallas kernels, closing_step(): pl.pallas_call(functools.partial(closing_kernel, n, replicas, layer, attn...  83.1 us
    unnamed x202, local copies, waits for them, and re-layouts  54.9 us
    pallas_call x2, Pallas kernels, first_gather(): pl.pallas_call(functools.partial(first_kernel, n, normed), out_shape=jax....  38.3 us
    pallas_call x2, Pallas kernels, weight_swap(): pl.pallas_call(functools.partial(weight_swap_kernel, n, jobs, len(plain))...  28.8 us
    pallas_call x4, Pallas kernels, widen(): pl.pallas_call(functools.partial(widen_kernel, lead), grid=(lead + folds,...  16 us
    pallas_call x1, Pallas kernels, small_sums(): pl.pallas_call(functools.partial(small_sums_kernel, n, replicas), out_sha...  15.9 us
  transfers between devices with their start and end apart: 9, of which 0 were waited for; matrix products, arithmetic and copies ran while one was open for 11% of the time, Pallas kernels for 65%

profile of v4, /device:TPU:0, one launch (start us, length us, event | category | flops | bytes accessed | tf_op | source)
XLA Modules:
  0.0 606.3 jit_solution(15874159858712238397)
XLA Ops:
  12.6 10.9 %weight_swap_0.1 = (bf16[4,32,768]{2,1,0:T(8,128)(2,1)S(1)}, bf16[4,16,256]{2,1,0:T(8,128)(2,1)S(1)}) custom-call(bf16[2,256,3072]{2,1,0:T(8,128)(2,1)S(1)} %copy-done.4, bf16[4,16,256]{2,1,0:T(8,128)(2,1)S(1)} %broadcast_in_dim.63.refs_1_, bf16[2,1024]{1,0:T(2,128)(2,1)S(1)} %copy-done.66), custom_call_target="tpu_custom_call" | custom-call | bytes 29700000 | tf_op jit(solution)/shard_map/weight_swap_0/pallas_call | solution.py:592
  25.4 19.7 %first_gather.1.refs_3_.a_ref = bf16[512,1024]{1,0:T(8,128)(2,1)S(1)} custom-call(bf16[128,1024]{1,0:T(8,128)(2,1)S(1)} %bitcast.233, f32[2,1024]{1,0:T(2,128)S(1)} %pad_maximum_fusion.9.vec, bf16[4,32,768]{2,1,0:T(8,128)(2,1)S(1)} %copy-done.54), custom_call_target="tpu_custom_call" | custom-call | bytes 69300000 | tf_op jit(solution)/shard_map/first_gather/pallas_call | solution.py:502
  45.1 17.9 %weight_swap_2.1 = (bf16[4,32,1024]{2,1,0:T(8,128)(2,1)S(1)}, bf16[4,32,1024]{2,1,0:T(8,128)(2,1)S(1)}, bf16[4,32,768]{2,1,0:T(8,128)(2,1)S(1)}) custom-call(bf16[2,256,4096]{2,1,0:T(8,128)(2,1)} %refs_1_.4, bf16[2,256,4096]{2,1,0:T(8,128)(2,1)} %refs_1_.4, bf16[2,256,3072]{2,1,0:T(8,128)(2,1)S(1)} %copy-done.5, bf16[512,1024]{1,0:T(8,128)(2,1)S(1)} %first_gather.1.refs_3_.a_ref), custom_call_target="tpu_custom_call" | custom-call | bytes 59400000 | tf_op jit(solution)/shard_map/weight_swap_2/pallas_call | solution.py:592
  68.3 18.6 %cot_gather.1.d_ref = bf16[512,1024]{1,0:T(8,128)(2,1)S(1)} custom-call(bf16[128,1024]{1,0:T(8,128)(2,1)S(1)} %bitcast.230, f32[2,1024]{1,0:T(2,128)S(1)} %pad_maximum_fusion.9.vec, bf16[4,32,1024]{2,1,0:T(8,128)(2,1)S(1)} %copy-done.46), custom_call_target="tpu_custom_call" | custom-call | bytes 69300000 | tf_op jit(solution)/shard_map/cot_gather/pallas_call | solution.py:502
  91.1 5.3 fusion.52
  96.4 2.8 multiply_convert_fusion.3
  101.2 42.0 %forward_gelu_0.1 = (f32[128,1024]{1,0:T(8,128)S(1)}, bf16[512,1024]{1,0:T(8,128)(2,1)S(1)}, bf16[512,1024]{1,0:T(8,128)(2,1)S(1)}, f32[512,1024]{1,0:T(8,128)}) custom-call(bf16[512,256]{1,0:T(8,128)(2,1)S(1)} %copy.128.refs_0_.c_ref, bf16[2,256,1024]{2,1,0:T(8,128)(2,1)S(1)} %copy-done.3, f32[128,1024]{1,0:T(8,128)S(1)} %bitcast_convert_fusion.2.refs_2_, ...), custom_call_target="tpu_custom_call" | custom-call | bytes 138600000 | tf_op jit(solution)/shard_map/forward_gelu_0/pallas_call | solution.py:367
  149.7 42.3 %forward_bias_0.1 = (f32[128,1024]{1,0:T(8,128)S(1)}, bf16[512,1024]{1,0:T(8,128)(2,1)S(1)}, bf16[512,768]{1,0:T(8,128)(2,1)S(1)}) custom-call(bf16[512,1024]{1,0:T(8,128)(2,1)S(1)} %copy-done.20, bf16[2,1024,1024]{2,1,0:T(8,128)(2,1)} %refs_6_.1, f32[128,1024]{1,0:T(8,128)S(1)} %copy-done.35, f32[3,1024]{1,0:T(4,128)S(1)} %pad_maximum_fusion.7.refs_3_, ...), custom_call_target="tpu_custom_call" | custom-call | bytes 138600000 | tf_op jit(solution)/shard_map/forward_bias_0/pallas_call | solution.py:367
  197.7 5.3 fusion.53
  209.5 42.1 %forward_gelu_1.1 = (f32[128,1024]{1,0:T(8,128)S(1)}, bf16[512,1024]{1,0:T(8,128)(2,1)S(1)}, bf16[512,1024]{1,0:T(8,128)(2,1)S(1)}, f32[512,1024]{1,0:T(8,128)}) custom-call(bf16[512,256]{1,0:T(8,128)(2,1)S(1)} %copy.134.refs_0_.c_ref, bf16[2,256,1024]{2,1,0:T(8,128)(2,1)S(1)} %copy-done.3, f32[128,1024]{1,0:T(8,128)S(1)} %copy-done.38, ...), custom_call_target="tpu_custom_call" | custom-call | bytes 138600000 | tf_op jit(solution)/shard_map/forward_gelu_1/pallas_call | solution.py:367
  251.7 4.1 fusion.36
  255.8 4.3 weight_grads.4.refs_6_
  265.4 40.1 %backward_plain_1.1 = (f32[128,1024]{1,0:T(8,128)S(1)}, f32[8,1024]{1,0:T(8,128)S(1)}, bf16[512,1024]{1,0:T(8,128)(2,1)S(1)}, bf16[512,256]{1,0:T(8,128)(2,1)S(1)}) custom-call(bf16[512,1024]{1,0:T(8,128)(2,1)S(1)} %copy-done.16, bf16[8,4,32,1024]{3,2,1,0:T(8,128)(2,1)} %bitcast.249, f32[128,1024]{1,0:T(8,128)S(1)} %copy-done.32, f32[1,1024]{1,0:T(1,128)S(1)} %bitcast.242, ...), custom_call_target="tpu_custom_call" | custom-call | bytes 138600000 | tf_op jit(solution)/shard_map/backward_plain_1/pallas_call | solution.py:476
  329.9 7.0 %swap_64.1.refs_8_ = bf16[4,32,1024]{2,1,0:T(8,128)(2,1)S(1)} custom-call(bf16[4,32,1024]{2,1,0:T(8,128)(2,1)S(1)} %bitcast.232, bf16[256,4096]{1,0:T(8,128)(2,1)} %weight_grads.5.refs_1_.refs_7_), custom_call_target="tpu_custom_call" | custom-call | bytes 26400000 | tf_op jit(solution)/shard_map/swap_64/pallas_call | solution.py:609
  337.0 46.7 %backward_gelu_0.1 = (f32[128,1024]{1,0:T(8,128)S(1)}, f32[8,1024]{1,0:T(8,128)S(1)}, bf16[512,1024]{1,0:T(8,128)(2,1)S(1)}, bf16[512,1024]{1,0:T(8,128)(2,1)S(1)}, f32[1,1024]{1,0:T(1,128)S(1)}) custom-call(bf16[512,768]{1,0:T(8,128)(2,1)S(1)} %pad_maximum_fusion.b_ref.refs_0_, bf16[8,4,32,768]{3,2,1,0:T(8,128)(2,1)} %bitcast.226, ...), custom_call_target="tpu_custom_call" | custom-call | bytes 138600000 | tf_op jit(solution)/shard_map/backward_gelu_0/pallas_call | solution.py:476
  384.5 4.3 weight_grads.6.refs_6_
  393.1 6.1 %swap_65.1.refs_7_ = bf16[4,32,768]{2,1,0:T(8,128)(2,1)S(1)} custom-call(bf16[4,32,768]{2,1,0:T(8,128)(2,1)S(1)} %bitcast.234, f32[8,1024]{1,0:T(8,128)S(1)} %get-tuple-element.76.refs_1_), custom_call_target="tpu_custom_call" | custom-call | bytes 26400000 | tf_op jit(solution)/shard_map/swap_65/pallas_call | solution.py:609
  411.6 39.6 %backward_plain_0.1 = (f32[128,1024]{1,0:T(8,128)S(1)}, f32[8,1024]{1,0:T(8,128)S(1)}, bf16[512,1024]{1,0:T(8,128)(2,1)S(1)}, bf16[512,256]{1,0:T(8,128)(2,1)S(1)}) custom-call(bf16[512,1024]{1,0:T(8,128)(2,1)S(1)} %copy-done.14, bf16[8,4,32,1024]{3,2,1,0:T(8,128)(2,1)} %bitcast.247, f32[128,1024]{1,0:T(8,128)S(1)} %copy-done.36, f32[1,1024]{1,0:T(1,128)S(1)} %bitcast.238, ...), custom_call_target="tpu_custom_call" | custom-call | bytes 138600000 | tf_op jit(solution)/shard_map/backward_plain_0/pallas_call | solution.py:476
  474.9 83.1 %closing.1 = (f32[128,1024]{1,0:T(8,128)S(1)}, f32[8,1024]{1,0:T(8,128)S(1)}, f32[128,1024]{1,0:T(8,128)S(1)}, bf16[8,32,4096]{2,1,0:T(8,128)(2,1)}, bf16[8,32,8192]{2,1,0:T(8,128)(2,1)}) custom-call(bf16[512,768]{1,0:T(8,128)(2,1)S(1)} %pad_maximum_fusion.1.b_ref.refs_0_, bf16[8,4,32,768]{3,2,1,0:T(8,128)(2,1)} %bitcast.251, ...), custom_call_target="tpu_custom_call" | custom-call | bytes 165000000 | tf_op jit(solution)/shard_map/closing/pallas_call | solution.py:931
  559.1 15.9 %small_sums.1 = f32[24,256]{1,0:T(8,128)S(1)} custom-call(f32[4,16,256]{2,1,0:T(8,128)S(1)} %bitcast.236, f32[8,256]{1,0:T(8,128)S(1)} %reshape.239.ups), custom_call_target="tpu_custom_call" | custom-call | bytes 29700000 | tf_op jit(solution)/shard_map/small_sums/pallas_call | solution.py:1013
  580.4 2.9 widen_1.2
  583.3 2.9 widen_0.2
  588.4 5.1 widen_1.3
  593.5 5.1 widen_0.3
  (339 shorter events, 116.4 us)
Async XLA Ops:
  7.2 80.7 %all-gather.15.cloned.1.call-start = ((), (), s32[]{:S(2)}) async-start(), calls=%async_computation.8 | async-start | bytes 1769472 | tf_op jit(solution)/shard_map/all_gather | solution.py:1129
  12.6 11.8 %copy-start.44 = (bf16[1,128,1024]{2,1,0:T(8,128)(2,1)S(1)}, bf16[1,128,1024]{2,1,0:T(8,128)(2,1)}, u32[]{:S(2)}) copy-start(bf16[1,128,1024]{2,1,0:T(8,128)(2,1)} %param.12) | copy-start | bytes 786436
  12.6 32.5 %copy-start.5 = (bf16[2,256,3072]{2,1,0:T(8,128)(2,1)S(1)}, bf16[2,256,3072]{2,1,0:T(8,128)(2,1)}, u32[]{:S(2)}) copy-start(bf16[2,256,3072]{2,1,0:T(8,128)(2,1)} %refs_2_.3) | copy-start | bytes 9437188
  24.2 76.5 %all-gather.17.cloned.1.call-start = ((), (), s32[]{:S(2)}) async-start(), calls=%async_computation.9 | async-start | bytes 2359296 | tf_op jit(solution)/shard_map/all_gather | solution.py:1129
  45.1 17.9 %copy-start.6 = (bf16[512,1024]{1,0:T(8,128)(2,1)}, bf16[512,1024]{1,0:T(8,128)(2,1)S(1)}, u32[]{:S(2)}) copy-start(bf16[512,1024]{1,0:T(8,128)(2,1)S(1)} %first_gather.1.refs_3_.a_ref) | copy-start | bytes 3145732
  45.1 22.8 %copy-start.67 = (bf16[2,1024]{1,0:T(2,128)(2,1)S(1)}, bf16[2,1024]{1,0:T(2,128)(2,1)}, u32[]{:S(2)}) copy-start(bf16[2,1024]{1,0:T(2,128)(2,1)} %refs_2_.2) | copy-start | bytes 12292
  65.1 80.9 %all-gather.19.cloned.1.call-start = ((), (), s32[]{:S(2)}) async-start(), calls=%async_computation.10 | async-start | bytes 1769472 | tf_op jit(solution)/shard_map/all_gather | solution.py:1129
  65.9 142.5 %all-gather.21.cloned.1.call-start = ((), (), s32[]{:S(2)}) async-start(), calls=%async_computation.11 | async-start | bytes 2359296 | tf_op jit(solution)/shard_map/all_gather | solution.py:1129
  66.4 254.9 %reduce-scatter.4.cloned.1.call-start = ((), (), s32[]{:S(2)}) async-start(), calls=%async_computation.3 | async-start | bytes 4718592 | tf_op jit(solution)/shard_map/reduce_scatter | solution.py:1184
  67.8 23.2 %copy-start.82 = (pred[512,512]{0,1:T(8,128)(4,1)}, pred[512,512]{0,1:T(8,128)(4,1)S(1)}, u32[]{:S(2)}) copy-start(pred[512,512]{0,1:T(8,128)(4,1)S(1)} %broadcast_compare_fusion) | copy-start | bytes 786436
  100.5 42.7 %copy-start.74 = (bf16[4,512,64]{1,2,0:T(8,128)(2,1)}, bf16[4,512,64]{1,2,0:T(8,128)(2,1)S(1)}, u32[]{:S(2)}) copy-start(bf16[4,512,64]{1,2,0:T(8,128)(2,1)S(1)} %convolution_convert_fusion.1) | copy-start | bytes 786436
  100.7 91.3 %copy-start.22 = (bf16[512,256]{1,0:T(8,128)(2,1)}, bf16[512,256]{1,0:T(8,128)(2,1)S(1)}, u32[]{:S(2)}) copy-start(bf16[512,256]{1,0:T(8,128)(2,1)S(1)} %copy.128.refs_0_.c_ref) | copy-start | bytes 786436
  208.3 47.4 %copy-start.24 = (bf16[512,256]{1,0:T(8,128)(2,1)}, bf16[512,256]{1,0:T(8,128)(2,1)S(1)}, u32[]{:S(2)}) copy-start(bf16[512,256]{1,0:T(8,128)(2,1)S(1)} %copy.134.refs_0_.c_ref) | copy-start | bytes 786436
  208.3 43.3 %copy-start.18 = (bf16[512,1024]{1,0:T(8,128)(2,1)S(1)}, bf16[512,1024]{1,0:T(8,128)(2,1)}, u32[]{:S(2)}) copy-start(bf16[512,1024]{1,0:T(8,128)(2,1)} %copy-done.17) | copy-start | bytes 3145732
  263.0 129.1 %reduce-scatter.6.cloned.1.call-start = ((), (), s32[]{:S(2)}) async-start(), calls=%async_computation.4 | async-start | bytes 2359296 | tf_op jit(solution)/shard_map/reduce_scatter | solution.py:1184
  328.0 143.6 %reduce-scatter.8.cloned.1.call-start = ((), (), s32[]{:S(2)}) async-start(), calls=%async_computation.5 | async-start | bytes 4718592 | tf_op jit(solution)/shard_map/reduce_scatter | solution.py:1184
  337.0 46.7 %copy-start.26 = (bf16[4,32,1024]{2,1,0:T(8,128)(2,1)}, bf16[4,32,1024]{2,1,0:T(8,128)(2,1)S(1)}, u32[]{:S(2)}) copy-start(bf16[4,32,1024]{2,1,0:T(8,128)(2,1)S(1)} %swap_64.1.refs_8_) | copy-start | bytes 786436
  337.0 47.5 %copy-start.21 = (bf16[512,1024]{1,0:T(8,128)(2,1)S(1)}, bf16[512,1024]{1,0:T(8,128)(2,1)}, u32[]{:S(2)}) copy-start(bf16[512,1024]{1,0:T(8,128)(2,1)} %copy-done.19) | copy-start | bytes 3145732
  337.0 47.5 %copy-start.52 = (bf16[512,1024]{1,0:T(8,128)(2,1)S(1)}, bf16[512,1024]{1,0:T(8,128)(2,1)}, u32[]{:S(2)}) copy-start(bf16[512,1024]{1,0:T(8,128)(2,1)} %copy-done.51) | copy-start | bytes 3145732
  391.8 13.5 %copy-start.27 = (bf16[4,32,1024]{2,1,0:T(8,128)(2,1)S(1)}, bf16[4,32,1024]{2,1,0:T(8,128)(2,1)}, u32[]{:S(2)}) copy-start(bf16[4,32,1024]{2,1,0:T(8,128)(2,1)} %copy-done.26) | copy-start | bytes 786436
  391.8 187.0 %all-gather.11.cloned.1.call-start = ((), (), s32[]{:S(2)}) async-start(), calls=%async_computation.6 | async-start | bytes 2359296 | tf_op jit(solution)/shard_map/all_gather | solution.py:1195
  405.3 180.9 %all-gather.13.cloned.1.call-start = ((), (), s32[]{:S(2)}) async-start(), calls=%async_computation.7 | async-start | bytes 4718592 | tf_op jit(solution)/shard_map/all_gather | solution.py:1195
  411.6 42.6 %copy-start.73 = (bf16[512,256]{0,1:T(8,128)(2,1)S(1)}, bf16[512,256]{0,1:T(8,128)(2,1)}, u32[]{:S(2)}) copy-start(bf16[512,256]{0,1:T(8,128)(2,1)} %copy-done.72) | copy-start | bytes 786436
  558.8 24.5 %copy-start.30 = (bf16[8,32,4096]{2,1,0:T(8,128)(2,1)S(1)}, bf16[8,32,4096]{2,1,0:T(8,128)(2,1)}, u32[]{:S(2)}) copy-start(bf16[8,32,4096]{2,1,0:T(8,128)(2,1)} %get-tuple-element.86) | copy-start | bytes 6291460
  (69 other events, 163.6 us)
Sparse Core Ops, SparseCore 0:
  24.4 25.8 all-gather.14
  65.2 27.0 all-gather.16
  94.2 25.5 all-gather.18
  121.6 27.8 all-gather.20
  263.2 48.4 reduce-scatter.3
  328.1 39.5 reduce-scatter.5
  391.9 48.7 reduce-scatter.7
  442.6 27.8 all-gather.10
  472.4 47.8 all-gather.12
